TPU v7x, 32 devices: a whole 2x2x4 slice. The times are simulated.
32 devices in a mesh: replica: 4 (over x, core), group: 8 (over z, y).
Axes of the slice: x: 2, y: 2, z: 4, core: 2. Of those that a mesh axis runs over, the one named last changes fastest.
Arguments:
- tokens: bfloat16 [25216, 512], P(('replica', 'group')), may hold values from -6 to 6
- cotangent: bfloat16 [25216, 512], P(('replica', 'group')), may hold values from -6 to 6
- expert_index: int32 [25216, 2], P(('replica', 'group')), may hold values from 0 to 3, all different within a row; in each aligned block of 394 rows (0 to 393, 394 to 787, ...) at most 392 rows name the same one
- qkv_weight: float32 [512, 1536], P('group'), may hold values from -0.25 to 0.25
- out_weight: float32 [512, 512], P('group'), may hold values from -1.5 to 1.5
- router_weight: float32 [512, 4], P('group'), may hold values from -0.1875 to 0.1875
- up_weight: float32 [4, 512, 2048], P(None, 'group'), may hold values from -0.25 to 0.25
- up_bias: float32 [4, 2048], P(None, 'group'), may hold values from -0.5 to 0.5
- down_weight: float32 [4, 2048, 512], P(None, 'group'), may hold values from -0.5 to 0.5
- vectors: float32 [11, 512], P(None, 'group'), may hold values from -0.4 to 1.4, as said below
- qkv_moments: float32 [2, 512, 1536], P(None, 'group'), as said below
- out_moments: float32 [2, 512, 512], P(None, 'group'), as said below
- router_moments: float32 [2, 512, 4], P(None, 'group'), as said below
- up_moments: float32 [2, 4, 512, 2048], P(None, None, 'group'), as said below
- up_bias_moments: float32 [2, 4, 2048], P(None, None, 'group'), as said below
- down_moments: float32 [2, 4, 2048, 512], P(None, None, 'group'), as said below
- vector_moments: float32 [2, 11, 512], P(None, None, 'group'), as said below
Outputs:
- block_out: bfloat16 [25216, 512], P(('replica', 'group'))
- input_grad: float32 [25216, 512], P(('replica', 'group'))
- qkv_grad: float32 [512, 1536], P('group')
- out_grad: float32 [512, 512], P('group')
- router_grad: float32 [512, 4], P('group')
- up_grad: float32 [4, 512, 2048], P(None, 'group')
- up_bias_grad: float32 [4, 2048], P(None, 'group')
- down_grad: float32 [4, 2048, 512], P(None, 'group')
- vectors_grad: float32 [11, 512], P(None, 'group')
- qkv_new: float32 [512, 1536], P('group')
- out_new: float32 [512, 512], P('group')
- router_new: float32 [512, 4], P('group')
- up_new: float32 [4, 512, 2048], P(None, 'group')
- up_bias_new: float32 [4, 2048], P(None, 'group')
- down_new: float32 [4, 2048, 512], P(None, 'group')
- vectors_new: float32 [11, 512], P(None, 'group')
- qkv_moments_new: float32 [2, 512, 1536], P(None, 'group')
- out_moments_new: float32 [2, 512, 512], P(None, 'group')
- router_moments_new: float32 [2, 512, 4], P(None, 'group')
- up_moments_new: float32 [2, 4, 512, 2048], P(None, None, 'group')
- up_bias_moments_new: float32 [2, 4, 2048], P(None, None, 'group')
- down_moments_new: float32 [2, 4, 2048, 512], P(None, None, 'group')
- vector_moments_new: float32 [2, 11, 512], P(None, None, 'group')
Inputs may be any that keep to these rules, and one draw needn't show every extreme that they name: `expert_index`: in each aligned block of 394 rows (one micro-batch of one device) no expert is named by more than 392 rows; a row names two different experts. `vectors`: rows 0 and 5 are gains near one, the others biases near zero. `qkv_moments`: index 1 of the first dimension is positive. `out_moments`: index 1 of the first dimension is positive. `router_moments`: index 1 of the first dimension is positive. `up_moments`: index 1 of the first dimension is positive. `up_bias_moments`: index 1 of the first dimension is positive. `down_moments`: index 1 of the first dimension is positive. `vector_moments`: index 1 of the first dimension is positive.
All inputs are finite; a program needn't handle non-finite values.
Results may differ from a plain program's by a relative error of at most 0.019.
Values may be sent and summed in bfloat16 or wider, within the bound.
A program may use at most 256 MiB of HBM per device.

v0:
```python
import functools

import jax
import jax.numpy as jnp
import numpy as np
from jax import lax
from jax.sharding import Mesh
from jax.sharding import PartitionSpec as P
from jax.experimental import pallas as pl
from jax.experimental.pallas import tpu as pltpu

D = 512
HEADS = 8
HEAD_DIM = 64
F = 2048
E = 4
S = 197
MB_TOK = 394
CAP = 392
NV = 11
DENSE_AG = 2560
DENSE_PAD = 2304
F32 = jnp.float32
BF16 = jnp.bfloat16
TOK = ("rx", "core", "group")


MESH_ID = pl.DeviceIdType.MESH


def ring_order(groups):
    if groups in (4, 8):
        zs = groups // 2

        def pos_of(g):
            y = g % 2
            z = g // 2
            return z + y * (2 * zs - 1 - 2 * z)

        def dev_at(p):
            p = p % groups
            yy = p // zs
            return 2 * (p + yy * (2 * zs - 1 - 2 * p)) + yy

        return pos_of, dev_at
    return (lambda g: g), (lambda p: p % groups)


def ring_rs_kernel(groups, n_in, *refs):
    ins = refs[:n_in]
    outs = refs[n_in : 2 * n_in]
    rbufs = refs[2 * n_in : 3 * n_in]
    sbufs = refs[3 * n_in : 4 * n_in]
    owns = refs[4 * n_in : 5 * n_in]
    send_sem, recv_sem, load_sem = refs[5 * n_in :]
    pos_of, dev_at = ring_order(groups)
    rx = lax.axis_index("rx")
    core = lax.axis_index("core")
    g = lax.axis_index("group")
    pos = pos_of(g)
    nbr = (dev_at(pos + 1), dev_at(pos + groups - 1))

    barrier = pltpu.get_barrier_semaphore()
    for n in nbr:
        pl.semaphore_signal(barrier, inc=1, device_id=(rx, core, n), device_id_type=MESH_ID)
    pl.semaphore_wait(barrier, 2)

    def block_dev(d, s):
        if d == 0:
            return dev_at(pos + 2 * groups - s - 1)
        return dev_at(pos + s + 1)

    def load(d, s, slot):
        b = block_dev(d, s)
        copies = []
        for i in range(n_in):
            rows = ins[i].shape[1] // groups
            half = ins[i].shape[2] // 2
            src = ins[i].at[:, pl.ds(pl.multiple_of(b * rows, rows), rows), pl.ds(d * half, half)]
            copies.append(pltpu.make_async_copy(src, owns[i].at[d, slot], load_sem.at[d, slot, i]))
        return copies

    def remote(d, s, i):
        return pltpu.make_async_remote_copy(
            src_ref=sbufs[i].at[d, s],
            dst_ref=rbufs[i].at[d, s],
            send_sem=send_sem.at[d, s, i],
            recv_sem=recv_sem.at[d, s, i],
            device_id=(rx, core, nbr[d]),
            device_id_type=MESH_ID,
        )

    for d in range(2):
        for c in load(d, 0, 0):
            c.start()
    sends = []
    for s in range(groups):
        slot = s % 2
        for d in range(2):
            for c in load(d, s, slot):
                c.wait()
            if s + 1 < groups:
                for c in load(d, s + 1, 1 - slot):
                    c.start()
            for i in range(n_in):
                if s > 0:
                    remote(d, s - 1, i).wait_recv()
                for a in range(ins[i].shape[0]):
                    mine = owns[i][d, slot, a].astype(F32)
                    if s > 0:
                        mine = mine + rbufs[i][d, s - 1, a].astype(F32)
                    if s < groups - 1:
                        sbufs[i][d, s, a] = mine.astype(sbufs[i].dtype)
                    else:
                        half = ins[i].shape[2] // 2
                        outs[i][a, :, pl.ds(d * half, half)] = mine.astype(outs[i].dtype)
                if s < groups - 1:
                    c = remote(d, s, i)
                    c.start()
                    sends.append(c)
    for c in sends:
        c.wait_send()


def ring_reduce_scatter(xs, groups, collective_id):
    n_in = len(xs)
    outs, rb, own = [], [], []
    flops = 0
    nbytes = 0
    for x in xs:
        a, total, c = x.shape
        rows = total // groups
        outs.append(jax.ShapeDtypeStruct((a, rows, c), x.dtype))
        rb.append(pltpu.VMEM((2, groups - 1, a, rows, c // 2), x.dtype))
        own.append(pltpu.VMEM((2, 2, a, rows, c // 2), x.dtype))
        flops += a * total * c
        nbytes += 3 * x.size * x.dtype.itemsize
    scratch = rb + rb + own + [
        pltpu.SemaphoreType.DMA((2, groups - 1, n_in)),
        pltpu.SemaphoreType.DMA((2, groups - 1, n_in)),
        pltpu.SemaphoreType.DMA((2, 2, n_in)),
    ]
    return pl.pallas_call(
        functools.partial(ring_rs_kernel, groups, n_in),
        out_shape=outs,
        in_specs=[pl.BlockSpec(memory_space=pl.ANY)] * n_in,
        out_specs=[pl.BlockSpec(memory_space=pltpu.VMEM)] * n_in,
        scratch_shapes=scratch,
        compiler_params=pltpu.CompilerParams(
            collective_id=collective_id, has_side_effects=True, vmem_limit_bytes=60 * 1024 * 1024
        ),
        cost_estimate=pl.CostEstimate(flops=flops, bytes_accessed=nbytes, transcendentals=0),
    )(*xs)


def ring_ag_kernel(groups, *refs):
    in_up, in_down, in_dense, out_up, out_down, out_dense = refs[:6]
    ring_send, ring_recv, part_send, part_recv, local_sem = refs[6:]
    pos_of, dev_at = ring_order(groups)
    rx = lax.axis_index("rx")
    core = lax.axis_index("core")
    g = lax.axis_index("group")
    other = 1 - core
    pos = pos_of(g)
    nbr = (dev_at(pos + 1), dev_at(pos + groups - 1))
    gs = in_up.shape[1]
    fs = in_down.shape[1]
    width = in_dense.shape[1] // 2

    barrier = pltpu.get_barrier_semaphore()
    for n in nbr:
        pl.semaphore_signal(barrier, inc=1, device_id=(rx, core, n), device_id_type=MESH_ID)
    pl.semaphore_signal(barrier, inc=1, device_id=(rx, other, g), device_id_type=MESH_ID)
    pl.semaphore_wait(barrier, 3)

    def items(owner):
        found = []
        for k in range(2):
            e = 2 * k + owner
            found.append((in_up.at[e], lambda b, e=e: out_up.at[e, pl.ds(pl.multiple_of(b * gs, gs), gs)], F // 2))
            found.append((in_down.at[e], lambda b, e=e: out_down.at[e, pl.ds(pl.multiple_of(b * fs, fs), fs)], D // 2))
        dense_in = in_dense.at[:, pl.ds(owner * width, width)]
        found.append(
            (dense_in, lambda b: out_dense.at[pl.ds(pl.multiple_of(b * gs, gs), gs), pl.ds(owner * width, width)], width // 2)
        )
        return found

    mine = items(core)
    theirs = items(other)
    n_items = len(mine)

    locals_ = [pltpu.make_async_copy(in_up.at[e], out_up.at[e, pl.ds(pl.multiple_of(g * gs, gs), gs)], local_sem.at[e]) for e in range(E)]
    locals_ += [
        pltpu.make_async_copy(in_down.at[e], out_down.at[e, pl.ds(pl.multiple_of(g * fs, fs), fs)], local_sem.at[E + e])
        for e in range(E)
    ]
    locals_.append(pltpu.make_async_copy(in_dense, out_dense.at[pl.ds(pl.multiple_of(g * gs, gs), gs)], local_sem.at[2 * E]))
    for c in locals_:
        c.start()

    def block_at(d, s):
        if d == 0:
            return dev_at(pos + 2 * groups - 1 - s)
        return dev_at(pos + 1 + s)

    def ring_copy(d, s, j, src_block):
        src_in, dst_of, half = mine[j]
        cols = pl.ds(d * half, half)
        if src_block is None:
            src = src_in.at[:, cols]
            dst = dst_of(g).at[:, cols]
        else:
            src = dst_of(src_block).at[:, cols]
            dst = src
        return pltpu.make_async_remote_copy(
            src_ref=src, dst_ref=dst, send_sem=ring_send.at[d, s, j], recv_sem=ring_recv.at[d, s, j],
            device_id=(rx, core, nbr[d]), device_id_type=MESH_ID,
        )

    def part_copy(d, s, j, table, block):
        _, dst_of, half = table[j]
        view = dst_of(block).at[:, pl.ds(d * half, half)]
        return pltpu.make_async_remote_copy(
            src_ref=view, dst_ref=view, send_sem=part_send.at[d, s, j], recv_sem=part_recv.at[d, s, j],
            device_id=(rx, other, g), device_id_type=MESH_ID,
        )

    sends = []
    for d in range(2):
        for j in range(n_items):
            c = ring_copy(d, 0, j, None)
            c.start()
            sends.append(c)
    for s in range(groups - 1):
        for d in range(2):
            b = block_at(d, s)
            for j in range(n_items):
                pltpu.make_async_remote_copy(
                    src_ref=mine[j][1](b).at[:, pl.ds(d * mine[j][2], mine[j][2])],
                    dst_ref=mine[j][1](b).at[:, pl.ds(d * mine[j][2], mine[j][2])],
                    send_sem=ring_send.at[d, s, j], recv_sem=ring_recv.at[d, s, j],
                    device_id=(rx, core, nbr[d]), device_id_type=MESH_ID,
                ).wait_recv()
                if s + 1 < groups - 1:
                    c = ring_copy(d, s + 1, j, b)
                    c.start()
                    sends.append(c)
                c = part_copy(d, s, j, mine, b)
                c.start()
                sends.append(c)
    for s in range(groups - 1):
        for d in range(2):
            b = block_at(d, s)
            for j in range(n_items):
                part_copy(d, s, j, theirs, b).wait_recv()
    for c in sends:
        c.wait_send()
    for c in locals_:
        c.wait()


def ring_all_gather(up_b, down_b, dense_b, groups, collective_id):
    n_items = 5
    gs = up_b.shape[1]
    shapes = [
        jax.ShapeDtypeStruct((E, gs * groups, F), BF16),
        jax.ShapeDtypeStruct((E, down_b.shape[1] * groups, D), BF16),
        jax.ShapeDtypeStruct((gs * groups, dense_b.shape[1]), BF16),
    ]
    nbytes = sum(int(np.prod(s.shape)) * 2 for s in shapes)
    return pl.pallas_call(
        functools.partial(ring_ag_kernel, groups),
        out_shape=shapes,
        in_specs=[pl.BlockSpec(memory_space=pl.ANY)] * 3,
        out_specs=[pl.BlockSpec(memory_space=pl.ANY)] * 3,
        scratch_shapes=[
            pltpu.SemaphoreType.DMA((2, groups - 1, n_items)),
            pltpu.SemaphoreType.DMA((2, groups - 1, n_items)),
            pltpu.SemaphoreType.DMA((2, groups - 1, n_items)),
            pltpu.SemaphoreType.DMA((2, groups - 1, n_items)),
            pltpu.SemaphoreType.DMA((2 * E + 1,)),
        ],
        compiler_params=pltpu.CompilerParams(collective_id=collective_id, has_side_effects=True),
        cost_estimate=pl.CostEstimate(flops=0, bytes_accessed=nbytes, transcendentals=0),
    )(up_b, down_b, dense_b)


def grad_items(gu, gd, gdense, owner, gs, fs, width):
    found = []
    for k in range(2):
        e = 2 * k + owner
        found.append((lambda b, e=e: gu.at[e, pl.ds(pl.multiple_of(b * gs, gs), gs)], F // 2))
        found.append((lambda b, e=e: gd.at[e, pl.ds(pl.multiple_of(b * fs, fs), fs)], D // 2))
    found.append((lambda b: gdense.at[pl.ds(pl.multiple_of(b * gs, gs), gs), pl.ds(owner * width, width)], width // 2))
    return found


def ring_rs2_kernel(groups, x_pair, *refs):
    gu, gd, gdense, out_up, out_down, out_dense = refs[:6]
    n_items = 5
    scr = refs[6:]
    rbuf, sbuf, pbuf, own, fin, xr, cr = (scr[i * n_items : (i + 1) * n_items] for i in range(7))
    ring_send, ring_recv, part_send, part_recv, load_sem, x_send, x_recv, c_send, c_recv = scr[7 * n_items :]
    pos_of, dev_at = ring_order(groups)
    rx = lax.axis_index("rx")
    core = lax.axis_index("core")
    g = lax.axis_index("group")
    other = 1 - core
    pos = pos_of(g)
    nbr = (dev_at(pos + 1), dev_at(pos + groups - 1))
    gs = gu.shape[1] // groups
    fs = gd.shape[1] // groups
    width = gdense.shape[1] // 2
    mine = grad_items(gu, gd, gdense, core, gs, fs, width)
    theirs = grad_items(gu, gd, gdense, other, gs, fs, width)

    barrier = pltpu.get_barrier_semaphore()
    for n in nbr:
        pl.semaphore_signal(barrier, inc=1, device_id=(rx, core, n), device_id_type=MESH_ID)
    pl.semaphore_signal(barrier, inc=1, device_id=(rx, other, g), device_id_type=MESH_ID)
    count = 3
    if x_pair:
        pl.semaphore_signal(barrier, inc=1, device_id=(1 - rx, core, g), device_id_type=MESH_ID)
        count = 4
    pl.semaphore_wait(barrier, count)

    def block_at(d, s):
        if d == 0:
            return dev_at(pos + 2 * groups - 1 - s)
        return dev_at(pos + 1 + s)

    def cols(j, d):
        half = mine[j][1]
        return pl.ds(d * half, half)

    def load(d, s, slot, j):
        return pltpu.make_async_copy(mine[j][0](block_at(d, s)).at[:, cols(j, d)], own[j].at[d, slot], load_sem.at[d, slot, j])

    def part(d, s, j):
        return pltpu.make_async_remote_copy(
            src_ref=theirs[j][0](block_at(d, s)).at[:, cols(j, d)], dst_ref=pbuf[j].at[d, s],
            send_sem=part_send.at[d, s, j], recv_sem=part_recv.at[d, s, j],
            device_id=(rx, other, g), device_id_type=MESH_ID,
        )

    def ring(d, s, j):
        return pltpu.make_async_remote_copy(
            src_ref=sbuf[j].at[d, s], dst_ref=rbuf[j].at[d, s],
            send_sem=ring_send.at[d, s, j], recv_sem=ring_recv.at[d, s, j],
            device_id=(rx, core, nbr[d]), device_id_type=MESH_ID,
        )

    sends = []
    for d in range(2):
        for j in range(n_items):
            load(d, 0, 0, j).start()
            c = part(d, 0, j)
            c.start()
            sends.append(c)
    for s in range(groups):
        slot = s % 2
        for d in range(2):
            for j in range(n_items):
                load(d, s, slot, j).wait()
                if s + 1 < groups:
                    load(d, s + 1, 1 - slot, j).start()
                    c = part(d, s + 1, j)
                    c.start()
                    sends.append(c)
                part(d, s, j).wait_recv()
                val = own[j][d, slot].astype(F32) + pbuf[j][d, s].astype(F32)
                if s > 0:
                    ring(d, s - 1, j).wait_recv()
                    val = val + rbuf[j][d, s - 1].astype(F32)
                if s < groups - 1:
                    sbuf[j][d, s] = val.astype(BF16)
                    c = ring(d, s, j)
                    c.start()
                    sends.append(c)
                else:
                    fin[j][d] = val

    for c in sends:
        c.wait_send()
    sends = []
    if x_pair:
        x_copies = []
        for d in range(2):
            for j in range(n_items):
                sbuf[j][d, 0] = fin[j][d].astype(BF16)
                c = pltpu.make_async_remote_copy(
                    src_ref=sbuf[j].at[d, 0], dst_ref=xr[j].at[d], send_sem=x_send.at[d, j], recv_sem=x_recv.at[d, j],
                    device_id=(1 - rx, core, g), device_id_type=MESH_ID,
                )
                c.start()
                x_copies.append(c)
        for c in x_copies:
            c.wait_recv()
        for d in range(2):
            for j in range(n_items):
                fin[j][d] = sbuf[j][d, 0].astype(F32) + xr[j][d].astype(F32)
        sends += x_copies

    c_copies = []
    for d in range(2):
        for j in range(n_items):
            c = pltpu.make_async_remote_copy(
                src_ref=fin[j].at[d], dst_ref=cr[j].at[d], send_sem=c_send.at[d, j], recv_sem=c_recv.at[d, j],
                device_id=(rx, other, g), device_id_type=MESH_ID,
            )
            c.start()
            c_copies.append(c)

    def out_items(owner):
        found = []
        for k in range(2):
            e = 2 * k + owner
            found.append(lambda d, e=e: out_up.at[e, :, pl.ds(d * (F // 2), F // 2)])
            found.append(lambda d, e=e: out_down.at[e, :, pl.ds(d * (D // 2), D // 2)])
        found.append(lambda d: out_dense.at[:, pl.ds(owner * width + d * (width // 2), width // 2)])
        return found

    mine_out = out_items(core)
    theirs_out = out_items(other)
    for d in range(2):
        for j in range(n_items):
            mine_out[j](d)[...] = fin[j][d]
    for c in c_copies:
        c.wait_recv()
    for d in range(2):
        for j in range(n_items):
            theirs_out[j](d)[...] = cr[j][d]
    for c in sends + c_copies:
        c.wait_send()


def grad_reduce(gu, gd, gdense, groups, x_pair, collective_id):
    gs = gu.shape[1] // groups
    fs = gd.shape[1] // groups
    width = gdense.shape[1] // 2
    item_shapes = [(gs, F // 2), (fs, D // 2), (gs, F // 2), (fs, D // 2), (gs, width // 2)]
    scratch = []
    for lead, dtype in (((2, groups - 1), BF16), ((2, groups - 1), BF16), ((2, groups), BF16), ((2, 2), BF16), ((2,), F32), ((2,), BF16), ((2,), F32)):
        scratch += [pltpu.VMEM(lead + shp, dtype) for shp in item_shapes]
    scratch += [
        pltpu.SemaphoreType.DMA((2, groups - 1, 5)),
        pltpu.SemaphoreType.DMA((2, groups - 1, 5)),
        pltpu.SemaphoreType.DMA((2, groups, 5)),
        pltpu.SemaphoreType.DMA((2, groups, 5)),
        pltpu.SemaphoreType.DMA((2, 2, 5)),
        pltpu.SemaphoreType.DMA((2, 5)),
        pltpu.SemaphoreType.DMA((2, 5)),
        pltpu.SemaphoreType.DMA((2, 5)),
        pltpu.SemaphoreType.DMA((2, 5)),
    ]
    outs = [
        jax.ShapeDtypeStruct((E, gs, F), F32),
        jax.ShapeDtypeStruct((E, fs, D), F32),
        jax.ShapeDtypeStruct((gs, gdense.shape[1]), F32),
    ]
    nbytes = 2 * (gu.size + gd.size + gdense.size)
    return pl.pallas_call(
        functools.partial(ring_rs2_kernel, groups, x_pair),
        out_shape=outs,
        in_specs=[pl.BlockSpec(memory_space=pl.ANY)] * 3,
        out_specs=[pl.BlockSpec(memory_space=pltpu.VMEM)] * 3,
        scratch_shapes=scratch,
        compiler_params=pltpu.CompilerParams(
            collective_id=collective_id, has_side_effects=True, vmem_limit_bytes=62 * 1024 * 1024
        ),
        cost_estimate=pl.CostEstimate(flops=gu.size + gd.size + gdense.size, bytes_accessed=nbytes, transcendentals=0),
    )(gu, gd, gdense)


TILE = 128
TILE_B = 256
CAPP = 512
SQRT_HALF = float(np.sqrt(0.5))
INV_SQRT_2PI = float(1.0 / np.sqrt(2.0 * np.pi))


def ffn_fwd_kernel(micro, counts, x_ref, w1_ref, b1_ref, w2_ref, b2_ref, hp_ref, h_ref, y_ref):
    e, m, t = pl.program_id(0), pl.program_id(1), pl.program_id(2)
    active = t * TILE < counts[e * micro + m]

    @pl.when(active)
    def _():
        hp = jnp.dot(x_ref[0], w1_ref[0], preferred_element_type=F32) + b1_ref[0]
        h = (0.5 * hp * (1.0 + lax.erf(hp * SQRT_HALF))).astype(BF16)
        hp_ref[0] = hp
        h_ref[0] = h
        y = jnp.dot(h, w2_ref[0], preferred_element_type=F32) + b2_ref[0]
        hi = y.astype(BF16)
        y_ref[0, :, :D] = hi
        y_ref[0, :, D:] = (y - hi.astype(F32)).astype(BF16)

    @pl.when(jnp.logical_not(active))
    def _():
        y_ref[0] = jnp.zeros(y_ref.shape[1:], BF16)


def ffn_forward(counts, table_in, w1, b1, w2, b2, micro):
    tiles = CAPP // TILE
    rows = table_in.shape[1]
    row_map = lambda e, m, t, c: (m, e * tiles + t, 0)
    w_map = lambda e, m, t, c: (e, 0, 0)
    grid_spec = pltpu.PrefetchScalarGridSpec(
        num_scalar_prefetch=1,
        grid=(E, micro, tiles),
        in_specs=[
            pl.BlockSpec((1, TILE, D), row_map),
            pl.BlockSpec((1, D, F), w_map),
            pl.BlockSpec((1, 1, F), w_map),
            pl.BlockSpec((1, F, D), w_map),
            pl.BlockSpec((1, 1, D), w_map),
        ],
        out_specs=[
            pl.BlockSpec((1, TILE, F), row_map),
            pl.BlockSpec((1, TILE, F), row_map),
            pl.BlockSpec((1, TILE, 2 * D), row_map),
        ],
    )
    work = micro * rows
    return pl.pallas_call(
        functools.partial(ffn_fwd_kernel, micro),
        grid_spec=grid_spec,
        out_shape=[
            jax.ShapeDtypeStruct((micro, rows, F), F32),
            jax.ShapeDtypeStruct((micro, rows, F), BF16),
            jax.ShapeDtypeStruct((micro, rows, 2 * D), BF16),
        ],
        compiler_params=pltpu.CompilerParams(vmem_limit_bytes=48 * 1024 * 1024),
        cost_estimate=pl.CostEstimate(
            flops=4 * work * D * F // 2, bytes_accessed=work * (2 * D + 6 * F + 4 * D) // 2, transcendentals=work * F // 2
        ),
    )(counts, table_in, w1, b1, w2, b2)


def ffn_bwd_kernel(micro, counts, dy_ref, x_ref, hp_ref, h_ref, w1_ref, w2_ref, dt_ref, gu_ref, gd_ref, gb_ref, gb2_ref, gu_acc, gd_acc):
    e, m, t = pl.program_id(0), pl.program_id(1), pl.program_id(2)
    active = t * TILE_B < counts[e * micro + m]

    @pl.when((m == 0) & (t == 0))
    def _():
        gu_acc[...] = jnp.zeros(gu_acc.shape, F32)
        gd_acc[...] = jnp.zeros(gd_acc.shape, F32)
        gb_ref[...] = jnp.zeros(gb_ref.shape, F32)
        gb2_ref[...] = jnp.zeros(gb2_ref.shape, F32)

    @pl.when(active)
    def _():
        dy = dy_ref[0]
        hp = hp_ref[0]
        d_hidden = lax.dot_general(dy, w2_ref[0], (((1,), (1,)), ((), ())), preferred_element_type=F32)
        slope = 0.5 * (1.0 + lax.erf(hp * SQRT_HALF)) + hp * jnp.exp(-0.5 * hp * hp) * INV_SQRT_2PI
        d_pre = (d_hidden * slope).astype(BF16)
        dt = lax.dot_general(d_pre, w1_ref[0], (((1,), (1,)), ((), ())), preferred_element_type=F32)
        hi = dt.astype(BF16)
        dt_ref[0, :, :D] = hi
        dt_ref[0, :, D:] = (dt - hi.astype(F32)).astype(BF16)
        gb2_ref[0] += jnp.sum(dy.astype(F32), 0, keepdims=True)
        gu_acc[...] += lax.dot_general(x_ref[0], d_pre, (((0,), (0,)), ((), ())), preferred_element_type=F32)
        gd_acc[...] += lax.dot_general(h_ref[0], dy, (((0,), (0,)), ((), ())), preferred_element_type=F32)
        gb_ref[0] += jnp.sum(d_pre.astype(F32), 0, keepdims=True)

    @pl.when(jnp.logical_not(active))
    def _():
        dt_ref[0] = jnp.zeros(dt_ref.shape[1:], BF16)

    @pl.when((m == micro - 1) & (t == pl.num_programs(2) - 1))
    def _():
        gu_ref[0] = gu_acc[...].astype(BF16)
        gd_ref[0] = gd_acc[...].astype(BF16)


def ffn_backward(counts, d_expert, table_in, hp, h, w1, w2, micro):
    tiles = CAPP // TILE_B
    rows = table_in.shape[1]
    row_map = lambda e, m, t, c: (m, e * tiles + t, 0)
    w_map = lambda e, m, t, c: (e, 0, 0)
    grid_spec = pltpu.PrefetchScalarGridSpec(
        num_scalar_prefetch=1,
        grid=(E, micro, tiles),
        in_specs=[
            pl.BlockSpec((1, TILE_B, D), row_map),
            pl.BlockSpec((1, TILE_B, D), row_map),
            pl.BlockSpec((1, TILE_B, F), row_map),
            pl.BlockSpec((1, TILE_B, F), row_map),
            pl.BlockSpec((1, D, F), w_map),
            pl.BlockSpec((1, F, D), w_map),
        ],
        out_specs=[
            pl.BlockSpec((1, TILE_B, 2 * D), row_map),
            pl.BlockSpec((1, D, F), w_map),
            pl.BlockSpec((1, F, D), w_map),
            pl.BlockSpec((1, 1, F), w_map),
            pl.BlockSpec((1, 1, D), w_map),
        ],
        scratch_shapes=[pltpu.VMEM((D, F), F32), pltpu.VMEM((F, D), F32)],
    )
    work = micro * rows
    return pl.pallas_call(
        functools.partial(ffn_bwd_kernel, micro),
        grid_spec=grid_spec,
        out_shape=[
            jax.ShapeDtypeStruct((micro, rows, 2 * D), BF16),
            jax.ShapeDtypeStruct((E, D, F), BF16),
            jax.ShapeDtypeStruct((E, F, D), BF16),
            jax.ShapeDtypeStruct((E, 1, F), F32),
            jax.ShapeDtypeStruct((E, 1, D), F32),
        ],
        compiler_params=pltpu.CompilerParams(vmem_limit_bytes=60 * 1024 * 1024),
        cost_estimate=pl.CostEstimate(
            flops=8 * work * D * F // 2, bytes_accessed=work * (8 * D + 6 * F) // 2 + 16 * E * D * F, transcendentals=2 * work * F // 2
        ),
    )(counts, d_expert, table_in, hp, h, w1, w2)

def layer_norm(value, gain, shift):
    center = value - jnp.mean(value, -1, keepdims=True)
    spread = jnp.mean(center * center, -1, keepdims=True)
    return center * lax.rsqrt(spread + 1e-06) * gain + shift


def gelu_exact(value):
    return jax.nn.gelu(value, approximate=False)


def split_heads(part):
    return part.reshape(-1, S, HEADS, HEAD_DIM)


def dot(a, b):
    return jnp.dot(a, b, preferred_element_type=F32)


def assign_places(route):
    chosen = jnp.concatenate([route[:, :, 0], route[:, :, 1]], 1)
    hits = (chosen[:, :, None] == jnp.arange(E, dtype=jnp.int32)).astype(jnp.int32)
    before = jnp.cumsum(hits, 1) - hits
    slot = jnp.sum(before * hits, 2)
    return chosen * CAPP + slot, jnp.sum(hits, 1)


def hi_lo(v):
    hi = v.astype(BF16)
    lo = (v - hi.astype(F32)).astype(BF16)
    return jnp.concatenate([hi, lo], -1)


def pick_rows(onehot, split):
    both = jnp.einsum("mnr,mrd->mnd", onehot, split, preferred_element_type=F32)
    return both[..., :D] + both[..., D:]


def pack_dense(qkv_w, out_w, router_w, vectors, up_bias):
    rows = qkv_w.shape[0]
    ub = up_bias.reshape(E, rows, 4).transpose(1, 0, 2).reshape(rows, E * 4)
    return jnp.concatenate([qkv_w, out_w, router_w, vectors.T, ub], 1)


def unpack_dense(packed):
    rows = packed.shape[0]
    w_qkv = packed[:, : 3 * D]
    w_out = packed[:, 3 * D : 4 * D]
    w_router = packed[:, 4 * D : 4 * D + E]
    table = packed[:, 4 * D + E : 4 * D + E + NV].T
    ub = packed[:, 4 * D + E + NV :].reshape(rows, E, 4).transpose(1, 0, 2).reshape(E, rows * 4)
    return w_qkv, w_out, w_router, table, ub


def attention_fwd(w_qkv, w_out, table, value):
    rows = value.shape[0]
    scale = HEAD_DIM ** (-0.5)
    first = layer_norm(value, table[0], table[1]).astype(BF16)
    qkv_bias = jnp.concatenate([table[2], jnp.zeros((D,), F32), table[3]])
    qkv = (dot(first, w_qkv) + qkv_bias).astype(BF16)
    query, key_part, val_part = (
        split_heads(qkv[:, :D]),
        split_heads(qkv[:, D : 2 * D]),
        split_heads(qkv[:, 2 * D :]),
    )
    scores = jnp.einsum("bqhd,bkhd->bhqk", query, key_part, preferred_element_type=F32) * scale
    peak = jnp.max(scores, -1, keepdims=True)
    expo = jnp.exp(scores - peak)
    total = jnp.sum(expo, -1, keepdims=True)
    probs_att = (expo / total).astype(BF16)
    log_total = peak + jnp.log(total)
    attended = jnp.einsum("bhqk,bkhd->bqhd", probs_att, val_part, preferred_element_type=F32)
    attended = attended.reshape(rows, D).astype(BF16)
    resid = value + (dot(attended, w_out) + table[4])
    return first, qkv, log_total, attended, resid


def attention_bwd(w_qkv, w_out, table, value, first, qkv, log_total, attended, d_resid):
    rows = value.shape[0]
    scale = HEAD_DIM ** (-0.5)
    d_branch = d_resid.astype(BF16)
    g_bias_out = jnp.sum(d_branch.astype(F32), 0)
    g_out = lax.dot_general(attended, d_branch, (((0,), (0,)), ((), ())), preferred_element_type=F32)
    d_att = split_heads(
        lax.dot_general(d_branch, w_out, (((1,), (1,)), ((), ())), preferred_element_type=F32).astype(BF16)
    )
    query, key_part, val_part = (
        split_heads(qkv[:, :D]),
        split_heads(qkv[:, D : 2 * D]),
        split_heads(qkv[:, 2 * D :]),
    )
    scores = jnp.einsum("bqhd,bkhd->bhqk", query, key_part, preferred_element_type=F32) * scale
    probs_f = jnp.exp(scores - log_total)
    probs_att = probs_f.astype(BF16)
    d_val = jnp.einsum("bhqk,bqhd->bkhd", probs_att, d_att, preferred_element_type=F32)
    d_prob = jnp.einsum("bqhd,bkhd->bhqk", d_att, val_part, preferred_element_type=F32)
    d_score = (probs_f * (d_prob - jnp.sum(d_prob * probs_f, -1, keepdims=True))).astype(BF16)
    d_query = jnp.einsum("bhqk,bkhd->bqhd", d_score, key_part, preferred_element_type=F32) * scale
    d_key = jnp.einsum("bhqk,bqhd->bkhd", d_score, query, preferred_element_type=F32) * scale
    d_qkv = jnp.concatenate(
        [d_query.reshape(rows, D), d_key.reshape(rows, D), d_val.reshape(rows, D)], 1
    ).astype(BF16)
    d_qkv_f = d_qkv.astype(F32)
    g_bias_q = jnp.sum(d_qkv_f[:, :D], 0)
    g_bias_v = jnp.sum(d_qkv_f[:, 2 * D :], 0)
    g_qkv = lax.dot_general(first, d_qkv, (((0,), (0,)), ((), ())), preferred_element_type=F32)
    d_first = lax.dot_general(d_qkv, w_qkv, (((1,), (1,)), ((), ())), preferred_element_type=F32)
    first_pull = jax.vjp(layer_norm, value, table[0], table[1])[1]
    d_input, g_gain_one, g_shift_one = first_pull(d_first)
    return (g_qkv, g_out, g_bias_out, g_bias_q, g_bias_v, g_gain_one, g_shift_one), d_input


def adamw(weight, moments, grad, rate):
    first = 0.5 * moments[0] + 0.5 * grad
    root = jnp.sqrt(0.5 * moments[1] * moments[1] + 0.5 * grad * grad)
    update = first / (root + 1e-08)
    return (weight - rate * (update + 0.1 * weight), jnp.stack([first, root]))


def shards(
    tokens,
    cotangent,
    expert_index,
    qkv_weight,
    out_weight,
    router_weight,
    up_weight,
    up_bias,
    down_weight,
    vectors,
    qkv_moments,
    out_moments,
    router_moments,
    up_moments,
    up_bias_moments,
    down_moments,
    vector_moments,
):
    rows = tokens.shape[0]
    micro = rows // MB_TOK
    gs = qkv_weight.shape[0]
    group_size = D // gs
    core = lax.axis_index("core")

    dense_in = pack_dense(qkv_weight, out_weight, router_weight, vectors, up_bias)
    width = dense_in.shape[1]
    dense_in = jnp.pad(dense_in, ((0, 0), (0, DENSE_AG - width))).astype(BF16)
    w_up_all, w_down_all, dense = ring_all_gather(
        up_weight.astype(BF16), down_weight.astype(BF16), dense_in, group_size, 1
    )
    w_qkv, w_out, w_router, table_b, b_up_b = unpack_dense(dense[:, :width])
    table = table_b.astype(F32)
    b_up = b_up_b.astype(F32)

    value = tokens.astype(F32)
    d_out = cotangent.astype(F32)
    first, qkv, log_total, attended, resid = attention_fwd(w_qkv, w_out, table, value)
    second = layer_norm(resid, table[5], table[6]).astype(BF16)
    logits = dot(second, w_router)
    probs = jax.nn.softmax(logits, -1)
    picked = expert_index[:, :, None] == jnp.arange(E, dtype=jnp.int32)
    gate = jnp.sum(jnp.where(picked, probs[:, None, :], 0.0), -1)

    route = expert_index.reshape(micro, MB_TOK, 2)
    places, counts = assign_places(route)
    counts = counts.T.reshape(E * micro)
    onehot = (places[:, :, None] == jnp.arange(E * CAPP, dtype=jnp.int32)).astype(BF16)
    second_m = second.reshape(micro, MB_TOK, D)
    pair = jnp.concatenate([second_m, second_m], 1)
    table_in = jnp.einsum("mnr,mnd->mrd", onehot, pair, preferred_element_type=F32).astype(BF16)

    hidden_pre, hidden, y_all = ffn_forward(
        counts, table_in, w_up_all, b_up[:, None, :], w_down_all, table[7 : 7 + E][:, None, :], micro
    )
    picked_rows = pick_rows(onehot, y_all)
    out_zero = picked_rows[:, :MB_TOK].reshape(rows, D)
    out_one = picked_rows[:, MB_TOK:].reshape(rows, D)
    result = resid + (gate[:, 0:1] * out_zero + gate[:, 1:2] * out_one)

    d_gate = jnp.stack([jnp.sum(d_out * out_zero, -1), jnp.sum(d_out * out_one, -1)], 1)
    d_out_m = d_out.reshape(micro, MB_TOK, D)
    gate_m = gate.reshape(micro, MB_TOK, 2)
    weighted = jnp.concatenate([gate_m[:, :, 0:1] * d_out_m, gate_m[:, :, 1:2] * d_out_m], 1).astype(BF16)
    d_expert = jnp.einsum("mnr,mnd->mrd", onehot, weighted, preferred_element_type=F32).astype(BF16)

    d_table, g_up, g_down, g_b1, g_b2 = ffn_backward(counts, d_expert, table_in, hidden_pre, hidden, w_up_all, w_down_all, micro)
    g_up_bias_all = g_b1[:, 0, :]
    g_bias_down = g_b2[:, 0, :]

    onehot_sum = onehot[:, :MB_TOK] + onehot[:, MB_TOK:]
    d_picked = pick_rows(onehot_sum, d_table).reshape(rows, D)

    d_probs = jnp.sum(jnp.where(picked, d_gate[:, :, None], 0.0), 1)
    d_logit = (probs * (d_probs - jnp.sum(d_probs * probs, -1, keepdims=True))).astype(BF16)
    g_router = lax.dot_general(second, d_logit, (((0,), (0,)), ((), ())), preferred_element_type=F32)
    d_second = d_picked + lax.dot_general(d_logit, w_router, (((1,), (1,)), ((), ())), preferred_element_type=F32)
    norm_pull = jax.vjp(layer_norm, resid, table[5], table[6])[1]
    d_resid, g_gain_two, g_shift_two = norm_pull(d_second)
    d_resid = d_out + d_resid

    att_grads, d_input = attention_bwd(w_qkv, w_out, table, value, first, qkv, log_total, attended, d_resid)
    g_qkv, g_out, g_bias_out, g_bias_q, g_bias_v, g_gain_one, g_shift_one = att_grads
    input_grad = d_resid + d_input

    g_table = jnp.concatenate(
        [
            jnp.stack([g_gain_one, g_shift_one, g_bias_q, g_bias_v, g_bias_out, g_gain_two, g_shift_two]),
            g_bias_down,
        ],
        0,
    )
    dense_g = pack_dense(g_qkv, g_out, g_router, g_table, g_up_bias_all)
    width = dense_g.shape[1]
    dense_g = jnp.pad(dense_g, ((0, 0), (0, DENSE_AG - width))).astype(BF16)
    x_pair = lax.axis_size("rx") == 2
    r_up, r_down, r_dense = grad_reduce(g_up, g_down, dense_g, group_size, x_pair, 0)
    if not x_pair:
        r_up, r_down, r_dense = lax.psum((r_up, r_down, r_dense), "rx")
    r_qkv, r_out, r_router, r_table, r_ub = unpack_dense(r_dense[:, :width])

    reduced = (r_qkv, r_out, r_router, r_up, r_ub, r_down, r_table)
    rates = (
        2.0 * D ** (-0.5),
        2.0 * (D // 32) ** (-0.5),
        2.0 * (2 * D) ** (-0.5),
        2.0 * D ** (-0.5),
        0.2,
        2.0 * (F // 16) ** (-0.5),
        0.2,
    )
    params = (qkv_weight, out_weight, router_weight, up_weight, up_bias, down_weight, vectors)
    moments = (qkv_moments, out_moments, router_moments, up_moments, up_bias_moments, down_moments, vector_moments)
    news = []
    states = []
    for weight, state, grad, rate in zip(params, moments, reduced, rates):
        new_weight, new_state = adamw(weight, state, grad, rate)
        news.append(new_weight)
        states.append(new_state)
    return (result.astype(BF16), input_grad) + reduced + tuple(news) + tuple(states)


def solution(mesh):
    replica, group = mesh.shape["replica"], mesh.shape["group"]
    view = Mesh(np.asarray(mesh.devices).reshape(replica // 2, 2, group), ("rx", "core", "group"))
    in_specs = (
        P(TOK, None),
        P(TOK, None),
        P(TOK, None),
        P("group", None),
        P("group", None),
        P("group", None),
        P(None, "group", None),
        P(None, "group"),
        P(None, "group", None),
        P(None, "group"),
        P(None, "group", None),
        P(None, "group", None),
        P(None, "group", None),
        P(None, None, "group", None),
        P(None, None, "group"),
        P(None, None, "group", None),
        P(None, None, "group"),
    )
    out_specs = (
        P(TOK, None),
        P(TOK, None),
        P("group", None),
        P("group", None),
        P("group", None),
        P(None, "group", None),
        P(None, "group"),
        P(None, "group", None),
        P(None, "group"),
        P("group", None),
        P("group", None),
        P("group", None),
        P(None, "group", None),
        P(None, "group"),
        P(None, "group", None),
        P(None, "group"),
        P(None, "group", None),
        P(None, "group", None),
        P(None, "group", None),
        P(None, None, "group", None),
        P(None, None, "group"),
        P(None, None, "group", None),
        P(None, None, "group"),
    )
    return jax.shard_map(shards, mesh=view, in_specs=in_specs, out_specs=out_specs, check_vma=False)
```

profile of v0, /device:TPU:1, one launch (start us, length us, event | category | flops | bytes accessed | tf_op | source)
XLA Modules:
  0.0 543.7 jit_solution(15580018740932879865)
XLA Ops:
  0.7 2.9 convert_element_type.104.refs_0_
  3.6 1.1 convert_element_type.105.refs_1_
  6.2 101.1 %shard_map.344 = (bf16[4,512,2048]{2,1,0:T(8,128)(2,1)}, bf16[4,2048,512]{2,1,0:T(8,128)(2,1)}, bf16[512,2560]{1,0:T(8,128)(2,1)}) custom-call(bf16[4,64,2048]{2,1,0:T(8,128)(2,1)} %convert_element_type.104.refs_0_, bf16[4,256,512]{2,1,0:T(8,128)(2,1)} %convert_element_type.105.refs_1_, bf16[64,2560]{1,0:T(8,128)(2,1)} %pad.14.refs_2_), custom_call_target="tpu_custom_call" | custom-call | bytes 19398656 | tf_op jit(solution)/shard_map/pallas_call | solution.py:271
  107.3 4.5 copy.323
  115.0 3.0 add_convert_fusion
  118.0 1.3 fusion.103
  120.1 1.0 copy.327
  121.2 3.5 reshape.321
  124.7 2.0 copy.328
  126.8 1.1 multiply_reduce_fusion.1
  127.9 1.3 fusion.7
  129.2 1.5 copy-done.2
  131.6 1.2 copy.329
  132.8 4.8 fusion.49
  139.4 2.1 fusion.107
  142.2 1.4 fusion.108
  144.1 2.3 reduce-window.6
  147.4 7.3 %fusion.9.x_ref = bf16[2,2048,512]{2,1,0:T(8,128)(2,1)} fusion(s32[2,788]{1,0:T(2,128)S(1)} %multiply_add_fusion.6, bf16[2,394,512]{2,1,0:T(8,128)(2,1)S(1)} %reshape.297), kind=kOutput, calls=%fused_computation.19 | convolution fusion | flops 3313664000 | bytes 5007520 | tf_op jit(solution)/shard_map/mnr,mnd->mrd/dot_general | solution.py:786
  157.9 2.2 copy-done
  160.0 39.6 %shard_map.345 = (f32[2,2048,2048]{2,1,0:T(8,128)}, bf16[2,2048,2048]{2,1,0:T(8,128)(2,1)}, bf16[2,2048,1024]{2,1,0:T(8,128)(2,1)}) custom-call(s32[8]{0:T(128)S(1)} %reshape.296.counts, bf16[2,2048,512]{2,1,0:T(8,128)(2,1)S(1)} %copy-done, bf16[4,512,2048]{2,1,0:T(8,128)(2,1)} %get-tuple-element.38.w1_ref, f32[4,1,2048]{2,1,0:T(1,128)S(1)} %reshape.318.b1_ref, ...), custom_call_target="tpu_custom_call" | custom-call | flops 8589934592 | bytes 31457280 | tf_op jit(solution)/shard_map/pallas_call | solution.py:524
  199.6 9.7 %fusion.2 = f32[2,788,1024]{2,1,0:T(8,128)S(1)} fusion(bf16[2,2048,1024]{2,1,0:T(8,128)(2,1)} %get-tuple-element.40, s32[2,788]{1,0:T(2,128)S(1)} %multiply_add_fusion.6), kind=kOutput, calls=%fused_computation.3 | convolution fusion | flops 6613450752 | bytes 14850208 | tf_op jit(solution)/shard_map/mnr,mrd->mnd/dot_general | solution.py:651
  210.2 2.1 fusion.102
  212.3 1.6 reshape.298
  213.9 2.7 reshape.299
  216.6 2.1 multiply_reduce_fusion.5
  219.0 2.5 reshape.301
  221.5 1.7 multiply_convert_fusion.4
  223.2 7.3 %fusion.10.dy_ref = bf16[2,2048,512]{2,1,0:T(8,128)(2,1)} fusion(s32[2,788]{1,0:T(2,128)S(1)} %multiply_add_fusion.6, bf16[2,394,512]{2,1,0:T(8,128)(2,1)S(1)} %get-tuple-element.226, bf16[2,394,512]{2,1,0:T(8,128)(2,1)S(1)} %get-tuple-element.225), kind=kOutput, calls=%fused_computation.20 | convolution fusion | flops 3313664000 | bytes 5814432 | tf_op jit(solution)/shard_map/mnr,mnd->mrd/dot_general | solution.py:800
  230.4 58.3 %shard_map.346 = (bf16[2,2048,1024]{2,1,0:T(8,128)(2,1)}, bf16[4,512,2048]{2,1,0:T(8,128)(2,1)}, bf16[4,2048,512]{2,1,0:T(8,128)(2,1)}, f32[4,1,2048]{2,1,0:T(1,128)}, f32[4,1,512]{2,1,0:T(1,128)}) custom-call(s32[8]{0:T(128)} %copy-done.1, bf16[2,2048,512]{2,1,0:T(8,128)(2,1)} %fusion.10.dy_ref, bf16[2,2048,512]{2,1,0:T(8,128)(2,1)} %fusion.9.x_ref, ...), custom_call_target="tpu_custom_call" | custom-call | flops 17179869184 | bytes 100663296 | tf_op jit(solution)/shard_map/pallas_call | solution.py:602
  288.7 1.1 fusion.1
  289.9 5.9 %fusion.13 = f32[2,394,1024]{2,1,0:T(8,128)S(1)} fusion(bf16[2,2048,1024]{2,1,0:T(8,128)(2,1)} %get-tuple-element.43, bf16[2,788,2048]{2,1,0:T(8,128)(2,1)S(1)} %fusion.1), kind=kOutput, calls=%fused_computation.23 | convolution fusion | flops 3306725376 | bytes 18169856 | tf_op jit(solution)/shard_map/mnr,mrd->mnd/dot_general | solution.py:651
  295.8 1.5 slice_add_fusion.3
  297.3 2.7 reshape.302
  300.1 2.6 multiply_reduce_fusion.2
  302.7 1.7 fusion.101
  304.4 1.2 copy-done.5
  306.8 1.7 convolution_convert_fusion.1
  309.3 1.0 copy.337
  310.3 4.2 fusion.46
  314.5 1.8 copy.347
  316.3 3.6 reshape.306
  320.0 7.8 %multiply_reduce_fusion = (f32[4,8,197]{2,1,0:T(8,128)S(1)}, f32[4,8,197,197]{2,3,1,0:T(8,128)}) fusion(f32[4,8,197,197]{2,3,1,0:T(8,128)} %copy-done.2, f32[4,8,197]{2,1,0:T(8,128)S(1)} %log_add_fusion, bf16[4,197,8,64]{1,3,2,0:T(8,128)(2,1)S(1)} %copy.337, bf16[4,197,8,64]{1,3,2,0:T(8,128)(2,1)} %copy-done.23), kind=kOutput, calls=%fused_computation.6 | convolution fusion | flops 163922912 | bytes 11599360 | tf_op jit(solution)/shard_map/bqhd,bkhd->bhqk/dot_general | solution.py:712
  327.8 4.5 multiply_convert_fusion
  332.3 1.2 fusion.51
  335.6 2.7 fusion.50
  344.3 2.0 fusion.98
  346.3 1.1 copy-done.20
  347.4 1.5 fusion.30
  350.5 1.5 convolution_convert_fusion.2
  352.5 3.4 convolution_convert_fusion
  355.9 1.1 reshape_squeeze.4
  357.4 4.4 concatenate.46
  361.8 3.3 pad.16.refs_2_
  365.2 134.8 %shard_map.347 = (f32[4,64,2048]{2,1,0:T(8,128)}, f32[4,256,512]{2,1,0:T(8,128)}, f32[64,2560]{1,0:T(8,128)}) custom-call(bf16[4,512,2048]{2,1,0:T(8,128)(2,1)} %get-tuple-element.44.refs_0_, bf16[4,2048,512]{2,1,0:T(8,128)(2,1)} %get-tuple-element.45.refs_1_, bf16[512,2560]{1,0:T(8,128)(2,1)} %pad.16.refs_2_), custom_call_target="tpu_custom_call" | custom-call | flops 9699328 | bytes 19398656 | tf_op jit(solution)/shard_map/pallas_call | solution.py:462
  501.9 6.2 %fusion.54 = (f32[1,4,256,512]{3,2,1,0:T(8,128)S(1)}, f32[1,4,256,512]{3,2,1,0:T(8,128)S(1)}, f32[4,256,512]{2,1,0:T(8,128)}) fusion(f32[4,256,512]{2,1,0:T(8,128)} %get-tuple-element.296, f32[2,4,256,512]{3,2,1,0:T(8,128)} %param.32, f32[4,256,512]{2,1,0:T(8,128)} %param.25), kind=kLoop, calls=%fused_computation.99 | loop fusion | flops 6815744 | bytes 14680064 | tf_op jit(solution)/shard_map/stack | solution.py:733
  508.1 2.5 pad_maximum_fusion.1
  511.6 6.5 %fusion.53 = (f32[1,4,64,2048]{3,2,1,0:T(8,128)S(1)}, f32[1,4,64,2048]{3,2,1,0:T(8,128)S(1)}, f32[4,64,2048]{2,1,0:T(8,128)}) fusion(f32[4,64,2048]{2,1,0:T(8,128)} %get-tuple-element.294, f32[2,4,64,2048]{3,2,1,0:T(8,128)} %param.30, f32[4,64,2048]{2,1,0:T(8,128)} %param.23), kind=kLoop, calls=%fused_computation.98 | loop fusion | flops 6815744 | bytes 14680064 | tf_op jit(solution)/shard_map/stack | solution.py:733
  518.1 2.5 pad_maximum_fusion
  524.6 2.4 fusion.68
  531.7 1.4 copy.369
  533.2 1.3 multiply_subtract_fusion.5
  536.8 3.1 add_add_fusion.2
  539.8 1.3 copy.396
  542.2 1.3 copy.397
  (262 shorter events, 41.8 us)
Async XLA Ops:
  0.7 2.9 copy-start.17
  3.5 1.1 copy-start.28
  3.5 1.2 copy-start.58
  3.5 1.6 copy-start.38
  3.5 1.6 copy-start.49
  3.6 1.7 copy-start.56
  107.3 6.4 %copy-start.9 = (bf16[788,512]{1,0:T(8,128)(2,1)S(1)}, bf16[788,512]{1,0:T(8,128)(2,1)}, u32[]{:S(2)}) copy-start(bf16[788,512]{1,0:T(8,128)(2,1)} %param.17) | copy-start | bytes 2420740
  113.7 0.7 copy-start.63
  121.2 5.6 %copy-start.15 = (bf16[4,197,8,64]{1,3,2,0:T(8,128)(2,1)}, bf16[4,197,8,64]{1,3,2,0:T(8,128)(2,1)S(1)}, u32[]{:S(2)}) copy-start(bf16[4,197,8,64]{1,3,2,0:T(8,128)(2,1)S(1)} %copy.327) | copy-start | bytes 2420740
  126.8 1.1 copy-start.13
  127.9 2.8 copy-start.2
  127.9 2.8 copy-start.26
  132.8 4.8 copy-start.23
  139.4 2.1 copy-start.30
  139.4 2.5 copy-start.48
  139.4 2.5 copy-start.60
  141.9 2.0 copy-start.53
  142.2 12.4 %copy-start.7 = (bf16[788,512]{1,0:T(8,128)(2,1)}, bf16[788,512]{1,0:T(8,128)(2,1)S(1)}, u32[]{:S(2)}) copy-start(bf16[788,512]{1,0:T(8,128)(2,1)S(1)} %add_convert_fusion.2) | copy-start | bytes 2420740
  154.8 44.8 %copy-start.1 = (s32[8]{0:T(128)}, s32[8]{0:T(128)S(1)}, u32[]{:S(2)}) copy-start(s32[8]{0:T(128)S(1)} %reshape.296.counts) | copy-start | bytes 100
  157.9 2.2 copy-start
  218.9 81.2 %copy-start.42 = (bf16[788,4]{0,1:T(4,128)(2,1)}, bf16[788,4]{0,1:T(4,128)(2,1)S(1)}, u32[]{:S(2)}) copy-start(bf16[788,4]{0,1:T(4,128)(2,1)S(1)} %multiply_convert_fusion.5) | copy-start | bytes 18916
  300.1 2.6 copy-start.4
  302.7 2.9 copy-start.11
  304.4 1.2 copy-start.5
  304.4 1.5 copy-start.46
  305.9 0.9 copy-start.32
  316.3 11.5 %slice-start = ((s8[6553600]{0:T(1024)(128)(4,1)}), s8[2359296]{0:T(1024)(128)(4,1)S(1)}, s32[]{:S(2)}) async-start(s8[6553600]{0:T(1024)(128)(4,1)} %bitcast.190), calls=%async_computation | async-start | bytes 4718592
  319.9 7.8 %slice-start.1 = ((s8[6553600]{0:T(1024)(128)(4,1)}), s8[4194304]{0:T(1024)(128)(4,1)S(1)}, s32[]{:S(2)}) async-start(s8[6553600]{0:T(1024)(128)(4,1)} %bitcast.190), calls=%async_computation.1 | async-start | bytes 8388608
  327.8 4.5 copy-start.16
  332.3 1.7 copy-start.3
  334.0 1.7 copy-start.14
  340.0 1.2 copy-start.24
  341.3 1.5 copy-start.21
  341.7 1.7 copy-start.10
  341.7 2.6 copy-start.25
  341.7 2.6 copy-start.55
  344.3 3.1 copy-start.45
  344.3 4.6 copy-start.61
  346.2 1.2 copy-start.20
  346.2 3.2 copy-start.8
  346.3 3.2 copy-start.43
  346.3 4.2 copy-start.31
  346.3 4.2 copy-start.33
  348.9 3.1 copy-start.64
  350.5 2.0 copy-start.22
  352.4 3.4 copy-start.51
  352.4 5.0 copy-start.36
  352.5 5.0 copy-start.37
  365.2 134.8 %copy-start.59 = (f32[2,11,64]{2,0,1:T(2,128)S(1)}, f32[2,11,64]{2,0,1:T(2,128)}, u32[]{:S(2)}) copy-start(f32[2,11,64]{2,0,1:T(2,128)} %param.33) | copy-start | bytes 16900
  365.2 135.0 %copy-start.50 = (f32[11,64]{1,0:T(8,128)S(1)}, f32[11,64]{1,0:T(8,128)}, u32[]{:S(2)}) copy-start(f32[11,64]{1,0:T(8,128)} %param.26) | copy-start | bytes 8452
  508.1 2.5 copy-start.34
  508.1 2.9 copy-start.52
  518.1 2.5 copy-start.62
  518.1 4.1 copy-start.35
  518.1 4.2 copy-start.39
  520.7 3.1 copy-start.27
  522.3 4.7 copy-start.40
  523.9 0.7 copy-start.29
  524.6 12.1 %copy-start.6 = (f32[788,512]{1,0:T(8,128)S(1)}, f32[788,512]{1,0:T(8,128)}, u32[]{:S(2)}) copy-start(f32[788,512]{1,0:T(8,128)} %copy-done.5) | copy-start | bytes 4841476
  524.6 12.1 %copy-start.12 = (bf16[788,512]{1,0:T(8,128)(2,1)S(1)}, bf16[788,512]{1,0:T(8,128)(2,1)}, u32[]{:S(2)}) copy-start(bf16[788,512]{1,0:T(8,128)(2,1)} %param.18) | copy-start | bytes 2420740
  524.6 12.1 %copy-start.47 = (f32[788]{0:T(1024)S(1)}, f32[788]{0:T(1024)}, u32[]{:S(2)}) copy-start(f32[788]{0:T(1024)} %copy-done.46) | copy-start | bytes 9460
  533.2 6.6 %copy-start.57 = (f32[4,256]{1,0:T(4,128)}, f32[4,256]{1,0:T(4,128)S(1)}, u32[]{:S(2)}) copy-start(f32[4,256]{1,0:T(4,128)S(1)} %reshape.313) | copy-start | bytes 12292
  536.8 3.1 copy-start.19
  539.8 2.3 copy-start.18
  (3 other events, 1.9 us)
where the time goes:
time: 554 us; the launch traced here: 544 us
  Pallas kernels  334 us (60%)
  local copies, waits for them, and re-layouts  79 us (14%)
  matrix products  69.7 us (13%)
  other arithmetic  59.4 us (11%)
    pallas_call x1, Pallas kernels, grad_reduce(): pl.pallas_call(functools.partial(ring_rs2_kernel, groups, x_pair), out_sh...  135 us
    pallas_call x1, Pallas kernels, ring_all_gather(): pl.pallas_call(functools.partial(ring_ag_kernel, groups), out_shape=shape...  101 us
    pallas_call x1, Pallas kernels, ffn_backward(): pl.pallas_call(functools.partial(ffn_bwd_kernel, micro), grid_spec=grid_s...  58.3 us
    pallas_call x1, Pallas kernels, ffn_forward(): pl.pallas_call(functools.partial(ffn_fwd_kernel, micro), grid_spec=grid_s...  39.6 us
    another operation x15, other arithmetic, adamw(): return (weight - rate * (update + 0.1 * weight), jnp.stack([first, root]))  26 us
    unnamed x148, local copies, waits for them, and re-layouts  21.7 us
    dot_general x2, matrix products, pick_rows(): both = jnp.einsum('mnr,mrd->mnd', onehot, split, preferred_element_type=F32)  15.7 us
    reshape x8, local copies, waits for them, and re-layouts, split_heads(): return part.reshape(-1, S, HEADS, HEAD_DIM)  11.3 us

commit v1 on v0

--- a/solution.py
+++ b/solution.py
@@ -730,7 +730,9 @@
     first = 0.5 * moments[0] + 0.5 * grad
     root = jnp.sqrt(0.5 * moments[1] * moments[1] + 0.5 * grad * grad)
     update = first / (root + 1e-08)
-    return (weight - rate * (update + 0.1 * weight), jnp.stack([first, root]))
+    which = lax.broadcasted_iota(jnp.int32, moments.shape, 0) == 0
+    both = jnp.where(which, 0.5 * moments + 0.5 * grad, jnp.sqrt(0.5 * moments * moments + 0.5 * grad * grad))
+    return (weight - rate * (update + 0.1 * weight), both)
 
 
 def shards(

time: 554 us -> 553 us (level)
    another operation x27 -> x12, other arithmetic: 30.6 us -> 4.59 us  [the longest x15 26 us: adamw(): return (weight - rate * (update + 0.1 * weight), jnp.stack([first, root]))]
    mul x1 -> x10, other arithmetic: 0.7 us -> 18 us  [the longest x7 14.8 us: adamw(): first = 0.5 * moments[0] + 0.5 * grad]
    select_n x0 -> x7, other arithmetic: none -> 11.4 us  [adamw(): jnp.where(which, 0.5 * moments + 0.5 * grad, jnp.sqrt(0.5 * moments * mom...]
    unnamed x148 -> x158, local copies, waits for them, and re-layouts: 21.7 us -> 20.3 us
where the time goes in v1:
time: 553 us; the launch traced here: 543 us
  Pallas kernels  334 us (60%)
  local copies, waits for them, and re-layouts  76.7 us (14%)
  matrix products  70.4 us (13%)
  other arithmetic  60.1 us (11%)
    pallas_call x1, Pallas kernels, grad_reduce(): pl.pallas_call(functools.partial(ring_rs2_kernel, groups, x_pair), out_sh...  135 us
    pallas_call x1, Pallas kernels, ring_all_gather(): pl.pallas_call(functools.partial(ring_ag_kernel, groups), out_shape=shape...  101 us
    pallas_call x1, Pallas kernels, ffn_backward(): pl.pallas_call(functools.partial(ffn_bwd_kernel, micro), grid_spec=grid_s...  58.3 us
    pallas_call x1, Pallas kernels, ffn_forward(): pl.pallas_call(functools.partial(ffn_fwd_kernel, micro), grid_spec=grid_s...  39.6 us
    unnamed x158, local copies, waits for them, and re-layouts  20.3 us
    dot_general x2, matrix products, pick_rows(): both = jnp.einsum('mnr,mrd->mnd', onehot, split, preferred_element_type=F32)  15.7 us
    mul x7, other arithmetic, adamw(): first = 0.5 * moments[0] + 0.5 * grad  14.8 us
    select_n x7, other arithmetic, adamw(): jnp.where(which, 0.5 * moments + 0.5 * grad, jnp.sqrt(0.5 * moments * mom...  11.4 us

profile of v1, /device:TPU:1, one launch (start us, length us, event | category | flops | bytes accessed | tf_op | source)
XLA Modules:
  0.0 543.2 jit_solution(2035821952306571373)
XLA Ops:
  0.7 2.9 convert_element_type.104.refs_0_
  3.6 1.1 convert_element_type.105.refs_1_
  6.2 101.1 %shard_map.344 = (bf16[4,512,2048]{2,1,0:T(8,128)(2,1)}, bf16[4,2048,512]{2,1,0:T(8,128)(2,1)}, bf16[512,2560]{1,0:T(8,128)(2,1)}) custom-call(bf16[4,64,2048]{2,1,0:T(8,128)(2,1)} %convert_element_type.104.refs_0_, bf16[4,256,512]{2,1,0:T(8,128)(2,1)} %convert_element_type.105.refs_1_, bf16[64,2560]{1,0:T(8,128)(2,1)} %pad.14.refs_2_), custom_call_target="tpu_custom_call" | custom-call | bytes 19398656 | tf_op jit(solution)/shard_map/pallas_call | solution.py:271
  107.3 4.5 copy.322
  115.0 3.0 add_convert_fusion
  118.0 1.3 fusion.143
  120.1 1.0 copy.326
  121.2 3.5 reshape.319
  124.7 2.0 copy.327
  126.8 1.1 multiply_reduce_fusion.1
  127.9 1.3 fusion.7
  129.2 1.5 copy-done.2
  131.6 1.2 copy.328
  132.8 4.8 fusion.65
  139.4 2.1 fusion.147
  142.2 1.4 fusion.148
  144.1 2.3 reduce-window.6
  147.4 7.3 %fusion.15.x_ref = bf16[2,2048,512]{2,1,0:T(8,128)(2,1)} fusion(s32[2,788]{1,0:T(2,128)S(1)} %multiply_add_fusion.6, bf16[2,394,512]{2,1,0:T(8,128)(2,1)S(1)} %reshape.296), kind=kOutput, calls=%fused_computation.27 | convolution fusion | flops 3313664000 | bytes 5007520 | tf_op jit(solution)/shard_map/mnr,mnd->mrd/dot_general | solution.py:788
  157.8 2.2 copy-done
  160.0 39.6 %shard_map.345 = (f32[2,2048,2048]{2,1,0:T(8,128)}, bf16[2,2048,2048]{2,1,0:T(8,128)(2,1)}, bf16[2,2048,1024]{2,1,0:T(8,128)(2,1)}) custom-call(s32[8]{0:T(128)S(1)} %reshape.295.counts, bf16[2,2048,512]{2,1,0:T(8,128)(2,1)S(1)} %copy-done, bf16[4,512,2048]{2,1,0:T(8,128)(2,1)} %get-tuple-element.38.w1_ref, f32[4,1,2048]{2,1,0:T(1,128)S(1)} %reshape.316.b1_ref, ...), custom_call_target="tpu_custom_call" | custom-call | flops 8589934592 | bytes 31457280 | tf_op jit(solution)/shard_map/pallas_call | solution.py:524
  199.7 9.7 %fusion.2 = f32[2,788,1024]{2,1,0:T(8,128)S(1)} fusion(bf16[2,2048,1024]{2,1,0:T(8,128)(2,1)} %get-tuple-element.40, s32[2,788]{1,0:T(2,128)S(1)} %multiply_add_fusion.6), kind=kOutput, calls=%fused_computation.3 | convolution fusion | flops 6613450752 | bytes 14850208 | tf_op jit(solution)/shard_map/mnr,mrd->mnd/dot_general | solution.py:651
  210.2 2.1 fusion.142
  212.3 1.6 reshape.297
  213.9 2.7 reshape.298
  216.6 2.1 multiply_reduce_fusion.5
  219.0 2.5 reshape.300
  221.5 1.7 multiply_convert_fusion.4
  223.2 7.3 %fusion.16.dy_ref = bf16[2,2048,512]{2,1,0:T(8,128)(2,1)} fusion(s32[2,788]{1,0:T(2,128)S(1)} %multiply_add_fusion.6, bf16[2,394,512]{2,1,0:T(8,128)(2,1)S(1)} %get-tuple-element.226, bf16[2,394,512]{2,1,0:T(8,128)(2,1)S(1)} %get-tuple-element.225), kind=kOutput, calls=%fused_computation.28 | convolution fusion | flops 3313664000 | bytes 5814432 | tf_op jit(solution)/shard_map/mnr,mnd->mrd/dot_general | solution.py:802
  230.4 58.3 %shard_map.346 = (bf16[2,2048,1024]{2,1,0:T(8,128)(2,1)}, bf16[4,512,2048]{2,1,0:T(8,128)(2,1)}, bf16[4,2048,512]{2,1,0:T(8,128)(2,1)}, f32[4,1,2048]{2,1,0:T(1,128)}, f32[4,1,512]{2,1,0:T(1,128)}) custom-call(s32[8]{0:T(128)} %copy-done.1, bf16[2,2048,512]{2,1,0:T(8,128)(2,1)} %fusion.16.dy_ref, bf16[2,2048,512]{2,1,0:T(8,128)(2,1)} %fusion.15.x_ref, ...), custom_call_target="tpu_custom_call" | custom-call | flops 17179869184 | bytes 100663296 | tf_op jit(solution)/shard_map/pallas_call | solution.py:602
  288.8 1.1 fusion.1
  289.9 5.9 %fusion.19 = f32[2,394,1024]{2,1,0:T(8,128)S(1)} fusion(bf16[2,2048,1024]{2,1,0:T(8,128)(2,1)} %get-tuple-element.43, bf16[2,788,2048]{2,1,0:T(8,128)(2,1)S(1)} %fusion.1), kind=kOutput, calls=%fused_computation.31 | convolution fusion | flops 3306725376 | bytes 18169856 | tf_op jit(solution)/shard_map/mnr,mrd->mnd/dot_general | solution.py:651
  295.8 1.5 slice_add_fusion.3
  297.3 2.7 reshape.301
  300.1 2.6 multiply_reduce_fusion.2
  302.7 1.7 fusion.141
  304.5 1.2 copy-done.7
  306.8 1.7 convolution_convert_fusion.1
  309.3 1.0 copy.336
  310.4 4.2 fusion.62
  314.5 1.8 copy.346
  316.3 3.6 reshape.305
  320.0 7.8 %multiply_reduce_fusion = (f32[4,8,197]{2,1,0:T(8,128)S(1)}, f32[4,8,197,197]{2,3,1,0:T(8,128)}) fusion(f32[4,8,197,197]{2,3,1,0:T(8,128)} %copy-done.2, f32[4,8,197]{2,1,0:T(8,128)S(1)} %log_add_fusion, bf16[4,197,8,64]{1,3,2,0:T(8,128)(2,1)S(1)} %copy.336, bf16[4,197,8,64]{1,3,2,0:T(8,128)(2,1)} %copy-done.25), kind=kOutput, calls=%fused_computation.6 | convolution fusion | flops 163922912 | bytes 11599360 | tf_op jit(solution)/shard_map/bqhd,bkhd->bhqk/dot_general | solution.py:712
  327.8 4.5 multiply_convert_fusion
  332.3 1.2 fusion.67
  335.6 2.7 fusion.66
  344.3 2.0 fusion.138
  346.3 1.1 copy-done.22
  347.4 1.5 fusion.46
  350.5 1.5 convolution_convert_fusion.2
  352.4 4.1 convolution_convert_fusion
  356.7 1.1 reshape_squeeze.4
  358.2 4.4 concatenate.46
  362.6 3.3 pad.16.refs_2_
  365.9 134.9 %shard_map.347 = (f32[4,64,2048]{2,1,0:T(8,128)}, f32[4,256,512]{2,1,0:T(8,128)}, f32[64,2560]{1,0:T(8,128)}) custom-call(bf16[4,512,2048]{2,1,0:T(8,128)(2,1)} %get-tuple-element.44.refs_0_, bf16[4,2048,512]{2,1,0:T(8,128)(2,1)} %get-tuple-element.45.refs_1_, bf16[512,2560]{1,0:T(8,128)(2,1)} %pad.16.refs_2_), custom_call_target="tpu_custom_call" | custom-call | flops 9699328 | bytes 19398656 | tf_op jit(solution)/shard_map/pallas_call | solution.py:462
  502.9 6.4 %broadcast_multiply_fusion = (f32[4,256,512]{2,1,0:T(8,128)S(1)}, f32[4,256,512]{2,1,0:T(8,128)}, f32[4,256,512]{2,1,0:T(8,128)S(1)}) fusion(f32[4,256,512]{2,1,0:T(8,128)} %get-tuple-element.297, f32[4,256,512]{2,1,0:T(8,128)} %param.25, f32[2,4,256,512]{3,2,1,0:T(8,128)} %param.32), kind=kLoop, calls=%fused_computation.109 | loop fusion | flops 6815744 | bytes 14680064 | tf_op jit(solution)/shard_map/mul | solution.py:730
  509.3 3.7 fusion.12
  514.7 6.9 %broadcast_multiply_fusion.1 = (f32[4,64,2048]{2,1,0:T(8,128)S(1)}, f32[4,64,2048]{2,1,0:T(8,128)}, f32[4,64,2048]{2,1,0:T(8,128)S(1)}) fusion(f32[4,64,2048]{2,1,0:T(8,128)} %get-tuple-element.295, f32[4,64,2048]{2,1,0:T(8,128)} %param.23, f32[2,4,64,2048]{3,2,1,0:T(8,128)} %param.30), kind=kLoop, calls=%fused_computation.110 | loop fusion | flops 6815744 | bytes 14680064 | tf_op jit(solution)/shard_map/mul | solution.py:730
  521.6 3.7 fusion.9
  528.8 2.4 fusion.86
  531.2 1.2 fusion.71
  536.2 3.1 add_add_fusion.2
  539.3 1.3 copy.398
  540.6 1.0 copy-done.20
  541.6 1.3 copy.399
  (271 shorter events, 37.9 us)
Async XLA Ops:
  0.7 2.9 copy-start.19
  3.5 1.2 copy-start.64
  3.5 1.6 copy-start.41
  3.5 1.6 copy-start.53
  3.6 1.7 copy-start.60
  107.3 6.4 %copy-start.11 = (bf16[788,512]{1,0:T(8,128)(2,1)S(1)}, bf16[788,512]{1,0:T(8,128)(2,1)}, u32[]{:S(2)}) copy-start(bf16[788,512]{1,0:T(8,128)(2,1)} %param.17) | copy-start | bytes 2420740
  121.2 5.6 %copy-start.17 = (bf16[4,197,8,64]{1,3,2,0:T(8,128)(2,1)}, bf16[4,197,8,64]{1,3,2,0:T(8,128)(2,1)S(1)}, u32[]{:S(2)}) copy-start(bf16[4,197,8,64]{1,3,2,0:T(8,128)(2,1)S(1)} %copy.326) | copy-start | bytes 2420740
  127.9 2.8 copy-start.2
  127.9 2.8 copy-start.28
  132.8 4.8 copy-start.25
  139.3 2.1 copy-start.33
  139.3 2.5 copy-start.51
  139.3 2.5 copy-start.67
  141.9 2.0 copy-start.56
  142.2 12.4 %copy-start.9 = (bf16[788,512]{1,0:T(8,128)(2,1)}, bf16[788,512]{1,0:T(8,128)(2,1)S(1)}, u32[]{:S(2)}) copy-start(bf16[788,512]{1,0:T(8,128)(2,1)S(1)} %add_convert_fusion.2) | copy-start | bytes 2420740
  154.8 44.9 %copy-start.1 = (s32[8]{0:T(128)}, s32[8]{0:T(128)S(1)}, u32[]{:S(2)}) copy-start(s32[8]{0:T(128)S(1)} %reshape.295.counts) | copy-start | bytes 100
  157.8 2.2 copy-start
  218.9 81.2 %copy-start.44 = (bf16[788,4]{0,1:T(4,128)(2,1)}, bf16[788,4]{0,1:T(4,128)(2,1)S(1)}, u32[]{:S(2)}) copy-start(bf16[788,4]{0,1:T(4,128)(2,1)S(1)} %multiply_convert_fusion.5) | copy-start | bytes 18916
  300.1 2.6 copy-start.6
  302.7 2.9 copy-start.13
  304.4 1.2 copy-start.7
  304.5 1.5 copy-start.49
  316.3 11.4 %slice-start = ((s8[6553600]{0:T(1024)(128)(4,1)}), s8[2359296]{0:T(1024)(128)(4,1)S(1)}, s32[]{:S(2)}) async-start(s8[6553600]{0:T(1024)(128)(4,1)} %bitcast.132), calls=%async_computation | async-start | bytes 4718592
  320.0 7.8 %slice-start.1 = ((s8[6553600]{0:T(1024)(128)(4,1)}), s8[4194304]{0:T(1024)(128)(4,1)S(1)}, s32[]{:S(2)}) async-start(s8[6553600]{0:T(1024)(128)(4,1)} %bitcast.132), calls=%async_computation.1 | async-start | bytes 8388608
  327.8 4.5 copy-start.18
  332.3 1.7 copy-start.3
  334.0 1.7 copy-start.16
  340.0 1.2 copy-start.26
  341.3 1.5 copy-start.23
  341.7 1.7 copy-start.12
  341.7 2.6 copy-start.27
  341.7 2.6 copy-start.58
  344.3 3.1 copy-start.48
  344.3 4.7 copy-start.68
  346.2 1.2 copy-start.22
  346.2 3.2 copy-start.10
  346.2 3.2 copy-start.45
  346.3 4.2 copy-start.34
  346.3 4.2 copy-start.36
  348.9 3.1 copy-start.59
  350.5 2.0 copy-start.24
  352.4 4.1 copy-start.55
  352.4 5.7 %copy-start.38 = (bf16[512,512]{1,0:T(8,128)(2,1)S(1)}, bf16[512,512]{1,0:T(8,128)(2,1)}, u32[]{:S(2)}) copy-start(bf16[512,512]{1,0:T(8,128)(2,1)} %convolution_convert_fusion.2) | copy-start | bytes 1572868
  352.4 5.7 %copy-start.39 = (bf16[512,4]{1,0:T(8,128)(2,1)S(1)}, bf16[512,4]{1,0:T(8,128)(2,1)}, u32[]{:S(2)}) copy-start(bf16[512,4]{1,0:T(8,128)(2,1)} %copy.350) | copy-start | bytes 12292
  365.9 135.0 %copy-start.46 = (f32[2,11,64]{2,0,1:T(2,128)S(1)}, f32[2,11,64]{2,0,1:T(2,128)}, u32[]{:S(2)}) copy-start(f32[2,11,64]{2,0,1:T(2,128)} %param.33) | copy-start | bytes 16900
  365.9 135.2 %copy-start.54 = (f32[11,64]{1,0:T(8,128)S(1)}, f32[11,64]{1,0:T(8,128)}, u32[]{:S(2)}) copy-start(f32[11,64]{1,0:T(8,128)} %param.26) | copy-start | bytes 8452
  502.9 6.4 %copy-start.4 = (f32[2,4,256,512]{3,2,1,0:T(8,128)S(1)}, f32[2,4,256,512]{3,2,1,0:T(8,128)}, u32[]{:S(2)}) copy-start(f32[2,4,256,512]{3,2,1,0:T(8,128)} %param.32) | copy-start | bytes 12582916
  509.3 3.7 copy-start.37
  509.3 4.1 copy-start.52
  509.3 4.1 copy-start.65
  513.4 8.2 %copy-start.63 = (f32[4,256]{1,0:T(4,128)}, f32[4,256]{1,0:T(4,128)S(1)}, u32[]{:S(2)}) copy-start(f32[4,256]{1,0:T(4,128)S(1)} %reshape.312) | copy-start | bytes 12292
  514.7 6.9 %copy-start.5 = (f32[2,4,64,2048]{3,2,1,0:T(8,128)S(1)}, f32[2,4,64,2048]{3,2,1,0:T(8,128)}, u32[]{:S(2)}) copy-start(f32[2,4,64,2048]{3,2,1,0:T(8,128)} %param.30) | copy-start | bytes 12582916
  521.5 3.7 copy-start.66
  521.5 4.8 copy-start.32
  521.6 4.8 copy-start.42
  526.3 4.9 copy-start.40
  527.1 4.1 copy-start.29
  528.8 3.7 copy-start.61
  528.8 7.4 %copy-start.62 = (f32[788]{0:T(1024)S(1)}, f32[788]{0:T(1024)}, u32[]{:S(2)}) copy-start(f32[788]{0:T(1024)} %get-tuple-element.194) | copy-start | bytes 9460
  528.8 7.4 %copy-start.8 = (f32[788,512]{1,0:T(8,128)S(1)}, f32[788,512]{1,0:T(8,128)}, u32[]{:S(2)}) copy-start(f32[788,512]{1,0:T(8,128)} %copy-done.7) | copy-start | bytes 4841476
  528.8 7.4 %copy-start.14 = (bf16[788,512]{1,0:T(8,128)(2,1)S(1)}, bf16[788,512]{1,0:T(8,128)(2,1)}, u32[]{:S(2)}) copy-start(bf16[788,512]{1,0:T(8,128)(2,1)} %param.18) | copy-start | bytes 2420740
  528.8 7.4 %copy-start.50 = (f32[788]{0:T(1024)S(1)}, f32[788]{0:T(1024)}, u32[]{:S(2)}) copy-start(f32[788]{0:T(1024)} %copy-done.49) | copy-start | bytes 9460
  536.2 3.1 copy-start.21
  539.3 2.3 copy-start.20
  (8 other events, 6.5 us)

commit v2 on v1

--- a/solution.py
+++ b/solution.py
@@ -472,7 +472,7 @@
     )(gu, gd, gdense)
 
 
-TILE = 128
+TILE = 256
 TILE_B = 256
 CAPP = 512
 SQRT_HALF = float(np.sqrt(0.5))

time: 553 us -> 552 us (level)
  no operation moved by 1% of the time
where the time goes in v2:
time: 552 us; the launch traced here: 542 us
  Pallas kernels  333 us (60%)
  local copies, waits for them, and re-layouts  76.7 us (14%)
  matrix products  70.4 us (13%)
  other arithmetic  60.1 us (11%)
    pallas_call x1, Pallas kernels, grad_reduce(): pl.pallas_call(functools.partial(ring_rs2_kernel, groups, x_pair), out_sh...  135 us
    pallas_call x1, Pallas kernels, ring_all_gather(): pl.pallas_call(functools.partial(ring_ag_kernel, groups), out_shape=shape...  101 us
    pallas_call x1, Pallas kernels, ffn_backward(): pl.pallas_call(functools.partial(ffn_bwd_kernel, micro), grid_spec=grid_s...  58.3 us
    pallas_call x1, Pallas kernels, ffn_forward(): pl.pallas_call(functools.partial(ffn_fwd_kernel, micro), grid_spec=grid_s...  38.6 us
    unnamed x158, local copies, waits for them, and re-layouts  20.3 us
    dot_general x2, matrix products, pick_rows(): both = jnp.einsum('mnr,mrd->mnd', onehot, split, preferred_element_type=F32)  15.7 us
    mul x7, other arithmetic, adamw(): first = 0.5 * moments[0] + 0.5 * grad  14.8 us
    select_n x7, other arithmetic, adamw(): jnp.where(which, 0.5 * moments + 0.5 * grad, jnp.sqrt(0.5 * moments * mom...  11.4 us

profile of v2, /device:TPU:1, one launch (start us, length us, event | category | flops | bytes accessed | tf_op | source)
XLA Modules:
  0.0 542.2 jit_solution(6813233119179391443)
XLA Ops:
  0.7 2.9 convert_element_type.104.refs_0_
  3.6 1.1 convert_element_type.105.refs_1_
  6.2 101.1 %shard_map.344 = (bf16[4,512,2048]{2,1,0:T(8,128)(2,1)}, bf16[4,2048,512]{2,1,0:T(8,128)(2,1)}, bf16[512,2560]{1,0:T(8,128)(2,1)}) custom-call(bf16[4,64,2048]{2,1,0:T(8,128)(2,1)} %convert_element_type.104.refs_0_, bf16[4,256,512]{2,1,0:T(8,128)(2,1)} %convert_element_type.105.refs_1_, bf16[64,2560]{1,0:T(8,128)(2,1)} %pad.14.refs_2_), custom_call_target="tpu_custom_call" | custom-call | bytes 19398656 | tf_op jit(solution)/shard_map/pallas_call | solution.py:271
  107.3 4.5 copy.322
  115.0 3.0 add_convert_fusion
  118.0 1.3 fusion.143
  120.1 1.0 copy.326
  121.2 3.5 reshape.319
  124.7 2.0 copy.327
  126.8 1.1 multiply_reduce_fusion.1
  127.9 1.3 fusion.7
  129.2 1.5 copy-done.2
  131.6 1.2 copy.328
  132.8 4.8 fusion.65
  139.4 2.1 fusion.147
  142.2 1.4 fusion.148
  144.1 2.3 reduce-window.6
  147.4 7.3 %fusion.15.x_ref = bf16[2,2048,512]{2,1,0:T(8,128)(2,1)} fusion(s32[2,788]{1,0:T(2,128)S(1)} %multiply_add_fusion.6, bf16[2,394,512]{2,1,0:T(8,128)(2,1)S(1)} %reshape.296), kind=kOutput, calls=%fused_computation.27 | convolution fusion | flops 3313664000 | bytes 5007520 | tf_op jit(solution)/shard_map/mnr,mnd->mrd/dot_general | solution.py:788
  157.8 2.2 copy-done
  160.0 38.6 %shard_map.345 = (f32[2,2048,2048]{2,1,0:T(8,128)}, bf16[2,2048,2048]{2,1,0:T(8,128)(2,1)}, bf16[2,2048,1024]{2,1,0:T(8,128)(2,1)}) custom-call(s32[8]{0:T(128)S(1)} %reshape.295.counts, bf16[2,2048,512]{2,1,0:T(8,128)(2,1)S(1)} %copy-done, bf16[4,512,2048]{2,1,0:T(8,128)(2,1)} %get-tuple-element.38.w1_ref, f32[4,1,2048]{2,1,0:T(1,128)S(1)} %reshape.316.b1_ref, ...), custom_call_target="tpu_custom_call" | custom-call | flops 8589934592 | bytes 31457280 | tf_op jit(solution)/shard_map/pallas_call | solution.py:524
  198.7 9.7 %fusion.2 = f32[2,788,1024]{2,1,0:T(8,128)S(1)} fusion(bf16[2,2048,1024]{2,1,0:T(8,128)(2,1)} %get-tuple-element.40, s32[2,788]{1,0:T(2,128)S(1)} %multiply_add_fusion.6), kind=kOutput, calls=%fused_computation.3 | convolution fusion | flops 6613450752 | bytes 14850208 | tf_op jit(solution)/shard_map/mnr,mrd->mnd/dot_general | solution.py:651
  209.2 2.1 fusion.142
  211.3 1.6 reshape.297
  212.9 2.7 reshape.298
  215.6 2.1 multiply_reduce_fusion.5
  218.0 2.5 reshape.300
  220.5 1.7 multiply_convert_fusion.4
  222.2 7.3 %fusion.16.dy_ref = bf16[2,2048,512]{2,1,0:T(8,128)(2,1)} fusion(s32[2,788]{1,0:T(2,128)S(1)} %multiply_add_fusion.6, bf16[2,394,512]{2,1,0:T(8,128)(2,1)S(1)} %get-tuple-element.226, bf16[2,394,512]{2,1,0:T(8,128)(2,1)S(1)} %get-tuple-element.225), kind=kOutput, calls=%fused_computation.28 | convolution fusion | flops 3313664000 | bytes 5814432 | tf_op jit(solution)/shard_map/mnr,mnd->mrd/dot_general | solution.py:802
  229.4 58.3 %shard_map.346 = (bf16[2,2048,1024]{2,1,0:T(8,128)(2,1)}, bf16[4,512,2048]{2,1,0:T(8,128)(2,1)}, bf16[4,2048,512]{2,1,0:T(8,128)(2,1)}, f32[4,1,2048]{2,1,0:T(1,128)}, f32[4,1,512]{2,1,0:T(1,128)}) custom-call(s32[8]{0:T(128)} %copy-done.1, bf16[2,2048,512]{2,1,0:T(8,128)(2,1)} %fusion.16.dy_ref, bf16[2,2048,512]{2,1,0:T(8,128)(2,1)} %fusion.15.x_ref, ...), custom_call_target="tpu_custom_call" | custom-call | flops 17179869184 | bytes 100663296 | tf_op jit(solution)/shard_map/pallas_call | solution.py:602
  287.8 1.1 fusion.1
  288.9 5.9 %fusion.19 = f32[2,394,1024]{2,1,0:T(8,128)S(1)} fusion(bf16[2,2048,1024]{2,1,0:T(8,128)(2,1)} %get-tuple-element.43, bf16[2,788,2048]{2,1,0:T(8,128)(2,1)S(1)} %fusion.1), kind=kOutput, calls=%fused_computation.31 | convolution fusion | flops 3306725376 | bytes 18169856 | tf_op jit(solution)/shard_map/mnr,mrd->mnd/dot_general | solution.py:651
  294.8 1.5 slice_add_fusion.3
  296.4 2.7 reshape.301
  299.1 2.6 multiply_reduce_fusion.2
  301.7 1.7 fusion.141
  303.5 1.2 copy-done.7
  305.8 1.7 convolution_convert_fusion.1
  308.3 1.0 copy.336
  309.4 4.2 fusion.62
  313.5 1.8 copy.346
  315.3 3.6 reshape.305
  319.0 7.8 %multiply_reduce_fusion = (f32[4,8,197]{2,1,0:T(8,128)S(1)}, f32[4,8,197,197]{2,3,1,0:T(8,128)}) fusion(f32[4,8,197,197]{2,3,1,0:T(8,128)} %copy-done.2, f32[4,8,197]{2,1,0:T(8,128)S(1)} %log_add_fusion, bf16[4,197,8,64]{1,3,2,0:T(8,128)(2,1)S(1)} %copy.336, bf16[4,197,8,64]{1,3,2,0:T(8,128)(2,1)} %copy-done.25), kind=kOutput, calls=%fused_computation.6 | convolution fusion | flops 163922912 | bytes 11599360 | tf_op jit(solution)/shard_map/bqhd,bkhd->bhqk/dot_general | solution.py:712
  326.8 4.5 multiply_convert_fusion
  331.3 1.2 fusion.67
  334.6 2.7 fusion.66
  343.3 2.0 fusion.138
  345.3 1.1 copy-done.22
  346.4 1.5 fusion.46
  349.5 1.5 convolution_convert_fusion.2
  351.5 4.1 convolution_convert_fusion
  355.7 1.1 reshape_squeeze.4
  357.2 4.4 concatenate.46
  361.6 3.3 pad.16.refs_2_
  364.9 135.0 %shard_map.347 = (f32[4,64,2048]{2,1,0:T(8,128)}, f32[4,256,512]{2,1,0:T(8,128)}, f32[64,2560]{1,0:T(8,128)}) custom-call(bf16[4,512,2048]{2,1,0:T(8,128)(2,1)} %get-tuple-element.44.refs_0_, bf16[4,2048,512]{2,1,0:T(8,128)(2,1)} %get-tuple-element.45.refs_1_, bf16[512,2560]{1,0:T(8,128)(2,1)} %pad.16.refs_2_), custom_call_target="tpu_custom_call" | custom-call | flops 9699328 | bytes 19398656 | tf_op jit(solution)/shard_map/pallas_call | solution.py:462
  502.0 6.4 %broadcast_multiply_fusion = (f32[4,256,512]{2,1,0:T(8,128)S(1)}, f32[4,256,512]{2,1,0:T(8,128)}, f32[4,256,512]{2,1,0:T(8,128)S(1)}) fusion(f32[4,256,512]{2,1,0:T(8,128)} %get-tuple-element.297, f32[4,256,512]{2,1,0:T(8,128)} %param.25, f32[2,4,256,512]{3,2,1,0:T(8,128)} %param.32), kind=kLoop, calls=%fused_computation.109 | loop fusion | flops 6815744 | bytes 14680064 | tf_op jit(solution)/shard_map/mul | solution.py:730
  508.3 3.7 fusion.12
  513.7 6.9 %broadcast_multiply_fusion.1 = (f32[4,64,2048]{2,1,0:T(8,128)S(1)}, f32[4,64,2048]{2,1,0:T(8,128)}, f32[4,64,2048]{2,1,0:T(8,128)S(1)}) fusion(f32[4,64,2048]{2,1,0:T(8,128)} %get-tuple-element.295, f32[4,64,2048]{2,1,0:T(8,128)} %param.23, f32[2,4,64,2048]{3,2,1,0:T(8,128)} %param.30), kind=kLoop, calls=%fused_computation.110 | loop fusion | flops 6815744 | bytes 14680064 | tf_op jit(solution)/shard_map/mul | solution.py:730
  520.6 3.7 fusion.9
  527.8 2.4 fusion.86
  530.3 1.2 fusion.71
  535.3 3.1 add_add_fusion.2
  538.3 1.3 copy.398
  539.7 1.0 copy-done.20
  540.7 1.3 copy.399
  (271 shorter events, 37.9 us)
Async XLA Ops:
  0.7 2.9 copy-start.19
  3.5 1.2 copy-start.64
  3.5 1.6 copy-start.41
  3.5 1.6 copy-start.53
  3.6 1.7 copy-start.60
  107.3 6.4 %copy-start.11 = (bf16[788,512]{1,0:T(8,128)(2,1)S(1)}, bf16[788,512]{1,0:T(8,128)(2,1)}, u32[]{:S(2)}) copy-start(bf16[788,512]{1,0:T(8,128)(2,1)} %param.17) | copy-start | bytes 2420740
  121.2 5.6 %copy-start.17 = (bf16[4,197,8,64]{1,3,2,0:T(8,128)(2,1)}, bf16[4,197,8,64]{1,3,2,0:T(8,128)(2,1)S(1)}, u32[]{:S(2)}) copy-start(bf16[4,197,8,64]{1,3,2,0:T(8,128)(2,1)S(1)} %copy.326) | copy-start | bytes 2420740
  127.9 2.8 copy-start.2
  127.9 2.8 copy-start.28
  132.8 4.8 copy-start.25
  139.3 2.1 copy-start.33
  139.3 2.5 copy-start.51
  139.3 2.5 copy-start.67
  141.9 2.0 copy-start.56
  142.2 12.4 %copy-start.9 = (bf16[788,512]{1,0:T(8,128)(2,1)}, bf16[788,512]{1,0:T(8,128)(2,1)S(1)}, u32[]{:S(2)}) copy-start(bf16[788,512]{1,0:T(8,128)(2,1)S(1)} %add_convert_fusion.2) | copy-start | bytes 2420740
  154.8 43.9 %copy-start.1 = (s32[8]{0:T(128)}, s32[8]{0:T(128)S(1)}, u32[]{:S(2)}) copy-start(s32[8]{0:T(128)S(1)} %reshape.295.counts) | copy-start | bytes 100
  157.8 2.2 copy-start
  217.9 81.2 %copy-start.44 = (bf16[788,4]{0,1:T(4,128)(2,1)}, bf16[788,4]{0,1:T(4,128)(2,1)S(1)}, u32[]{:S(2)}) copy-start(bf16[788,4]{0,1:T(4,128)(2,1)S(1)} %multiply_convert_fusion.5) | copy-start | bytes 18916
  299.1 2.6 copy-start.6
  301.7 2.9 copy-start.13
  303.5 1.2 copy-start.7
  303.5 1.5 copy-start.49
  315.3 11.4 %slice-start = ((s8[6553600]{0:T(1024)(128)(4,1)}), s8[2359296]{0:T(1024)(128)(4,1)S(1)}, s32[]{:S(2)}) async-start(s8[6553600]{0:T(1024)(128)(4,1)} %bitcast.132), calls=%async_computation | async-start | bytes 4718592
  319.0 7.8 %slice-start.1 = ((s8[6553600]{0:T(1024)(128)(4,1)}), s8[4194304]{0:T(1024)(128)(4,1)S(1)}, s32[]{:S(2)}) async-start(s8[6553600]{0:T(1024)(128)(4,1)} %bitcast.132), calls=%async_computation.1 | async-start | bytes 8388608
  326.8 4.5 copy-start.18
  331.3 1.7 copy-start.3
  333.0 1.7 copy-start.16
  339.0 1.2 copy-start.26
  340.3 1.5 copy-start.23
  340.7 1.7 copy-start.12
  340.7 2.6 copy-start.27
  340.7 2.6 copy-start.58
  343.3 3.1 copy-start.48
  343.3 4.7 copy-start.68
  345.2 1.2 copy-start.22
  345.2 3.2 copy-start.10
  345.2 3.2 copy-start.45
  345.3 4.2 copy-start.34
  345.3 4.2 copy-start.36
  347.9 3.1 copy-start.59
  349.5 2.0 copy-start.24
  351.4 4.1 copy-start.55
  351.5 5.7 %copy-start.38 = (bf16[512,512]{1,0:T(8,128)(2,1)S(1)}, bf16[512,512]{1,0:T(8,128)(2,1)}, u32[]{:S(2)}) copy-start(bf16[512,512]{1,0:T(8,128)(2,1)} %convolution_convert_fusion.2) | copy-start | bytes 1572868
  351.5 5.7 %copy-start.39 = (bf16[512,4]{1,0:T(8,128)(2,1)S(1)}, bf16[512,4]{1,0:T(8,128)(2,1)}, u32[]{:S(2)}) copy-start(bf16[512,4]{1,0:T(8,128)(2,1)} %copy.350) | copy-start | bytes 12292
  364.9 135.0 %copy-start.46 = (f32[2,11,64]{2,0,1:T(2,128)S(1)}, f32[2,11,64]{2,0,1:T(2,128)}, u32[]{:S(2)}) copy-start(f32[2,11,64]{2,0,1:T(2,128)} %param.33) | copy-start | bytes 16900
  364.9 135.2 %copy-start.54 = (f32[11,64]{1,0:T(8,128)S(1)}, f32[11,64]{1,0:T(8,128)}, u32[]{:S(2)}) copy-start(f32[11,64]{1,0:T(8,128)} %param.26) | copy-start | bytes 8452
  502.0 6.4 %copy-start.4 = (f32[2,4,256,512]{3,2,1,0:T(8,128)S(1)}, f32[2,4,256,512]{3,2,1,0:T(8,128)}, u32[]{:S(2)}) copy-start(f32[2,4,256,512]{3,2,1,0:T(8,128)} %param.32) | copy-start | bytes 12582916
  508.3 3.7 copy-start.37
  508.3 4.1 copy-start.52
  508.3 4.1 copy-start.65
  512.4 8.2 %copy-start.63 = (f32[4,256]{1,0:T(4,128)}, f32[4,256]{1,0:T(4,128)S(1)}, u32[]{:S(2)}) copy-start(f32[4,256]{1,0:T(4,128)S(1)} %reshape.312) | copy-start | bytes 12292
  513.7 6.9 %copy-start.5 = (f32[2,4,64,2048]{3,2,1,0:T(8,128)S(1)}, f32[2,4,64,2048]{3,2,1,0:T(8,128)}, u32[]{:S(2)}) copy-start(f32[2,4,64,2048]{3,2,1,0:T(8,128)} %param.30) | copy-start | bytes 12582916
  520.6 3.7 copy-start.66
  520.6 4.8 copy-start.32
  520.6 4.8 copy-start.42
  525.4 4.9 copy-start.40
  526.2 4.1 copy-start.29
  527.8 3.7 copy-start.61
  527.8 7.4 %copy-start.62 = (f32[788]{0:T(1024)S(1)}, f32[788]{0:T(1024)}, u32[]{:S(2)}) copy-start(f32[788]{0:T(1024)} %get-tuple-element.194) | copy-start | bytes 9460
  527.8 7.4 %copy-start.8 = (f32[788,512]{1,0:T(8,128)S(1)}, f32[788,512]{1,0:T(8,128)}, u32[]{:S(2)}) copy-start(f32[788,512]{1,0:T(8,128)} %copy-done.7) | copy-start | bytes 4841476
  527.8 7.4 %copy-start.14 = (bf16[788,512]{1,0:T(8,128)(2,1)S(1)}, bf16[788,512]{1,0:T(8,128)(2,1)}, u32[]{:S(2)}) copy-start(bf16[788,512]{1,0:T(8,128)(2,1)} %param.18) | copy-start | bytes 2420740
  527.8 7.4 %copy-start.50 = (f32[788]{0:T(1024)S(1)}, f32[788]{0:T(1024)}, u32[]{:S(2)}) copy-start(f32[788]{0:T(1024)} %copy-done.49) | copy-start | bytes 9460
  535.3 3.1 copy-start.21
  538.3 2.3 copy-start.20
  (8 other events, 6.5 us)

commit v3 on v2

--- a/solution.py
+++ b/solution.py
@@ -299,8 +299,8 @@
     gu, gd, gdense, out_up, out_down, out_dense = refs[:6]
     n_items = 5
     scr = refs[6:]
-    rbuf, sbuf, pbuf, own, fin, xr, cr = (scr[i * n_items : (i + 1) * n_items] for i in range(7))
-    ring_send, ring_recv, part_send, part_recv, load_sem, x_send, x_recv, c_send, c_recv = scr[7 * n_items :]
+    rbuf, sbuf, pbuf, own, fin, xr, cr, xs = (scr[i * n_items : (i + 1) * n_items] for i in range(8))
+    ring_send, ring_recv, part_send, part_recv, load_sem, x_send, x_recv, c_send, c_recv = scr[8 * n_items :]
     pos_of, dev_at = ring_order(groups)
     rx = lax.axis_index("rx")
     core = lax.axis_index("core")
@@ -351,65 +351,81 @@
         )
 
     sends = []
-    for d in range(2):
-        for j in range(n_items):
-            load(d, 0, 0, j).start()
-            c = part(d, 0, j)
-            c.start()
-            sends.append(c)
-    for s in range(groups):
-        slot = s % 2
+
+    def ring_wave(items):
         for d in range(2):
-            for j in range(n_items):
-                load(d, s, slot, j).wait()
-                if s + 1 < groups:
-                    load(d, s + 1, 1 - slot, j).start()
-                    c = part(d, s + 1, j)
-                    c.start()
-                    sends.append(c)
-                part(d, s, j).wait_recv()
-                val = own[j][d, slot].astype(F32) + pbuf[j][d, s].astype(F32)
-                if s > 0:
-                    ring(d, s - 1, j).wait_recv()
-                    val = val + rbuf[j][d, s - 1].astype(F32)
-                if s < groups - 1:
-                    sbuf[j][d, s] = val.astype(BF16)
-                    c = ring(d, s, j)
-                    c.start()
-                    sends.append(c)
-                else:
-                    fin[j][d] = val
-
-    for c in sends:
-        c.wait_send()
-    sends = []
-    if x_pair:
-        x_copies = []
+            for j in items:
+                load(d, 0, 0, j).start()
+                c = part(d, 0, j)
+                c.start()
+                sends.append(c)
+        for s in range(groups):
+            slot = s % 2
+            for d in range(2):
+                for j in items:
+                    load(d, s, slot, j).wait()
+                    if s + 1 < groups:
+                        load(d, s + 1, 1 - slot, j).start()
+                        c = part(d, s + 1, j)
+                        c.start()
+                        sends.append(c)
+                    part(d, s, j).wait_recv()
+                    val = own[j][d, slot].astype(F32) + pbuf[j][d, s].astype(F32)
+                    if s > 0:
+                        ring(d, s - 1, j).wait_recv()
+                        val = val + rbuf[j][d, s - 1].astype(F32)
+                    if s < groups - 1:
+                        sbuf[j][d, s] = val.astype(BF16)
+                        c = ring(d, s, j)
+                        c.start()
+                        sends.append(c)
+                    else:
+                        fin[j][d] = val
+
+    def x_start(items):
+        copies = []
         for d in range(2):
-            for j in range(n_items):
-                sbuf[j][d, 0] = fin[j][d].astype(BF16)
+            for j in items:
+                xs[j][d] = fin[j][d].astype(BF16)
                 c = pltpu.make_async_remote_copy(
-                    src_ref=sbuf[j].at[d, 0], dst_ref=xr[j].at[d], send_sem=x_send.at[d, j], recv_sem=x_recv.at[d, j],
+                    src_ref=xs[j].at[d], dst_ref=xr[j].at[d], send_sem=x_send.at[d, j], recv_sem=x_recv.at[d, j],
                     device_id=(1 - rx, core, g), device_id_type=MESH_ID,
                 )
                 c.start()
-                x_copies.append(c)
-        for c in x_copies:
+                copies.append(c)
+        sends.extend(copies)
+        return copies
+
+    def x_finish(items, copies):
+        for c in copies:
             c.wait_recv()
         for d in range(2):
-            for j in range(n_items):
-                fin[j][d] = sbuf[j][d, 0].astype(F32) + xr[j][d].astype(F32)
-        sends += x_copies
-
-    c_copies = []
-    for d in range(2):
-        for j in range(n_items):
-            c = pltpu.make_async_remote_copy(
-                src_ref=fin[j].at[d], dst_ref=cr[j].at[d], send_sem=c_send.at[d, j], recv_sem=c_recv.at[d, j],
-                device_id=(rx, other, g), device_id_type=MESH_ID,
-            )
-            c.start()
-            c_copies.append(c)
+            for j in items:
+                fin[j][d] = xs[j][d].astype(F32) + xr[j][d].astype(F32)
+
+    def c_start(items):
+        copies = []
+        for d in range(2):
+            for j in items:
+                c = pltpu.make_async_remote_copy(
+                    src_ref=fin[j].at[d], dst_ref=cr[j].at[d], send_sem=c_send.at[d, j], recv_sem=c_recv.at[d, j],
+                    device_id=(rx, other, g), device_id_type=MESH_ID,
+                )
+                c.start()
+                copies.append(c)
+        return copies
+
+    wave_a, wave_b = (0, 1, 4), (2, 3)
+    ring_wave(wave_a)
+    if x_pair:
+        xa = x_start(wave_a)
+    ring_wave(wave_b)
+    if x_pair:
+        x_finish(wave_a, xa)
+    c_copies = c_start(wave_a)
+    if x_pair:
+        x_finish(wave_b, x_start(wave_b))
+    c_copies += c_start(wave_b)
 
     def out_items(owner):
         found = []
@@ -440,7 +456,7 @@
     width = gdense.shape[1] // 2
     item_shapes = [(gs, F // 2), (fs, D // 2), (gs, F // 2), (fs, D // 2), (gs, width // 2)]
     scratch = []
-    for lead, dtype in (((2, groups - 1), BF16), ((2, groups - 1), BF16), ((2, groups), BF16), ((2, 2), BF16), ((2,), F32), ((2,), BF16), ((2,), F32)):
+    for lead, dtype in (((2, groups - 1), BF16), ((2, groups - 1), BF16), ((2, groups), BF16), ((2, 2), BF16), ((2,), F32), ((2,), BF16), ((2,), F32), ((2,), BF16)):
         scratch += [pltpu.VMEM(lead + shp, dtype) for shp in item_shapes]
     scratch += [
         pltpu.SemaphoreType.DMA((2, groups - 1, 5)),

time: 552 us -> 540 us (0.978)
  Pallas kernels: 333 us -> 322 us
    pallas_call x1, Pallas kernels: 135 us -> 124 us  [grad_reduce(): pl.pallas_call(functools.partial(ring_rs2_kernel, groups, x_pair), out_sh...]
where the time goes in v3:
time: 540 us; the launch traced here: 531 us
  Pallas kernels  322 us (60%)
  local copies, waits for them, and re-layouts  76.7 us (14%)
  matrix products  70.4 us (13%)
  other arithmetic  60.1 us (11%)
    pallas_call x1, Pallas kernels, grad_reduce(): pl.pallas_call(functools.partial(ring_rs2_kernel, groups, x_pair), out_sh...  124 us
    pallas_call x1, Pallas kernels, ring_all_gather(): pl.pallas_call(functools.partial(ring_ag_kernel, groups), out_shape=shape...  101 us
    pallas_call x1, Pallas kernels, ffn_backward(): pl.pallas_call(functools.partial(ffn_bwd_kernel, micro), grid_spec=grid_s...  58.3 us
    pallas_call x1, Pallas kernels, ffn_forward(): pl.pallas_call(functools.partial(ffn_fwd_kernel, micro), grid_spec=grid_s...  38.6 us
    unnamed x158, local copies, waits for them, and re-layouts  20.3 us
    dot_general x2, matrix products, pick_rows(): both = jnp.einsum('mnr,mrd->mnd', onehot, split, preferred_element_type=F32)  15.7 us
    mul x7, other arithmetic, adamw(): first = 0.5 * moments[0] + 0.5 * grad  14.8 us
    select_n x7, other arithmetic, adamw(): jnp.where(which, 0.5 * moments + 0.5 * grad, jnp.sqrt(0.5 * moments * mom...  11.4 us

profile of v3, /device:TPU:1, one launch (start us, length us, event | category | flops | bytes accessed | tf_op | source)
XLA Modules:
  0.0 531.0 jit_solution(11082402075555878890)
XLA Ops:
  0.7 2.9 convert_element_type.104.refs_0_
  3.6 1.1 convert_element_type.105.refs_1_
  6.2 101.1 %shard_map.344 = (bf16[4,512,2048]{2,1,0:T(8,128)(2,1)}, bf16[4,2048,512]{2,1,0:T(8,128)(2,1)}, bf16[512,2560]{1,0:T(8,128)(2,1)}) custom-call(bf16[4,64,2048]{2,1,0:T(8,128)(2,1)} %convert_element_type.104.refs_0_, bf16[4,256,512]{2,1,0:T(8,128)(2,1)} %convert_element_type.105.refs_1_, bf16[64,2560]{1,0:T(8,128)(2,1)} %pad.14.refs_2_), custom_call_target="tpu_custom_call" | custom-call | bytes 19398656 | tf_op jit(solution)/shard_map/pallas_call | solution.py:271
  107.3 4.5 copy.322
  115.0 3.0 add_convert_fusion
  118.0 1.3 fusion.143
  120.1 1.0 copy.326
  121.2 3.5 reshape.319
  124.7 2.0 copy.327
  126.8 1.1 multiply_reduce_fusion.1
  127.9 1.3 fusion.7
  129.2 1.5 copy-done.2
  131.6 1.2 copy.328
  132.8 4.8 fusion.65
  139.4 2.1 fusion.147
  142.2 1.4 fusion.148
  144.1 2.3 reduce-window.6
  147.4 7.3 %fusion.15.x_ref = bf16[2,2048,512]{2,1,0:T(8,128)(2,1)} fusion(s32[2,788]{1,0:T(2,128)S(1)} %multiply_add_fusion.6, bf16[2,394,512]{2,1,0:T(8,128)(2,1)S(1)} %reshape.296), kind=kOutput, calls=%fused_computation.27 | convolution fusion | flops 3313664000 | bytes 5007520 | tf_op jit(solution)/shard_map/mnr,mnd->mrd/dot_general | solution.py:804
  157.8 2.2 copy-done
  160.0 38.6 %shard_map.345 = (f32[2,2048,2048]{2,1,0:T(8,128)}, bf16[2,2048,2048]{2,1,0:T(8,128)(2,1)}, bf16[2,2048,1024]{2,1,0:T(8,128)(2,1)}) custom-call(s32[8]{0:T(128)S(1)} %reshape.295.counts, bf16[2,2048,512]{2,1,0:T(8,128)(2,1)S(1)} %copy-done, bf16[4,512,2048]{2,1,0:T(8,128)(2,1)} %get-tuple-element.38.w1_ref, f32[4,1,2048]{2,1,0:T(1,128)S(1)} %reshape.316.b1_ref, ...), custom_call_target="tpu_custom_call" | custom-call | flops 8589934592 | bytes 31457280 | tf_op jit(solution)/shard_map/pallas_call | solution.py:540
  198.7 9.7 %fusion.2 = f32[2,788,1024]{2,1,0:T(8,128)S(1)} fusion(bf16[2,2048,1024]{2,1,0:T(8,128)(2,1)} %get-tuple-element.40, s32[2,788]{1,0:T(2,128)S(1)} %multiply_add_fusion.6), kind=kOutput, calls=%fused_computation.3 | convolution fusion | flops 6613450752 | bytes 14850208 | tf_op jit(solution)/shard_map/mnr,mrd->mnd/dot_general | solution.py:667
  209.2 2.1 fusion.142
  211.3 1.6 reshape.297
  212.9 2.7 reshape.298
  215.6 2.1 multiply_reduce_fusion.5
  218.0 2.5 reshape.300
  220.5 1.7 multiply_convert_fusion.4
  222.2 7.3 %fusion.16.dy_ref = bf16[2,2048,512]{2,1,0:T(8,128)(2,1)} fusion(s32[2,788]{1,0:T(2,128)S(1)} %multiply_add_fusion.6, bf16[2,394,512]{2,1,0:T(8,128)(2,1)S(1)} %get-tuple-element.226, bf16[2,394,512]{2,1,0:T(8,128)(2,1)S(1)} %get-tuple-element.225), kind=kOutput, calls=%fused_computation.28 | convolution fusion | flops 3313664000 | bytes 5814432 | tf_op jit(solution)/shard_map/mnr,mnd->mrd/dot_general | solution.py:818
  229.4 58.3 %shard_map.346 = (bf16[2,2048,1024]{2,1,0:T(8,128)(2,1)}, bf16[4,512,2048]{2,1,0:T(8,128)(2,1)}, bf16[4,2048,512]{2,1,0:T(8,128)(2,1)}, f32[4,1,2048]{2,1,0:T(1,128)}, f32[4,1,512]{2,1,0:T(1,128)}) custom-call(s32[8]{0:T(128)} %copy-done.1, bf16[2,2048,512]{2,1,0:T(8,128)(2,1)} %fusion.16.dy_ref, bf16[2,2048,512]{2,1,0:T(8,128)(2,1)} %fusion.15.x_ref, ...), custom_call_target="tpu_custom_call" | custom-call | flops 17179869184 | bytes 100663296 | tf_op jit(solution)/shard_map/pallas_call | solution.py:618
  287.8 1.1 fusion.1
  288.9 5.9 %fusion.19 = f32[2,394,1024]{2,1,0:T(8,128)S(1)} fusion(bf16[2,2048,1024]{2,1,0:T(8,128)(2,1)} %get-tuple-element.43, bf16[2,788,2048]{2,1,0:T(8,128)(2,1)S(1)} %fusion.1), kind=kOutput, calls=%fused_computation.31 | convolution fusion | flops 3306725376 | bytes 18169856 | tf_op jit(solution)/shard_map/mnr,mrd->mnd/dot_general | solution.py:667
  294.8 1.5 slice_add_fusion.3
  296.4 2.7 reshape.301
  299.1 2.6 multiply_reduce_fusion.2
  301.8 1.7 fusion.141
  303.5 1.2 copy-done.7
  305.8 1.7 convolution_convert_fusion.1
  308.3 1.0 copy.336
  309.4 4.2 fusion.62
  313.6 1.8 copy.346
  315.4 3.6 reshape.305
  319.0 7.8 %multiply_reduce_fusion = (f32[4,8,197]{2,1,0:T(8,128)S(1)}, f32[4,8,197,197]{2,3,1,0:T(8,128)}) fusion(f32[4,8,197,197]{2,3,1,0:T(8,128)} %copy-done.2, f32[4,8,197]{2,1,0:T(8,128)S(1)} %log_add_fusion, bf16[4,197,8,64]{1,3,2,0:T(8,128)(2,1)S(1)} %copy.336, bf16[4,197,8,64]{1,3,2,0:T(8,128)(2,1)} %copy-done.25), kind=kOutput, calls=%fused_computation.6 | convolution fusion | flops 163922912 | bytes 11599360 | tf_op jit(solution)/shard_map/bqhd,bkhd->bhqk/dot_general | solution.py:728
  326.8 4.5 multiply_convert_fusion
  331.3 1.2 fusion.67
  334.7 2.7 fusion.66
  343.3 2.0 fusion.138
  345.3 1.1 copy-done.22
  346.4 1.5 fusion.46
  349.5 1.5 convolution_convert_fusion.2
  351.5 4.1 convolution_convert_fusion
  355.7 1.1 reshape_squeeze.4
  357.2 4.4 concatenate.46
  361.6 3.3 pad.16.refs_2_
  364.9 123.8 %shard_map.347 = (f32[4,64,2048]{2,1,0:T(8,128)}, f32[4,256,512]{2,1,0:T(8,128)}, f32[64,2560]{1,0:T(8,128)}) custom-call(bf16[4,512,2048]{2,1,0:T(8,128)(2,1)} %get-tuple-element.44.refs_0_, bf16[4,2048,512]{2,1,0:T(8,128)(2,1)} %get-tuple-element.45.refs_1_, bf16[512,2560]{1,0:T(8,128)(2,1)} %pad.16.refs_2_), custom_call_target="tpu_custom_call" | custom-call | flops 9699328 | bytes 19398656 | tf_op jit(solution)/shard_map/pallas_call | solution.py:478
  490.8 6.4 %broadcast_multiply_fusion = (f32[4,256,512]{2,1,0:T(8,128)S(1)}, f32[4,256,512]{2,1,0:T(8,128)}, f32[4,256,512]{2,1,0:T(8,128)S(1)}) fusion(f32[4,256,512]{2,1,0:T(8,128)} %get-tuple-element.297, f32[4,256,512]{2,1,0:T(8,128)} %param.25, f32[2,4,256,512]{3,2,1,0:T(8,128)} %param.32), kind=kLoop, calls=%fused_computation.109 | loop fusion | flops 6815744 | bytes 14680064 | tf_op jit(solution)/shard_map/mul | solution.py:746
  497.1 3.7 fusion.12
  502.5 6.9 %broadcast_multiply_fusion.1 = (f32[4,64,2048]{2,1,0:T(8,128)S(1)}, f32[4,64,2048]{2,1,0:T(8,128)}, f32[4,64,2048]{2,1,0:T(8,128)S(1)}) fusion(f32[4,64,2048]{2,1,0:T(8,128)} %get-tuple-element.295, f32[4,64,2048]{2,1,0:T(8,128)} %param.23, f32[2,4,64,2048]{3,2,1,0:T(8,128)} %param.30), kind=kLoop, calls=%fused_computation.110 | loop fusion | flops 6815744 | bytes 14680064 | tf_op jit(solution)/shard_map/mul | solution.py:746
  509.4 3.7 fusion.9
  516.6 2.4 fusion.86
  519.0 1.2 fusion.71
  524.1 3.1 add_add_fusion.2
  527.1 1.3 copy.398
  528.4 1.0 copy-done.20
  529.5 1.3 copy.399
  (271 shorter events, 37.9 us)
Async XLA Ops:
  0.7 2.9 copy-start.19
  3.5 1.2 copy-start.64
  3.5 1.6 copy-start.41
  3.5 1.6 copy-start.53
  3.6 1.7 copy-start.60
  107.3 6.4 %copy-start.11 = (bf16[788,512]{1,0:T(8,128)(2,1)S(1)}, bf16[788,512]{1,0:T(8,128)(2,1)}, u32[]{:S(2)}) copy-start(bf16[788,512]{1,0:T(8,128)(2,1)} %param.17) | copy-start | bytes 2420740
  121.2 5.6 %copy-start.17 = (bf16[4,197,8,64]{1,3,2,0:T(8,128)(2,1)}, bf16[4,197,8,64]{1,3,2,0:T(8,128)(2,1)S(1)}, u32[]{:S(2)}) copy-start(bf16[4,197,8,64]{1,3,2,0:T(8,128)(2,1)S(1)} %copy.326) | copy-start | bytes 2420740
  127.9 2.8 copy-start.2
  127.9 2.8 copy-start.28
  132.8 4.8 copy-start.25
  139.3 2.1 copy-start.33
  139.3 2.5 copy-start.51
  139.3 2.5 copy-start.67
  141.9 2.0 copy-start.56
  142.2 12.4 %copy-start.9 = (bf16[788,512]{1,0:T(8,128)(2,1)}, bf16[788,512]{1,0:T(8,128)(2,1)S(1)}, u32[]{:S(2)}) copy-start(bf16[788,512]{1,0:T(8,128)(2,1)S(1)} %add_convert_fusion.2) | copy-start | bytes 2420740
  154.8 43.9 %copy-start.1 = (s32[8]{0:T(128)}, s32[8]{0:T(128)S(1)}, u32[]{:S(2)}) copy-start(s32[8]{0:T(128)S(1)} %reshape.295.counts) | copy-start | bytes 100
  157.8 2.2 copy-start
  217.9 81.2 %copy-start.44 = (bf16[788,4]{0,1:T(4,128)(2,1)}, bf16[788,4]{0,1:T(4,128)(2,1)S(1)}, u32[]{:S(2)}) copy-start(bf16[788,4]{0,1:T(4,128)(2,1)S(1)} %multiply_convert_fusion.5) | copy-start | bytes 18916
  299.1 2.6 copy-start.6
  301.8 2.9 copy-start.13
  303.5 1.2 copy-start.7
  303.5 1.5 copy-start.49
  315.3 11.4 %slice-start = ((s8[6553600]{0:T(1024)(128)(4,1)}), s8[2359296]{0:T(1024)(128)(4,1)S(1)}, s32[]{:S(2)}) async-start(s8[6553600]{0:T(1024)(128)(4,1)} %bitcast.132), calls=%async_computation | async-start | bytes 4718592
  319.0 7.8 %slice-start.1 = ((s8[6553600]{0:T(1024)(128)(4,1)}), s8[4194304]{0:T(1024)(128)(4,1)S(1)}, s32[]{:S(2)}) async-start(s8[6553600]{0:T(1024)(128)(4,1)} %bitcast.132), calls=%async_computation.1 | async-start | bytes 8388608
  326.8 4.5 copy-start.18
  331.3 1.7 copy-start.3
  333.0 1.7 copy-start.16
  339.0 1.2 copy-start.26
  340.3 1.5 copy-start.23
  340.7 1.7 copy-start.12
  340.7 2.6 copy-start.27
  340.7 2.6 copy-start.58
  343.3 3.1 copy-start.48
  343.3 4.7 copy-start.68
  345.2 1.2 copy-start.22
  345.3 3.2 copy-start.10
  345.3 3.2 copy-start.45
  345.3 4.2 copy-start.34
  345.3 4.2 copy-start.36
  347.9 3.1 copy-start.59
  349.5 2.0 copy-start.24
  351.5 4.1 copy-start.55
  351.5 5.7 %copy-start.38 = (bf16[512,512]{1,0:T(8,128)(2,1)S(1)}, bf16[512,512]{1,0:T(8,128)(2,1)}, u32[]{:S(2)}) copy-start(bf16[512,512]{1,0:T(8,128)(2,1)} %convolution_convert_fusion.2) | copy-start | bytes 1572868
  351.5 5.7 %copy-start.39 = (bf16[512,4]{1,0:T(8,128)(2,1)S(1)}, bf16[512,4]{1,0:T(8,128)(2,1)}, u32[]{:S(2)}) copy-start(bf16[512,4]{1,0:T(8,128)(2,1)} %copy.350) | copy-start | bytes 12292
  364.9 123.8 %copy-start.46 = (f32[2,11,64]{2,0,1:T(2,128)S(1)}, f32[2,11,64]{2,0,1:T(2,128)}, u32[]{:S(2)}) copy-start(f32[2,11,64]{2,0,1:T(2,128)} %param.33) | copy-start | bytes 16900
  364.9 124.0 %copy-start.54 = (f32[11,64]{1,0:T(8,128)S(1)}, f32[11,64]{1,0:T(8,128)}, u32[]{:S(2)}) copy-start(f32[11,64]{1,0:T(8,128)} %param.26) | copy-start | bytes 8452
  490.8 6.4 %copy-start.4 = (f32[2,4,256,512]{3,2,1,0:T(8,128)S(1)}, f32[2,4,256,512]{3,2,1,0:T(8,128)}, u32[]{:S(2)}) copy-start(f32[2,4,256,512]{3,2,1,0:T(8,128)} %param.32) | copy-start | bytes 12582916
  497.1 3.7 copy-start.37
  497.1 4.1 copy-start.52
  497.1 4.1 copy-start.65
  501.2 8.2 %copy-start.63 = (f32[4,256]{1,0:T(4,128)}, f32[4,256]{1,0:T(4,128)S(1)}, u32[]{:S(2)}) copy-start(f32[4,256]{1,0:T(4,128)S(1)} %reshape.312) | copy-start | bytes 12292
  502.5 6.9 %copy-start.5 = (f32[2,4,64,2048]{3,2,1,0:T(8,128)S(1)}, f32[2,4,64,2048]{3,2,1,0:T(8,128)}, u32[]{:S(2)}) copy-start(f32[2,4,64,2048]{3,2,1,0:T(8,128)} %param.30) | copy-start | bytes 12582916
  509.4 3.7 copy-start.66
  509.4 4.8 copy-start.32
  509.4 4.8 copy-start.42
  514.2 4.9 copy-start.40
  515.0 4.1 copy-start.29
  516.6 3.7 copy-start.61
  516.6 7.4 %copy-start.62 = (f32[788]{0:T(1024)S(1)}, f32[788]{0:T(1024)}, u32[]{:S(2)}) copy-start(f32[788]{0:T(1024)} %get-tuple-element.194) | copy-start | bytes 9460
  516.6 7.4 %copy-start.8 = (f32[788,512]{1,0:T(8,128)S(1)}, f32[788,512]{1,0:T(8,128)}, u32[]{:S(2)}) copy-start(f32[788,512]{1,0:T(8,128)} %copy-done.7) | copy-start | bytes 4841476
  516.6 7.4 %copy-start.14 = (bf16[788,512]{1,0:T(8,128)(2,1)S(1)}, bf16[788,512]{1,0:T(8,128)(2,1)}, u32[]{:S(2)}) copy-start(bf16[788,512]{1,0:T(8,128)(2,1)} %param.18) | copy-start | bytes 2420740
  516.6 7.4 %copy-start.50 = (f32[788]{0:T(1024)S(1)}, f32[788]{0:T(1024)}, u32[]{:S(2)}) copy-start(f32[788]{0:T(1024)} %copy-done.49) | copy-start | bytes 9460
  524.1 3.1 copy-start.21
  527.1 2.3 copy-start.20
  (8 other events, 6.5 us)

commit v4 on v3

--- a/solution.py
+++ b/solution.py
@@ -415,7 +415,7 @@
                 copies.append(c)
         return copies
 
-    wave_a, wave_b = (0, 1, 4), (2, 3)
+    wave_a, wave_b = (0, 1, 2, 4), (3,)
     ring_wave(wave_a)
     if x_pair:
         xa = x_start(wave_a)

time: 540 us -> 543 us (level)
  no operation moved by 1% of the time
where the time goes in v4:
time: 543 us; the launch traced here: 533 us
  Pallas kernels  324 us (60%)
  local copies, waits for them, and re-layouts  76.7 us (14%)
  matrix products  70.4 us (13%)
  other arithmetic  60.1 us (11%)
    pallas_call x1, Pallas kernels, grad_reduce(): pl.pallas_call(functools.partial(ring_rs2_kernel, groups, x_pair), out_sh...  126 us
    pallas_call x1, Pallas kernels, ring_all_gather(): pl.pallas_call(functools.partial(ring_ag_kernel, groups), out_shape=shape...  101 us
    pallas_call x1, Pallas kernels, ffn_backward(): pl.pallas_call(functools.partial(ffn_bwd_kernel, micro), grid_spec=grid_s...  58.3 us
    pallas_call x1, Pallas kernels, ffn_forward(): pl.pallas_call(functools.partial(ffn_fwd_kernel, micro), grid_spec=grid_s...  38.6 us
    unnamed x158, local copies, waits for them, and re-layouts  20.3 us
    dot_general x2, matrix products, pick_rows(): both = jnp.einsum('mnr,mrd->mnd', onehot, split, preferred_element_type=F32)  15.7 us
    mul x7, other arithmetic, adamw(): first = 0.5 * moments[0] + 0.5 * grad  14.8 us
    select_n x7, other arithmetic, adamw(): jnp.where(which, 0.5 * moments + 0.5 * grad, jnp.sqrt(0.5 * moments * mom...  11.4 us

profile of v4, /device:TPU:1, one launch (start us, length us, event | category | flops | bytes accessed | tf_op | source)
XLA Modules:
  0.0 533.4 jit_solution(6398461578714188890)
XLA Ops:
  0.7 2.9 convert_element_type.104.refs_0_
  3.6 1.1 convert_element_type.105.refs_1_
  6.2 101.1 %shard_map.344 = (bf16[4,512,2048]{2,1,0:T(8,128)(2,1)}, bf16[4,2048,512]{2,1,0:T(8,128)(2,1)}, bf16[512,2560]{1,0:T(8,128)(2,1)}) custom-call(bf16[4,64,2048]{2,1,0:T(8,128)(2,1)} %convert_element_type.104.refs_0_, bf16[4,256,512]{2,1,0:T(8,128)(2,1)} %convert_element_type.105.refs_1_, bf16[64,2560]{1,0:T(8,128)(2,1)} %pad.14.refs_2_), custom_call_target="tpu_custom_call" | custom-call | bytes 19398656 | tf_op jit(solution)/shard_map/pallas_call | solution.py:271
  107.3 4.5 copy.322
  115.0 3.0 add_convert_fusion
  118.0 1.3 fusion.143
  120.1 1.0 copy.326
  121.2 3.5 reshape.319
  124.7 2.0 copy.327
  126.8 1.1 multiply_reduce_fusion.1
  127.9 1.3 fusion.7
  129.2 1.5 copy-done.2
  131.6 1.2 copy.328
  132.8 4.8 fusion.65
  139.4 2.1 fusion.147
  142.2 1.4 fusion.148
  144.1 2.3 reduce-window.6
  147.4 7.3 %fusion.15.x_ref = bf16[2,2048,512]{2,1,0:T(8,128)(2,1)} fusion(s32[2,788]{1,0:T(2,128)S(1)} %multiply_add_fusion.6, bf16[2,394,512]{2,1,0:T(8,128)(2,1)S(1)} %reshape.296), kind=kOutput, calls=%fused_computation.27 | convolution fusion | flops 3313664000 | bytes 5007520 | tf_op jit(solution)/shard_map/mnr,mnd->mrd/dot_general | solution.py:804
  157.8 2.2 copy-done
  160.0 38.6 %shard_map.345 = (f32[2,2048,2048]{2,1,0:T(8,128)}, bf16[2,2048,2048]{2,1,0:T(8,128)(2,1)}, bf16[2,2048,1024]{2,1,0:T(8,128)(2,1)}) custom-call(s32[8]{0:T(128)S(1)} %reshape.295.counts, bf16[2,2048,512]{2,1,0:T(8,128)(2,1)S(1)} %copy-done, bf16[4,512,2048]{2,1,0:T(8,128)(2,1)} %get-tuple-element.38.w1_ref, f32[4,1,2048]{2,1,0:T(1,128)S(1)} %reshape.316.b1_ref, ...), custom_call_target="tpu_custom_call" | custom-call | flops 8589934592 | bytes 31457280 | tf_op jit(solution)/shard_map/pallas_call | solution.py:540
  198.7 9.7 %fusion.2 = f32[2,788,1024]{2,1,0:T(8,128)S(1)} fusion(bf16[2,2048,1024]{2,1,0:T(8,128)(2,1)} %get-tuple-element.40, s32[2,788]{1,0:T(2,128)S(1)} %multiply_add_fusion.6), kind=kOutput, calls=%fused_computation.3 | convolution fusion | flops 6613450752 | bytes 14850208 | tf_op jit(solution)/shard_map/mnr,mrd->mnd/dot_general | solution.py:667
  209.2 2.1 fusion.142
  211.3 1.6 reshape.297
  212.9 2.7 reshape.298
  215.6 2.1 multiply_reduce_fusion.5
  218.0 2.5 reshape.300
  220.5 1.7 multiply_convert_fusion.4
  222.2 7.3 %fusion.16.dy_ref = bf16[2,2048,512]{2,1,0:T(8,128)(2,1)} fusion(s32[2,788]{1,0:T(2,128)S(1)} %multiply_add_fusion.6, bf16[2,394,512]{2,1,0:T(8,128)(2,1)S(1)} %get-tuple-element.226, bf16[2,394,512]{2,1,0:T(8,128)(2,1)S(1)} %get-tuple-element.225), kind=kOutput, calls=%fused_computation.28 | convolution fusion | flops 3313664000 | bytes 5814432 | tf_op jit(solution)/shard_map/mnr,mnd->mrd/dot_general | solution.py:818
  229.4 58.3 %shard_map.346 = (bf16[2,2048,1024]{2,1,0:T(8,128)(2,1)}, bf16[4,512,2048]{2,1,0:T(8,128)(2,1)}, bf16[4,2048,512]{2,1,0:T(8,128)(2,1)}, f32[4,1,2048]{2,1,0:T(1,128)}, f32[4,1,512]{2,1,0:T(1,128)}) custom-call(s32[8]{0:T(128)} %copy-done.1, bf16[2,2048,512]{2,1,0:T(8,128)(2,1)} %fusion.16.dy_ref, bf16[2,2048,512]{2,1,0:T(8,128)(2,1)} %fusion.15.x_ref, ...), custom_call_target="tpu_custom_call" | custom-call | flops 17179869184 | bytes 100663296 | tf_op jit(solution)/shard_map/pallas_call | solution.py:618
  287.8 1.1 fusion.1
  288.9 5.9 %fusion.19 = f32[2,394,1024]{2,1,0:T(8,128)S(1)} fusion(bf16[2,2048,1024]{2,1,0:T(8,128)(2,1)} %get-tuple-element.43, bf16[2,788,2048]{2,1,0:T(8,128)(2,1)S(1)} %fusion.1), kind=kOutput, calls=%fused_computation.31 | convolution fusion | flops 3306725376 | bytes 18169856 | tf_op jit(solution)/shard_map/mnr,mrd->mnd/dot_general | solution.py:667
  294.8 1.5 slice_add_fusion.3
  296.4 2.7 reshape.301
  299.1 2.6 multiply_reduce_fusion.2
  301.7 1.7 fusion.141
  303.5 1.2 copy-done.7
  305.8 1.7 convolution_convert_fusion.1
  308.3 1.0 copy.336
  309.4 4.2 fusion.62
  313.5 1.8 copy.346
  315.3 3.6 reshape.305
  319.0 7.8 %multiply_reduce_fusion = (f32[4,8,197]{2,1,0:T(8,128)S(1)}, f32[4,8,197,197]{2,3,1,0:T(8,128)}) fusion(f32[4,8,197,197]{2,3,1,0:T(8,128)} %copy-done.2, f32[4,8,197]{2,1,0:T(8,128)S(1)} %log_add_fusion, bf16[4,197,8,64]{1,3,2,0:T(8,128)(2,1)S(1)} %copy.336, bf16[4,197,8,64]{1,3,2,0:T(8,128)(2,1)} %copy-done.25), kind=kOutput, calls=%fused_computation.6 | convolution fusion | flops 163922912 | bytes 11599360 | tf_op jit(solution)/shard_map/bqhd,bkhd->bhqk/dot_general | solution.py:728
  326.8 4.5 multiply_convert_fusion
  331.3 1.2 fusion.67
  334.6 2.7 fusion.66
  343.3 2.0 fusion.138
  345.3 1.1 copy-done.22
  346.4 1.5 fusion.46
  349.5 1.5 convolution_convert_fusion.2
  351.5 4.1 convolution_convert_fusion
  355.7 1.1 reshape_squeeze.4
  357.2 4.4 concatenate.46
  361.6 3.3 pad.16.refs_2_
  364.9 126.2 %shard_map.347 = (f32[4,64,2048]{2,1,0:T(8,128)}, f32[4,256,512]{2,1,0:T(8,128)}, f32[64,2560]{1,0:T(8,128)}) custom-call(bf16[4,512,2048]{2,1,0:T(8,128)(2,1)} %get-tuple-element.44.refs_0_, bf16[4,2048,512]{2,1,0:T(8,128)(2,1)} %get-tuple-element.45.refs_1_, bf16[512,2560]{1,0:T(8,128)(2,1)} %pad.16.refs_2_), custom_call_target="tpu_custom_call" | custom-call | flops 9699328 | bytes 19398656 | tf_op jit(solution)/shard_map/pallas_call | solution.py:478
  493.1 6.4 %broadcast_multiply_fusion = (f32[4,256,512]{2,1,0:T(8,128)S(1)}, f32[4,256,512]{2,1,0:T(8,128)}, f32[4,256,512]{2,1,0:T(8,128)S(1)}) fusion(f32[4,256,512]{2,1,0:T(8,128)} %get-tuple-element.297, f32[4,256,512]{2,1,0:T(8,128)} %param.25, f32[2,4,256,512]{3,2,1,0:T(8,128)} %param.32), kind=kLoop, calls=%fused_computation.109 | loop fusion | flops 6815744 | bytes 14680064 | tf_op jit(solution)/shard_map/mul | solution.py:746
  499.5 3.7 fusion.12
  504.9 6.9 %broadcast_multiply_fusion.1 = (f32[4,64,2048]{2,1,0:T(8,128)S(1)}, f32[4,64,2048]{2,1,0:T(8,128)}, f32[4,64,2048]{2,1,0:T(8,128)S(1)}) fusion(f32[4,64,2048]{2,1,0:T(8,128)} %get-tuple-element.295, f32[4,64,2048]{2,1,0:T(8,128)} %param.23, f32[2,4,64,2048]{3,2,1,0:T(8,128)} %param.30), kind=kLoop, calls=%fused_computation.110 | loop fusion | flops 6815744 | bytes 14680064 | tf_op jit(solution)/shard_map/mul | solution.py:746
  511.8 3.7 fusion.9
  519.0 2.4 fusion.86
  521.4 1.2 fusion.71
  526.4 3.1 add_add_fusion.2
  529.5 1.3 copy.398
  530.8 1.0 copy-done.20
  531.8 1.3 copy.399
  (271 shorter events, 37.9 us)
Async XLA Ops:
  0.7 2.9 copy-start.19
  3.5 1.2 copy-start.64
  3.5 1.6 copy-start.41
  3.5 1.6 copy-start.53
  3.6 1.7 copy-start.60
  107.3 6.4 %copy-start.11 = (bf16[788,512]{1,0:T(8,128)(2,1)S(1)}, bf16[788,512]{1,0:T(8,128)(2,1)}, u32[]{:S(2)}) copy-start(bf16[788,512]{1,0:T(8,128)(2,1)} %param.17) | copy-start | bytes 2420740
  121.2 5.6 %copy-start.17 = (bf16[4,197,8,64]{1,3,2,0:T(8,128)(2,1)}, bf16[4,197,8,64]{1,3,2,0:T(8,128)(2,1)S(1)}, u32[]{:S(2)}) copy-start(bf16[4,197,8,64]{1,3,2,0:T(8,128)(2,1)S(1)} %copy.326) | copy-start | bytes 2420740
  127.9 2.8 copy-start.2
  127.9 2.8 copy-start.28
  132.8 4.8 copy-start.25
  139.3 2.1 copy-start.33
  139.3 2.5 copy-start.51
  139.3 2.5 copy-start.67
  141.9 2.0 copy-start.56
  142.2 12.4 %copy-start.9 = (bf16[788,512]{1,0:T(8,128)(2,1)}, bf16[788,512]{1,0:T(8,128)(2,1)S(1)}, u32[]{:S(2)}) copy-start(bf16[788,512]{1,0:T(8,128)(2,1)S(1)} %add_convert_fusion.2) | copy-start | bytes 2420740
  154.8 43.9 %copy-start.1 = (s32[8]{0:T(128)}, s32[8]{0:T(128)S(1)}, u32[]{:S(2)}) copy-start(s32[8]{0:T(128)S(1)} %reshape.295.counts) | copy-start | bytes 100
  157.8 2.2 copy-start
  217.9 81.2 %copy-start.44 = (bf16[788,4]{0,1:T(4,128)(2,1)}, bf16[788,4]{0,1:T(4,128)(2,1)S(1)}, u32[]{:S(2)}) copy-start(bf16[788,4]{0,1:T(4,128)(2,1)S(1)} %multiply_convert_fusion.5) | copy-start | bytes 18916
  299.1 2.6 copy-start.6
  301.7 2.9 copy-start.13
  303.5 1.2 copy-start.7
  303.5 1.5 copy-start.49
  315.3 11.4 %slice-start = ((s8[6553600]{0:T(1024)(128)(4,1)}), s8[2359296]{0:T(1024)(128)(4,1)S(1)}, s32[]{:S(2)}) async-start(s8[6553600]{0:T(1024)(128)(4,1)} %bitcast.132), calls=%async_computation | async-start | bytes 4718592
  319.0 7.8 %slice-start.1 = ((s8[6553600]{0:T(1024)(128)(4,1)}), s8[4194304]{0:T(1024)(128)(4,1)S(1)}, s32[]{:S(2)}) async-start(s8[6553600]{0:T(1024)(128)(4,1)} %bitcast.132), calls=%async_computation.1 | async-start | bytes 8388608
  326.8 4.5 copy-start.18
  331.3 1.7 copy-start.3
  333.0 1.7 copy-start.16
  339.0 1.2 copy-start.26
  340.3 1.5 copy-start.23
  340.7 1.7 copy-start.12
  340.7 2.6 copy-start.27
  340.7 2.6 copy-start.58
  343.3 3.1 copy-start.48
  343.3 4.7 copy-start.68
  345.2 1.2 copy-start.22
  345.2 3.2 copy-start.10
  345.2 3.2 copy-start.45
  345.3 4.2 copy-start.34
  345.3 4.2 copy-start.36
  347.9 3.1 copy-start.59
  349.5 2.0 copy-start.24
  351.4 4.1 copy-start.55
  351.5 5.7 %copy-start.38 = (bf16[512,512]{1,0:T(8,128)(2,1)S(1)}, bf16[512,512]{1,0:T(8,128)(2,1)}, u32[]{:S(2)}) copy-start(bf16[512,512]{1,0:T(8,128)(2,1)} %convolution_convert_fusion.2) | copy-start | bytes 1572868
  351.5 5.7 %copy-start.39 = (bf16[512,4]{1,0:T(8,128)(2,1)S(1)}, bf16[512,4]{1,0:T(8,128)(2,1)}, u32[]{:S(2)}) copy-start(bf16[512,4]{1,0:T(8,128)(2,1)} %copy.350) | copy-start | bytes 12292
  364.9 126.2 %copy-start.46 = (f32[2,11,64]{2,0,1:T(2,128)S(1)}, f32[2,11,64]{2,0,1:T(2,128)}, u32[]{:S(2)}) copy-start(f32[2,11,64]{2,0,1:T(2,128)} %param.33) | copy-start | bytes 16900
  364.9 126.4 %copy-start.54 = (f32[11,64]{1,0:T(8,128)S(1)}, f32[11,64]{1,0:T(8,128)}, u32[]{:S(2)}) copy-start(f32[11,64]{1,0:T(8,128)} %param.26) | copy-start | bytes 8452
  493.1 6.4 %copy-start.4 = (f32[2,4,256,512]{3,2,1,0:T(8,128)S(1)}, f32[2,4,256,512]{3,2,1,0:T(8,128)}, u32[]{:S(2)}) copy-start(f32[2,4,256,512]{3,2,1,0:T(8,128)} %param.32) | copy-start | bytes 12582916
  499.5 3.7 copy-start.37
  499.5 4.1 copy-start.52
  499.5 4.1 copy-start.65
  503.6 8.2 %copy-start.63 = (f32[4,256]{1,0:T(4,128)}, f32[4,256]{1,0:T(4,128)S(1)}, u32[]{:S(2)}) copy-start(f32[4,256]{1,0:T(4,128)S(1)} %reshape.312) | copy-start | bytes 12292
  504.9 6.9 %copy-start.5 = (f32[2,4,64,2048]{3,2,1,0:T(8,128)S(1)}, f32[2,4,64,2048]{3,2,1,0:T(8,128)}, u32[]{:S(2)}) copy-start(f32[2,4,64,2048]{3,2,1,0:T(8,128)} %param.30) | copy-start | bytes 12582916
  511.8 3.7 copy-start.66
  511.8 4.8 copy-start.32
  511.8 4.8 copy-start.42
  516.5 4.9 copy-start.40
  517.3 4.1 copy-start.29
  519.0 3.7 copy-start.61
  519.0 7.4 %copy-start.62 = (f32[788]{0:T(1024)S(1)}, f32[788]{0:T(1024)}, u32[]{:S(2)}) copy-start(f32[788]{0:T(1024)} %get-tuple-element.194) | copy-start | bytes 9460
  519.0 7.4 %copy-start.8 = (f32[788,512]{1,0:T(8,128)S(1)}, f32[788,512]{1,0:T(8,128)}, u32[]{:S(2)}) copy-start(f32[788,512]{1,0:T(8,128)} %copy-done.7) | copy-start | bytes 4841476
  519.0 7.4 %copy-start.14 = (bf16[788,512]{1,0:T(8,128)(2,1)S(1)}, bf16[788,512]{1,0:T(8,128)(2,1)}, u32[]{:S(2)}) copy-start(bf16[788,512]{1,0:T(8,128)(2,1)} %param.18) | copy-start | bytes 2420740
  519.0 7.4 %copy-start.50 = (f32[788]{0:T(1024)S(1)}, f32[788]{0:T(1024)}, u32[]{:S(2)}) copy-start(f32[788]{0:T(1024)} %copy-done.49) | copy-start | bytes 9460
  526.4 3.1 copy-start.21
  529.5 2.3 copy-start.20
  (8 other events, 6.5 us)

commit v5 on v4

--- a/solution.py
+++ b/solution.py
@@ -502,8 +502,9 @@
     @pl.when(active)
     def _():
         hp = jnp.dot(x_ref[0], w1_ref[0], preferred_element_type=F32) + b1_ref[0]
-        h = (0.5 * hp * (1.0 + lax.erf(hp * SQRT_HALF))).astype(BF16)
-        hp_ref[0] = hp
+        cdf = 0.5 * (1.0 + lax.erf(hp * SQRT_HALF))
+        h = (hp * cdf).astype(BF16)
+        hp_ref[0] = cdf + hp * jnp.exp(-0.5 * hp * hp) * INV_SQRT_2PI
         h_ref[0] = h
         y = jnp.dot(h, w2_ref[0], preferred_element_type=F32) + b2_ref[0]
         hi = y.astype(BF16)
@@ -566,10 +567,8 @@
     @pl.when(active)
     def _():
         dy = dy_ref[0]
-        hp = hp_ref[0]
         d_hidden = lax.dot_general(dy, w2_ref[0], (((1,), (1,)), ((), ())), preferred_element_type=F32)
-        slope = 0.5 * (1.0 + lax.erf(hp * SQRT_HALF)) + hp * jnp.exp(-0.5 * hp * hp) * INV_SQRT_2PI
-        d_pre = (d_hidden * slope).astype(BF16)
+        d_pre = (d_hidden * hp_ref[0]).astype(BF16)
         dt = lax.dot_general(d_pre, w1_ref[0], (((1,), (1,)), ((), ())), preferred_element_type=F32)
         hi = dt.astype(BF16)
         dt_ref[0, :, :D] = hi

time: 543 us -> 538 us (level)
    pallas_call x1, Pallas kernels: 58.3 us -> 52.4 us  [ffn_backward(): pl.pallas_call(functools.partial(ffn_bwd_kernel, micro), grid_spec=grid_s...]
where the time goes in v5:
time: 538 us; the launch traced here: 528 us
  Pallas kernels  319 us (59%)
  local copies, waits for them, and re-layouts  76.7 us (14%)
  matrix products  70.4 us (13%)
  other arithmetic  60.1 us (11%)
    pallas_call x1, Pallas kernels, grad_reduce(): pl.pallas_call(functools.partial(ring_rs2_kernel, groups, x_pair), out_sh...  126 us
    pallas_call x1, Pallas kernels, ring_all_gather(): pl.pallas_call(functools.partial(ring_ag_kernel, groups), out_shape=shape...  101 us
    pallas_call x1, Pallas kernels, ffn_backward(): pl.pallas_call(functools.partial(ffn_bwd_kernel, micro), grid_spec=grid_s...  52.4 us
    pallas_call x1, Pallas kernels, ffn_forward(): pl.pallas_call(functools.partial(ffn_fwd_kernel, micro), grid_spec=grid_s...  39.5 us
    unnamed x158, local copies, waits for them, and re-layouts  20.3 us
    dot_general x2, matrix products, pick_rows(): both = jnp.einsum('mnr,mrd->mnd', onehot, split, preferred_element_type=F32)  15.7 us
    mul x7, other arithmetic, adamw(): first = 0.5 * moments[0] + 0.5 * grad  14.8 us
    select_n x7, other arithmetic, adamw(): jnp.where(which, 0.5 * moments + 0.5 * grad, jnp.sqrt(0.5 * moments * mom...  11.4 us

profile of v5, /device:TPU:1, one launch (start us, length us, event | category | flops | bytes accessed | tf_op | source)
XLA Modules:
  0.0 528.3 jit_solution(3213678013625908897)
XLA Ops:
  0.7 2.9 convert_element_type.104.refs_0_
  3.6 1.1 convert_element_type.105.refs_1_
  6.2 101.1 %shard_map.344 = (bf16[4,512,2048]{2,1,0:T(8,128)(2,1)}, bf16[4,2048,512]{2,1,0:T(8,128)(2,1)}, bf16[512,2560]{1,0:T(8,128)(2,1)}) custom-call(bf16[4,64,2048]{2,1,0:T(8,128)(2,1)} %convert_element_type.104.refs_0_, bf16[4,256,512]{2,1,0:T(8,128)(2,1)} %convert_element_type.105.refs_1_, bf16[64,2560]{1,0:T(8,128)(2,1)} %pad.14.refs_2_), custom_call_target="tpu_custom_call" | custom-call | bytes 19398656 | tf_op jit(solution)/shard_map/pallas_call | solution.py:271
  107.3 4.5 copy.322
  115.0 3.0 add_convert_fusion
  118.0 1.3 fusion.143
  120.1 1.0 copy.326
  121.2 3.5 reshape.319
  124.7 2.0 copy.327
  126.8 1.1 multiply_reduce_fusion.1
  127.9 1.3 fusion.7
  129.2 1.5 copy-done.2
  131.6 1.2 copy.328
  132.8 4.8 fusion.65
  139.4 2.1 fusion.147
  142.2 1.4 fusion.148
  144.1 2.3 reduce-window.6
  147.4 7.3 %fusion.15.x_ref = bf16[2,2048,512]{2,1,0:T(8,128)(2,1)} fusion(s32[2,788]{1,0:T(2,128)S(1)} %multiply_add_fusion.6, bf16[2,394,512]{2,1,0:T(8,128)(2,1)S(1)} %reshape.296), kind=kOutput, calls=%fused_computation.27 | convolution fusion | flops 3313664000 | bytes 5007520 | tf_op jit(solution)/shard_map/mnr,mnd->mrd/dot_general | solution.py:803
  157.8 2.2 copy-done
  160.0 39.5 %shard_map.345 = (f32[2,2048,2048]{2,1,0:T(8,128)}, bf16[2,2048,2048]{2,1,0:T(8,128)(2,1)}, bf16[2,2048,1024]{2,1,0:T(8,128)(2,1)}) custom-call(s32[8]{0:T(128)S(1)} %reshape.295.counts, bf16[2,2048,512]{2,1,0:T(8,128)(2,1)S(1)} %copy-done, bf16[4,512,2048]{2,1,0:T(8,128)(2,1)} %get-tuple-element.38.w1_ref, f32[4,1,2048]{2,1,0:T(1,128)S(1)} %reshape.316.b1_ref, ...), custom_call_target="tpu_custom_call" | custom-call | flops 8589934592 | bytes 31457280 | tf_op jit(solution)/shard_map/pallas_call | solution.py:541
  199.5 9.7 %fusion.2 = f32[2,788,1024]{2,1,0:T(8,128)S(1)} fusion(bf16[2,2048,1024]{2,1,0:T(8,128)(2,1)} %get-tuple-element.40, s32[2,788]{1,0:T(2,128)S(1)} %multiply_add_fusion.6), kind=kOutput, calls=%fused_computation.3 | convolution fusion | flops 6613450752 | bytes 14850208 | tf_op jit(solution)/shard_map/mnr,mrd->mnd/dot_general | solution.py:666
  210.0 2.1 fusion.142
  212.1 1.6 reshape.297
  213.7 2.7 reshape.298
  216.5 2.1 multiply_reduce_fusion.5
  218.9 2.5 reshape.300
  221.3 1.7 multiply_convert_fusion.4
  223.0 7.3 %fusion.16.dy_ref = bf16[2,2048,512]{2,1,0:T(8,128)(2,1)} fusion(s32[2,788]{1,0:T(2,128)S(1)} %multiply_add_fusion.6, bf16[2,394,512]{2,1,0:T(8,128)(2,1)S(1)} %get-tuple-element.226, bf16[2,394,512]{2,1,0:T(8,128)(2,1)S(1)} %get-tuple-element.225), kind=kOutput, calls=%fused_computation.28 | convolution fusion | flops 3313664000 | bytes 5814432 | tf_op jit(solution)/shard_map/mnr,mnd->mrd/dot_general | solution.py:817
  230.3 52.4 %shard_map.346 = (bf16[2,2048,1024]{2,1,0:T(8,128)(2,1)}, bf16[4,512,2048]{2,1,0:T(8,128)(2,1)}, bf16[4,2048,512]{2,1,0:T(8,128)(2,1)}, f32[4,1,2048]{2,1,0:T(1,128)}, f32[4,1,512]{2,1,0:T(1,128)}) custom-call(s32[8]{0:T(128)} %copy-done.1, bf16[2,2048,512]{2,1,0:T(8,128)(2,1)} %fusion.16.dy_ref, bf16[2,2048,512]{2,1,0:T(8,128)(2,1)} %fusion.15.x_ref, ...), custom_call_target="tpu_custom_call" | custom-call | flops 17179869184 | bytes 100663296 | tf_op jit(solution)/shard_map/pallas_call | solution.py:617
  282.7 1.1 fusion.1
  283.8 5.9 %fusion.19 = f32[2,394,1024]{2,1,0:T(8,128)S(1)} fusion(bf16[2,2048,1024]{2,1,0:T(8,128)(2,1)} %get-tuple-element.43, bf16[2,788,2048]{2,1,0:T(8,128)(2,1)S(1)} %fusion.1), kind=kOutput, calls=%fused_computation.31 | convolution fusion | flops 3306725376 | bytes 18169856 | tf_op jit(solution)/shard_map/mnr,mrd->mnd/dot_general | solution.py:666
  289.7 1.5 slice_add_fusion.3
  291.3 2.7 reshape.301
  294.0 2.6 multiply_reduce_fusion.2
  296.7 1.7 fusion.141
  298.4 1.2 copy-done.7
  300.7 1.7 convolution_convert_fusion.1
  303.2 1.0 copy.336
  304.3 4.2 fusion.62
  308.5 1.8 copy.346
  310.2 3.6 reshape.305
  313.9 7.8 %multiply_reduce_fusion = (f32[4,8,197]{2,1,0:T(8,128)S(1)}, f32[4,8,197,197]{2,3,1,0:T(8,128)}) fusion(f32[4,8,197,197]{2,3,1,0:T(8,128)} %copy-done.2, f32[4,8,197]{2,1,0:T(8,128)S(1)} %log_add_fusion, bf16[4,197,8,64]{1,3,2,0:T(8,128)(2,1)S(1)} %copy.336, bf16[4,197,8,64]{1,3,2,0:T(8,128)(2,1)} %copy-done.25), kind=kOutput, calls=%fused_computation.6 | convolution fusion | flops 163922912 | bytes 11599360 | tf_op jit(solution)/shard_map/bqhd,bkhd->bhqk/dot_general | solution.py:727
  321.7 4.5 multiply_convert_fusion
  326.2 1.2 fusion.67
  329.6 2.7 fusion.66
  338.2 2.0 fusion.138
  340.2 1.1 copy-done.22
  341.3 1.5 fusion.46
  344.4 1.5 convolution_convert_fusion.2
  346.4 4.1 convolution_convert_fusion
  350.6 1.1 reshape_squeeze.4
  352.1 4.4 concatenate.46
  356.5 3.3 pad.16.refs_2_
  359.8 126.2 %shard_map.347 = (f32[4,64,2048]{2,1,0:T(8,128)}, f32[4,256,512]{2,1,0:T(8,128)}, f32[64,2560]{1,0:T(8,128)}) custom-call(bf16[4,512,2048]{2,1,0:T(8,128)(2,1)} %get-tuple-element.44.refs_0_, bf16[4,2048,512]{2,1,0:T(8,128)(2,1)} %get-tuple-element.45.refs_1_, bf16[512,2560]{1,0:T(8,128)(2,1)} %pad.16.refs_2_), custom_call_target="tpu_custom_call" | custom-call | flops 9699328 | bytes 19398656 | tf_op jit(solution)/shard_map/pallas_call | solution.py:478
  488.0 6.4 %broadcast_multiply_fusion = (f32[4,256,512]{2,1,0:T(8,128)S(1)}, f32[4,256,512]{2,1,0:T(8,128)}, f32[4,256,512]{2,1,0:T(8,128)S(1)}) fusion(f32[4,256,512]{2,1,0:T(8,128)} %get-tuple-element.297, f32[4,256,512]{2,1,0:T(8,128)} %param.25, f32[2,4,256,512]{3,2,1,0:T(8,128)} %param.32), kind=kLoop, calls=%fused_computation.109 | loop fusion | flops 6815744 | bytes 14680064 | tf_op jit(solution)/shard_map/mul | solution.py:745
  494.4 3.7 fusion.12
  499.8 6.9 %broadcast_multiply_fusion.1 = (f32[4,64,2048]{2,1,0:T(8,128)S(1)}, f32[4,64,2048]{2,1,0:T(8,128)}, f32[4,64,2048]{2,1,0:T(8,128)S(1)}) fusion(f32[4,64,2048]{2,1,0:T(8,128)} %get-tuple-element.295, f32[4,64,2048]{2,1,0:T(8,128)} %param.23, f32[2,4,64,2048]{3,2,1,0:T(8,128)} %param.30), kind=kLoop, calls=%fused_computation.110 | loop fusion | flops 6815744 | bytes 14680064 | tf_op jit(solution)/shard_map/mul | solution.py:745
  506.7 3.7 fusion.9
  513.9 2.4 fusion.86
  516.3 1.2 fusion.71
  521.3 3.1 add_add_fusion.2
  524.4 1.3 copy.398
  525.7 1.0 copy-done.20
  526.7 1.3 copy.399
  (271 shorter events, 37.9 us)
Async XLA Ops:
  0.7 2.9 copy-start.19
  3.5 1.2 copy-start.64
  3.5 1.6 copy-start.41
  3.5 1.6 copy-start.53
  3.6 1.7 copy-start.60
  107.3 6.4 %copy-start.11 = (bf16[788,512]{1,0:T(8,128)(2,1)S(1)}, bf16[788,512]{1,0:T(8,128)(2,1)}, u32[]{:S(2)}) copy-start(bf16[788,512]{1,0:T(8,128)(2,1)} %param.17) | copy-start | bytes 2420740
  121.2 5.6 %copy-start.17 = (bf16[4,197,8,64]{1,3,2,0:T(8,128)(2,1)}, bf16[4,197,8,64]{1,3,2,0:T(8,128)(2,1)S(1)}, u32[]{:S(2)}) copy-start(bf16[4,197,8,64]{1,3,2,0:T(8,128)(2,1)S(1)} %copy.326) | copy-start | bytes 2420740
  127.9 2.8 copy-start.2
  127.9 2.8 copy-start.28
  132.8 4.8 copy-start.25
  139.3 2.1 copy-start.33
  139.3 2.5 copy-start.51
  139.3 2.5 copy-start.67
  141.9 2.0 copy-start.56
  142.2 12.4 %copy-start.9 = (bf16[788,512]{1,0:T(8,128)(2,1)}, bf16[788,512]{1,0:T(8,128)(2,1)S(1)}, u32[]{:S(2)}) copy-start(bf16[788,512]{1,0:T(8,128)(2,1)S(1)} %add_convert_fusion.2) | copy-start | bytes 2420740
  154.8 44.7 %copy-start.1 = (s32[8]{0:T(128)}, s32[8]{0:T(128)S(1)}, u32[]{:S(2)}) copy-start(s32[8]{0:T(128)S(1)} %reshape.295.counts) | copy-start | bytes 100
  157.8 2.2 copy-start
  218.7 75.3 %copy-start.44 = (bf16[788,4]{0,1:T(4,128)(2,1)}, bf16[788,4]{0,1:T(4,128)(2,1)S(1)}, u32[]{:S(2)}) copy-start(bf16[788,4]{0,1:T(4,128)(2,1)S(1)} %multiply_convert_fusion.5) | copy-start | bytes 18916
  294.0 2.6 copy-start.6
  296.6 2.9 copy-start.13
  298.4 1.2 copy-start.7
  298.4 1.5 copy-start.49
  310.2 11.4 %slice-start = ((s8[6553600]{0:T(1024)(128)(4,1)}), s8[2359296]{0:T(1024)(128)(4,1)S(1)}, s32[]{:S(2)}) async-start(s8[6553600]{0:T(1024)(128)(4,1)} %bitcast.132), calls=%async_computation | async-start | bytes 4718592
  313.9 7.8 %slice-start.1 = ((s8[6553600]{0:T(1024)(128)(4,1)}), s8[4194304]{0:T(1024)(128)(4,1)S(1)}, s32[]{:S(2)}) async-start(s8[6553600]{0:T(1024)(128)(4,1)} %bitcast.132), calls=%async_computation.1 | async-start | bytes 8388608
  321.7 4.5 copy-start.18
  326.2 1.7 copy-start.3
  327.9 1.7 copy-start.16
  333.9 1.2 copy-start.26
  335.2 1.5 copy-start.23
  335.6 1.7 copy-start.12
  335.6 2.6 copy-start.27
  335.6 2.6 copy-start.58
  338.2 3.1 copy-start.48
  338.2 4.7 copy-start.68
  340.1 1.2 copy-start.22
  340.1 3.2 copy-start.10
  340.2 3.2 copy-start.45
  340.2 4.2 copy-start.34
  340.2 4.2 copy-start.36
  342.8 3.1 copy-start.59
  344.4 2.0 copy-start.24
  346.4 4.1 copy-start.55
  346.4 5.7 %copy-start.38 = (bf16[512,512]{1,0:T(8,128)(2,1)S(1)}, bf16[512,512]{1,0:T(8,128)(2,1)}, u32[]{:S(2)}) copy-start(bf16[512,512]{1,0:T(8,128)(2,1)} %convolution_convert_fusion.2) | copy-start | bytes 1572868
  346.4 5.7 %copy-start.39 = (bf16[512,4]{1,0:T(8,128)(2,1)S(1)}, bf16[512,4]{1,0:T(8,128)(2,1)}, u32[]{:S(2)}) copy-start(bf16[512,4]{1,0:T(8,128)(2,1)} %copy.350) | copy-start | bytes 12292
  359.8 126.2 %copy-start.46 = (f32[2,11,64]{2,0,1:T(2,128)S(1)}, f32[2,11,64]{2,0,1:T(2,128)}, u32[]{:S(2)}) copy-start(f32[2,11,64]{2,0,1:T(2,128)} %param.33) | copy-start | bytes 16900
  359.8 126.4 %copy-start.54 = (f32[11,64]{1,0:T(8,128)S(1)}, f32[11,64]{1,0:T(8,128)}, u32[]{:S(2)}) copy-start(f32[11,64]{1,0:T(8,128)} %param.26) | copy-start | bytes 8452
  488.0 6.4 %copy-start.4 = (f32[2,4,256,512]{3,2,1,0:T(8,128)S(1)}, f32[2,4,256,512]{3,2,1,0:T(8,128)}, u32[]{:S(2)}) copy-start(f32[2,4,256,512]{3,2,1,0:T(8,128)} %param.32) | copy-start | bytes 12582916
  494.4 3.7 copy-start.37
  494.4 4.1 copy-start.52
  494.4 4.1 copy-start.65
  498.5 8.2 %copy-start.63 = (f32[4,256]{1,0:T(4,128)}, f32[4,256]{1,0:T(4,128)S(1)}, u32[]{:S(2)}) copy-start(f32[4,256]{1,0:T(4,128)S(1)} %reshape.312) | copy-start | bytes 12292
  499.8 6.9 %copy-start.5 = (f32[2,4,64,2048]{3,2,1,0:T(8,128)S(1)}, f32[2,4,64,2048]{3,2,1,0:T(8,128)}, u32[]{:S(2)}) copy-start(f32[2,4,64,2048]{3,2,1,0:T(8,128)} %param.30) | copy-start | bytes 12582916
  506.7 3.7 copy-start.66
  506.7 4.8 copy-start.32
  506.7 4.8 copy-start.42
  511.4 4.9 copy-start.40
  512.2 4.1 copy-start.29
  513.9 3.7 copy-start.61
  513.9 7.4 %copy-start.62 = (f32[788]{0:T(1024)S(1)}, f32[788]{0:T(1024)}, u32[]{:S(2)}) copy-start(f32[788]{0:T(1024)} %get-tuple-element.194) | copy-start | bytes 9460
  513.9 7.4 %copy-start.8 = (f32[788,512]{1,0:T(8,128)S(1)}, f32[788,512]{1,0:T(8,128)}, u32[]{:S(2)}) copy-start(f32[788,512]{1,0:T(8,128)} %copy-done.7) | copy-start | bytes 4841476
  513.9 7.4 %copy-start.14 = (bf16[788,512]{1,0:T(8,128)(2,1)S(1)}, bf16[788,512]{1,0:T(8,128)(2,1)}, u32[]{:S(2)}) copy-start(bf16[788,512]{1,0:T(8,128)(2,1)} %param.18) | copy-start | bytes 2420740
  513.9 7.4 %copy-start.50 = (f32[788]{0:T(1024)S(1)}, f32[788]{0:T(1024)}, u32[]{:S(2)}) copy-start(f32[788]{0:T(1024)} %copy-done.49) | copy-start | bytes 9460
  521.3 3.1 copy-start.21
  524.4 2.3 copy-start.20
  (8 other events, 6.5 us)

commit v6 on v5

--- a/solution.py
+++ b/solution.py
@@ -630,6 +630,30 @@
         ),
     )(counts, d_expert, table_in, hp, h, w1, w2)
 
+def adamw_kernel(rate, w_ref, m_ref, g_ref, wo_ref, mo_ref):
+    g = g_ref[...]
+    first = 0.5 * m_ref[0] + 0.5 * g
+    root = jnp.sqrt(0.5 * m_ref[1] * m_ref[1] + 0.5 * g * g)
+    w = w_ref[...]
+    wo_ref[...] = w - rate * (first / (root + 1e-08) + 0.1 * w)
+    mo_ref[0] = first
+    mo_ref[1] = root
+
+
+def adamw_pass(weight, moments, grad, rate):
+    n, r, c = weight.shape
+    spec = pl.BlockSpec((1, r, c), lambda i: (i, 0, 0))
+    mspec = pl.BlockSpec((2, 1, r, c), lambda i: (0, i, 0, 0))
+    return pl.pallas_call(
+        functools.partial(adamw_kernel, rate),
+        grid=(n,),
+        in_specs=[spec, mspec, spec],
+        out_specs=[spec, mspec],
+        out_shape=[jax.ShapeDtypeStruct(weight.shape, F32), jax.ShapeDtypeStruct(moments.shape, F32)],
+        cost_estimate=pl.CostEstimate(flops=12 * weight.size, bytes_accessed=28 * weight.size, transcendentals=2 * weight.size),
+    )(weight, moments, grad)
+
+
 def layer_norm(value, gain, shift):
     center = value - jnp.mean(value, -1, keepdims=True)
     spread = jnp.mean(center * center, -1, keepdims=True)
@@ -866,7 +890,10 @@
     news = []
     states = []
     for weight, state, grad, rate in zip(params, moments, reduced, rates):
-        new_weight, new_state = adamw(weight, state, grad, rate)
+        if weight.ndim == 3:
+            new_weight, new_state = adamw_pass(weight, state, grad, rate)
+        else:
+            new_weight, new_state = adamw(weight, state, grad, rate)
         news.append(new_weight)
         states.append(new_state)
     return (result.astype(BF16), input_grad) + reduced + tuple(news) + tuple(states)

time: 538 us -> 535 us (level)
  other arithmetic: 60.1 us -> 42 us
  Pallas kernels: 319 us -> 333 us
    pallas_call x0 -> x2, Pallas kernels: none -> 13.9 us  [adamw_pass(): pl.pallas_call(functools.partial(adamw_kernel, rate), grid=(n,), in_specs...]
    mul x7 -> x5, other arithmetic: 14.8 us -> 3.87 us  [adamw(): first = 0.5 * moments[0] + 0.5 * grad]
    select_n x7 -> x5, other arithmetic: 11.4 us -> 4.74 us  [adamw(): jnp.where(which, 0.5 * moments + 0.5 * grad, jnp.sqrt(0.5 * moments * mom...]
    unnamed x158 -> x164, local copies, waits for them, and re-layouts: 20.3 us -> 19.5 us
where the time goes in v6:
time: 535 us; the launch traced here: 525 us
  Pallas kernels  333 us (62%)
  local copies, waits for them, and re-layouts  77.4 us (14%)
  matrix products  70.4 us (13%)
  other arithmetic  42 us (8%)
    pallas_call x1, Pallas kernels, grad_reduce(): pl.pallas_call(functools.partial(ring_rs2_kernel, groups, x_pair), out_sh...  126 us
    pallas_call x1, Pallas kernels, ring_all_gather(): pl.pallas_call(functools.partial(ring_ag_kernel, groups), out_shape=shape...  101 us
    pallas_call x1, Pallas kernels, ffn_backward(): pl.pallas_call(functools.partial(ffn_bwd_kernel, micro), grid_spec=grid_s...  52.4 us
    pallas_call x1, Pallas kernels, ffn_forward(): pl.pallas_call(functools.partial(ffn_fwd_kernel, micro), grid_spec=grid_s...  39.5 us
    unnamed x164, local copies, waits for them, and re-layouts  19.5 us
    dot_general x2, matrix products, pick_rows(): both = jnp.einsum('mnr,mrd->mnd', onehot, split, preferred_element_type=F32)  15.7 us
    pallas_call x2, Pallas kernels, adamw_pass(): pl.pallas_call(functools.partial(adamw_kernel, rate), grid=(n,), in_specs...  13.9 us
    reshape x8, local copies, waits for them, and re-layouts, split_heads(): return part.reshape(-1, S, HEADS, HEAD_DIM)  11.3 us

profile of v6, /device:TPU:1, one launch (start us, length us, event | category | flops | bytes accessed | tf_op | source)
XLA Modules:
  0.0 525.0 jit_solution(13712389519784861484)
XLA Ops:
  0.7 2.9 convert_element_type.104.refs_0_
  3.6 1.1 convert_element_type.105.refs_1_
  6.2 101.1 %shard_map.344 = (bf16[4,512,2048]{2,1,0:T(8,128)(2,1)}, bf16[4,2048,512]{2,1,0:T(8,128)(2,1)}, bf16[512,2560]{1,0:T(8,128)(2,1)}) custom-call(bf16[4,64,2048]{2,1,0:T(8,128)(2,1)} %convert_element_type.104.refs_0_, bf16[4,256,512]{2,1,0:T(8,128)(2,1)} %convert_element_type.105.refs_1_, bf16[64,2560]{1,0:T(8,128)(2,1)} %pad.14.refs_2_), custom_call_target="tpu_custom_call" | custom-call | bytes 19398656 | tf_op jit(solution)/shard_map/pallas_call | solution.py:271
  107.3 4.5 copy.322
  115.0 3.0 add_convert_fusion
  118.0 1.3 fusion.121
  120.1 1.0 copy.326
  121.2 3.5 reshape.311
  124.7 2.0 copy.327
  126.8 1.1 multiply_reduce_fusion.1
  127.9 1.3 fusion.7
  129.2 1.5 copy-done.2
  131.5 1.2 copy.328
  132.8 4.8 fusion.45
  139.3 2.1 fusion.125
  142.2 1.4 fusion.126
  144.1 2.3 reduce-window.6
  147.3 7.3 %fusion.9.x_ref = bf16[2,2048,512]{2,1,0:T(8,128)(2,1)} fusion(s32[2,788]{1,0:T(2,128)S(1)} %multiply_add_fusion.4, bf16[2,394,512]{2,1,0:T(8,128)(2,1)S(1)} %reshape.288), kind=kOutput, calls=%fused_computation.17 | convolution fusion | flops 3313664000 | bytes 5007520 | tf_op jit(solution)/shard_map/mnr,mnd->mrd/dot_general | solution.py:827
  157.8 2.2 copy-done
  160.0 39.5 %shard_map.345 = (f32[2,2048,2048]{2,1,0:T(8,128)}, bf16[2,2048,2048]{2,1,0:T(8,128)(2,1)}, bf16[2,2048,1024]{2,1,0:T(8,128)(2,1)}) custom-call(s32[8]{0:T(128)S(1)} %reshape.287.counts, bf16[2,2048,512]{2,1,0:T(8,128)(2,1)S(1)} %copy-done, bf16[4,512,2048]{2,1,0:T(8,128)(2,1)} %get-tuple-element.42.w1_ref, f32[4,1,2048]{2,1,0:T(1,128)S(1)} %reshape.308.b1_ref, ...), custom_call_target="tpu_custom_call" | custom-call | flops 8589934592 | bytes 31457280 | tf_op jit(solution)/shard_map/pallas_call | solution.py:541
  199.5 9.7 %fusion.2 = f32[2,788,1024]{2,1,0:T(8,128)S(1)} fusion(bf16[2,2048,1024]{2,1,0:T(8,128)(2,1)} %get-tuple-element.44, s32[2,788]{1,0:T(2,128)S(1)} %multiply_add_fusion.4), kind=kOutput, calls=%fused_computation.3 | convolution fusion | flops 6613450752 | bytes 14850208 | tf_op jit(solution)/shard_map/mnr,mrd->mnd/dot_general | solution.py:690
  210.0 2.1 fusion.120
  212.1 1.6 reshape.289
  213.7 2.7 reshape.290
  216.5 2.1 multiply_reduce_fusion.5
  218.9 2.5 reshape.292
  221.3 1.7 multiply_convert_fusion.4
  223.0 7.3 %fusion.10.dy_ref = bf16[2,2048,512]{2,1,0:T(8,128)(2,1)} fusion(s32[2,788]{1,0:T(2,128)S(1)} %multiply_add_fusion.4, bf16[2,394,512]{2,1,0:T(8,128)(2,1)S(1)} %get-tuple-element.228, bf16[2,394,512]{2,1,0:T(8,128)(2,1)S(1)} %get-tuple-element.227), kind=kOutput, calls=%fused_computation.18 | convolution fusion | flops 3313664000 | bytes 5814432 | tf_op jit(solution)/shard_map/mnr,mnd->mrd/dot_general | solution.py:841
  230.3 52.4 %shard_map.346 = (bf16[2,2048,1024]{2,1,0:T(8,128)(2,1)}, bf16[4,512,2048]{2,1,0:T(8,128)(2,1)}, bf16[4,2048,512]{2,1,0:T(8,128)(2,1)}, f32[4,1,2048]{2,1,0:T(1,128)}, f32[4,1,512]{2,1,0:T(1,128)}) custom-call(s32[8]{0:T(128)} %copy-done.1, bf16[2,2048,512]{2,1,0:T(8,128)(2,1)} %fusion.10.dy_ref, bf16[2,2048,512]{2,1,0:T(8,128)(2,1)} %fusion.9.x_ref, ...), custom_call_target="tpu_custom_call" | custom-call | flops 17179869184 | bytes 100663296 | tf_op jit(solution)/shard_map/pallas_call | solution.py:617
  282.7 1.1 fusion.1
  283.8 5.9 %fusion.13 = f32[2,394,1024]{2,1,0:T(8,128)S(1)} fusion(bf16[2,2048,1024]{2,1,0:T(8,128)(2,1)} %get-tuple-element.47, bf16[2,788,2048]{2,1,0:T(8,128)(2,1)S(1)} %fusion.1), kind=kOutput, calls=%fused_computation.21 | convolution fusion | flops 3306725376 | bytes 18169856 | tf_op jit(solution)/shard_map/mnr,mrd->mnd/dot_general | solution.py:690
  289.7 1.5 slice_add_fusion.3
  291.3 2.7 reshape.293
  294.0 2.6 multiply_reduce_fusion.2
  296.7 1.7 fusion.119
  298.4 1.2 copy-done.5
  300.7 1.7 convolution_convert_fusion.1
  303.2 1.0 copy.336
  304.3 4.2 fusion.42
  308.5 1.8 copy.346
  310.2 3.6 reshape.297
  313.9 7.8 %multiply_reduce_fusion = (f32[4,8,197]{2,1,0:T(8,128)S(1)}, f32[4,8,197,197]{2,3,1,0:T(8,128)}) fusion(f32[4,8,197,197]{2,3,1,0:T(8,128)} %copy-done.2, f32[4,8,197]{2,1,0:T(8,128)S(1)} %log_add_fusion, bf16[4,197,8,64]{1,3,2,0:T(8,128)(2,1)S(1)} %copy.336, bf16[4,197,8,64]{1,3,2,0:T(8,128)(2,1)} %copy-done.23), kind=kOutput, calls=%fused_computation.6 | convolution fusion | flops 163922912 | bytes 11599360 | tf_op jit(solution)/shard_map/bqhd,bkhd->bhqk/dot_general | solution.py:751
  321.7 4.5 multiply_convert_fusion
  326.2 1.2 fusion.47
  329.5 2.7 fusion.46
  338.2 2.0 fusion.116
  340.2 1.1 copy-done.20
  341.3 1.5 fusion.26
  344.4 1.5 convolution_convert_fusion.2
  346.3 4.1 convolution_convert_fusion
  350.6 1.1 reshape_squeeze.4
  352.1 4.4 concatenate.46
  356.5 3.3 pad.16.refs_2_
  359.8 126.2 %shard_map.347 = (f32[4,64,2048]{2,1,0:T(8,128)}, f32[4,256,512]{2,1,0:T(8,128)}, f32[64,2560]{1,0:T(8,128)}) custom-call(bf16[4,512,2048]{2,1,0:T(8,128)(2,1)} %get-tuple-element.48.refs_0_, bf16[4,2048,512]{2,1,0:T(8,128)(2,1)} %get-tuple-element.49.refs_1_, bf16[512,2560]{1,0:T(8,128)(2,1)} %pad.16.refs_2_), custom_call_target="tpu_custom_call" | custom-call | flops 9699328 | bytes 19398656 | tf_op jit(solution)/shard_map/pallas_call | solution.py:478
  491.5 1.4 broadcast_multiply_fusion.3
  493.0 1.4 fusion.99
  495.4 1.7 fusion.75
  498.0 1.0 fusion.64
  499.1 1.2 fusion.49
  500.3 6.9 %shard_map.348 = (f32[4,64,2048]{2,1,0:T(8,128)}, f32[2,4,64,2048]{3,2,1,0:T(8,128)}) custom-call(f32[4,64,2048]{2,1,0:T(8,128)} %w_ref.2, f32[2,4,64,2048]{3,2,1,0:T(8,128)} %m_ref.2, f32[4,64,2048]{2,1,0:T(8,128)} %get-tuple-element.297.g_ref), custom_call_target="tpu_custom_call" | custom-call | flops 6291456 | bytes 14680064 | tf_op jit(solution)/shard_map/pallas_call | solution.py:647
  507.2 7.0 %shard_map.349 = (f32[4,256,512]{2,1,0:T(8,128)}, f32[2,4,256,512]{3,2,1,0:T(8,128)}) custom-call(f32[4,256,512]{2,1,0:T(8,128)} %w_ref.3, f32[2,4,256,512]{3,2,1,0:T(8,128)} %m_ref.3, f32[4,256,512]{2,1,0:T(8,128)} %get-tuple-element.299.g_ref), custom_call_target="tpu_custom_call" | custom-call | flops 6291456 | bytes 14680064 | tf_op jit(solution)/shard_map/pallas_call | solution.py:647
  518.0 3.1 add_add_fusion.2
  521.1 1.3 copy.398
  523.5 1.3 copy.399
  (275 shorter events, 39.1 us)
Async XLA Ops:
  0.7 2.9 copy-start.17
  3.5 1.2 copy-start.66
  3.5 1.6 copy-start.40
  3.5 1.6 copy-start.55
  3.6 1.7 copy-start.62
  107.3 6.4 %copy-start.9 = (bf16[788,512]{1,0:T(8,128)(2,1)S(1)}, bf16[788,512]{1,0:T(8,128)(2,1)}, u32[]{:S(2)}) copy-start(bf16[788,512]{1,0:T(8,128)(2,1)} %param.17) | copy-start | bytes 2420740
  121.2 5.6 %copy-start.15 = (bf16[4,197,8,64]{1,3,2,0:T(8,128)(2,1)}, bf16[4,197,8,64]{1,3,2,0:T(8,128)(2,1)S(1)}, u32[]{:S(2)}) copy-start(bf16[4,197,8,64]{1,3,2,0:T(8,128)(2,1)S(1)} %copy.326) | copy-start | bytes 2420740
  127.9 2.8 copy-start.2
  127.9 2.8 copy-start.26
  132.8 4.8 copy-start.23
  139.3 2.1 copy-start.32
  139.3 2.5 copy-start.53
  139.3 2.5 copy-start.70
  141.9 2.0 copy-start.58
  142.2 12.4 %copy-start.7 = (bf16[788,512]{1,0:T(8,128)(2,1)}, bf16[788,512]{1,0:T(8,128)(2,1)S(1)}, u32[]{:S(2)}) copy-start(bf16[788,512]{1,0:T(8,128)(2,1)S(1)} %add_convert_fusion.2) | copy-start | bytes 2420740
  154.8 44.7 %copy-start.1 = (s32[8]{0:T(128)}, s32[8]{0:T(128)S(1)}, u32[]{:S(2)}) copy-start(s32[8]{0:T(128)S(1)} %reshape.287.counts) | copy-start | bytes 100
  157.8 2.2 copy-start
  218.8 75.3 %copy-start.43 = (bf16[788,4]{0,1:T(4,128)(2,1)}, bf16[788,4]{0,1:T(4,128)(2,1)S(1)}, u32[]{:S(2)}) copy-start(bf16[788,4]{0,1:T(4,128)(2,1)S(1)} %multiply_convert_fusion.5) | copy-start | bytes 18916
  294.0 2.6 copy-start.4
  296.6 2.9 copy-start.11
  298.4 1.5 copy-start.51
  310.2 11.4 %slice-start = ((s8[6553600]{0:T(1024)(128)(4,1)}), s8[2359296]{0:T(1024)(128)(4,1)S(1)}, s32[]{:S(2)}) async-start(s8[6553600]{0:T(1024)(128)(4,1)} %bitcast.120), calls=%async_computation | async-start | bytes 4718592
  313.9 7.8 %slice-start.1 = ((s8[6553600]{0:T(1024)(128)(4,1)}), s8[4194304]{0:T(1024)(128)(4,1)S(1)}, s32[]{:S(2)}) async-start(s8[6553600]{0:T(1024)(128)(4,1)} %bitcast.120), calls=%async_computation.1 | async-start | bytes 8388608
  321.7 4.5 copy-start.16
  326.2 1.7 copy-start.3
  327.9 1.7 copy-start.14
  333.9 1.2 copy-start.24
  335.2 1.5 copy-start.21
  335.6 1.7 copy-start.10
  335.6 2.6 copy-start.25
  335.6 2.6 copy-start.60
  338.2 3.1 copy-start.49
  338.2 4.6 copy-start.71
  340.1 3.2 copy-start.8
  340.1 3.2 copy-start.44
  340.2 4.2 copy-start.33
  340.2 4.2 copy-start.35
  340.2 5.7 %copy-start.46 = (f32[788]{0:T(1024)}, f32[788]{0:T(1024)S(1)}, u32[]{:S(2)}) copy-start(f32[788]{0:T(1024)S(1)} %multiply_multiply_fusion.10) | copy-start | bytes 9460
  342.7 3.1 copy-start.61
  344.4 2.0 copy-start.22
  346.3 4.1 copy-start.57
  346.3 5.7 %copy-start.37 = (bf16[512,512]{1,0:T(8,128)(2,1)S(1)}, bf16[512,512]{1,0:T(8,128)(2,1)}, u32[]{:S(2)}) copy-start(bf16[512,512]{1,0:T(8,128)(2,1)} %convolution_convert_fusion.2) | copy-start | bytes 1572868
  346.3 5.7 %copy-start.38 = (bf16[512,4]{1,0:T(8,128)(2,1)S(1)}, bf16[512,4]{1,0:T(8,128)(2,1)}, u32[]{:S(2)}) copy-start(bf16[512,4]{1,0:T(8,128)(2,1)} %copy.350) | copy-start | bytes 12292
  359.8 126.3 %copy-start.45 = (f32[2,11,64]{2,0,1:T(2,128)S(1)}, f32[2,11,64]{2,0,1:T(2,128)}, u32[]{:S(2)}) copy-start(f32[2,11,64]{2,0,1:T(2,128)} %param.33) | copy-start | bytes 16900
  359.8 126.5 %copy-start.56 = (f32[11,64]{1,0:T(8,128)S(1)}, f32[11,64]{1,0:T(8,128)}, u32[]{:S(2)}) copy-start(f32[11,64]{1,0:T(8,128)} %param.26) | copy-start | bytes 8452
  359.8 129.5 %copy-start.54 = (f32[2,4,256]{2,1,0:T(4,128)S(1)}, f32[2,4,256]{2,1,0:T(4,128)}, u32[]{:S(2)}) copy-start(f32[2,4,256]{2,1,0:T(4,128)} %param.31) | copy-start | bytes 24580
  359.8 129.5 %copy-start.67 = (f32[4,256]{1,0:T(4,128)S(1)}, f32[4,256]{1,0:T(4,128)}, u32[]{:S(2)}) copy-start(f32[4,256]{1,0:T(4,128)} %param.24) | copy-start | bytes 12292
  359.8 135.5 %copy-start.31 = (f32[2,64,512]{2,1,0:T(8,128)S(1)}, f32[2,64,512]{2,1,0:T(8,128)}, u32[]{:S(2)}) copy-start(f32[2,64,512]{2,1,0:T(8,128)} %param.28) | copy-start | bytes 786436
  486.1 11.8 %copy-start.36 = (f32[64,2560]{1,0:T(8,128)S(1)}, f32[64,2560]{1,0:T(8,128)}, u32[]{:S(2)}) copy-start(f32[64,2560]{1,0:T(8,128)} %get-tuple-element.52) | copy-start | bytes 1966084
  487.3 10.7 %copy-start.27 = (f32[2,64,1536]{2,1,0:T(8,128)S(1)}, f32[2,64,1536]{2,1,0:T(8,128)}, u32[]{:S(2)}) copy-start(f32[2,64,1536]{2,1,0:T(8,128)} %param.27) | copy-start | bytes 2359300
  487.3 10.7 %copy-start.29 = (f32[64,1536]{1,0:T(8,128)S(1)}, f32[64,1536]{1,0:T(8,128)}, u32[]{:S(2)}) copy-start(f32[64,1536]{1,0:T(8,128)} %param.20) | copy-start | bytes 1179652
  487.4 10.5 %copy-start.68 = (pred[2]{0:T(512)(128)(4,1)}, pred[2]{0:T(512)(128)(4,1)S(1)}, u32[]{:S(2)}) copy-start(pred[2]{0:T(512)(128)(4,1)S(1)} %iota_compare_fusion.11) | copy-start | bytes 10
  489.3 2.1 copy-start.65
  495.3 3.7 copy-start.39
  507.1 7.1 %copy-start.41 = (f32[64,4]{1,0:T(8,128)S(1)}, f32[64,4]{1,0:T(8,128)}, u32[]{:S(2)}) copy-start(f32[64,4]{1,0:T(8,128)} %get-tuple-element.235) | copy-start | bytes 3076
  507.1 7.2 %copy-start.63 = (f32[64,4]{0,1:T(4,128)S(1)}, f32[64,4]{0,1:T(4,128)}, u32[]{:S(2)}) copy-start(f32[64,4]{0,1:T(4,128)} %param.22) | copy-start | bytes 3076
  507.1 10.9 %copy-start.64 = (f32[788]{0:T(1024)S(1)}, f32[788]{0:T(1024)}, u32[]{:S(2)}) copy-start(f32[788]{0:T(1024)} %get-tuple-element.202) | copy-start | bytes 9460
  507.1 10.9 %copy-start.6 = (f32[788,512]{1,0:T(8,128)S(1)}, f32[788,512]{1,0:T(8,128)}, u32[]{:S(2)}) copy-start(f32[788,512]{1,0:T(8,128)} %copy-done.5) | copy-start | bytes 4841476
  507.1 10.9 %copy-start.12 = (bf16[788,512]{1,0:T(8,128)(2,1)S(1)}, bf16[788,512]{1,0:T(8,128)(2,1)}, u32[]{:S(2)}) copy-start(bf16[788,512]{1,0:T(8,128)(2,1)} %param.18) | copy-start | bytes 2420740
  507.1 10.9 %copy-start.47 = (f32[788]{0:T(1024)S(1)}, f32[788]{0:T(1024)}, u32[]{:S(2)}) copy-start(f32[788]{0:T(1024)} %copy-done.46) | copy-start | bytes 9460
  507.2 10.9 %copy-start.50 = (f32[788]{0:T(1024)S(1)}, f32[788]{0:T(1024)}, u32[]{:S(2)}) copy-start(f32[788]{0:T(1024)} %copy-done.48) | copy-start | bytes 9460
  507.2 10.9 %copy-start.52 = (f32[788]{0:T(1024)S(1)}, f32[788]{0:T(1024)}, u32[]{:S(2)}) copy-start(f32[788]{0:T(1024)} %copy-done.51) | copy-start | bytes 9460
  518.0 3.1 copy-start.19
  521.1 2.3 copy-start.18
  (11 other events, 10.2 us)

commit v7 on v6

--- a/solution.py
+++ b/solution.py
@@ -823,8 +823,8 @@
     counts = counts.T.reshape(E * micro)
     onehot = (places[:, :, None] == jnp.arange(E * CAPP, dtype=jnp.int32)).astype(BF16)
     second_m = second.reshape(micro, MB_TOK, D)
-    pair = jnp.concatenate([second_m, second_m], 1)
-    table_in = jnp.einsum("mnr,mnd->mrd", onehot, pair, preferred_element_type=F32).astype(BF16)
+    onehot_sum = onehot[:, :MB_TOK] + onehot[:, MB_TOK:]
+    table_in = jnp.einsum("mnr,mnd->mrd", onehot_sum, second_m, preferred_element_type=F32).astype(BF16)
 
     hidden_pre, hidden, y_all = ffn_forward(
         counts, table_in, w_up_all, b_up[:, None, :], w_down_all, table[7 : 7 + E][:, None, :], micro
@@ -844,7 +844,6 @@
     g_up_bias_all = g_b1[:, 0, :]
     g_bias_down = g_b2[:, 0, :]
 
-    onehot_sum = onehot[:, :MB_TOK] + onehot[:, MB_TOK:]
     d_picked = pick_rows(onehot_sum, d_table).reshape(rows, D)
 
     d_probs = jnp.sum(jnp.where(picked, d_gate[:, :, None], 0.0), 1)

time: 535 us -> 537 us (level)
  other arithmetic: 42 us -> 49.1 us
    unnamed x164 -> x132, local copies, waits for them, and re-layouts: 19.5 us -> 15.7 us
where the time goes in v7:
time: 537 us; the launch traced here: 527 us
  Pallas kernels  334 us (62%)
  local copies, waits for them, and re-layouts  76.5 us (14%)
  matrix products  65.8 us (12%)
  other arithmetic  49.1 us (9%)
    pallas_call x1, Pallas kernels, grad_reduce(): pl.pallas_call(functools.partial(ring_rs2_kernel, groups, x_pair), out_sh...  126 us
    pallas_call x1, Pallas kernels, ring_all_gather(): pl.pallas_call(functools.partial(ring_ag_kernel, groups), out_shape=shape...  101 us
    pallas_call x1, Pallas kernels, ffn_backward(): pl.pallas_call(functools.partial(ffn_bwd_kernel, micro), grid_spec=grid_s...  52.3 us
    pallas_call x1, Pallas kernels, ffn_forward(): pl.pallas_call(functools.partial(ffn_fwd_kernel, micro), grid_spec=grid_s...  40.6 us
    dot_general x2, matrix products, pick_rows(): both = jnp.einsum('mnr,mrd->mnd', onehot, split, preferred_element_type=F32)  17.6 us
    reshape x8, local copies, waits for them, and re-layouts, split_heads(): return part.reshape(-1, S, HEADS, HEAD_DIM)  16.5 us
    unnamed x132, local copies, waits for them, and re-layouts  15.7 us
    pallas_call x2, Pallas kernels, adamw_pass(): pl.pallas_call(functools.partial(adamw_kernel, rate), grid=(n,), in_specs...  13.9 us

profile of v7, /device:TPU:1, one launch (start us, length us, event | category | flops | bytes accessed | tf_op | source)
XLA Modules:
  0.0 527.4 jit_solution(1959983864622240843)
XLA Ops:
  3.3 1.4 convert_reduce_fusion
  4.7 1.5 fusion.22
  8.8 2.3 reduce-window.6
  17.8 2.7 convert_element_type.104.refs_0_
  20.5 1.1 convert_element_type.105.refs_1_
  21.9 1.3 reshape.292
  23.2 3.8 fusion.2
  27.0 101.1 %shard_map.344 = (bf16[4,512,2048]{2,1,0:T(8,128)(2,1)}, bf16[4,2048,512]{2,1,0:T(8,128)(2,1)}, bf16[512,2560]{1,0:T(8,128)(2,1)}) custom-call(bf16[4,64,2048]{2,1,0:T(8,128)(2,1)} %convert_element_type.104.refs_0_, bf16[4,256,512]{2,1,0:T(8,128)(2,1)} %convert_element_type.105.refs_1_, bf16[64,2560]{1,0:T(8,128)(2,1)} %pad.14.refs_2_), custom_call_target="tpu_custom_call" | custom-call | bytes 19398656 | tf_op jit(solution)/shard_map/pallas_call | solution.py:271
  128.1 1.0 slice_convert_fusion
  130.3 4.5 copy.322
  136.7 3.0 add_convert_fusion
  139.7 1.0 fusion.113
  140.7 2.0 reshape.311
  142.7 2.0 copy.327
  144.8 2.0 reshape.310
  146.8 2.0 copy.326
  148.9 3.5 reshape.309
  152.4 3.0 copy.328
  155.4 1.1 multiply_reduce_fusion.1
  156.5 1.4 fusion.5
  158.0 1.4 copy-done.2
  159.4 1.6 fusion.37
  162.7 2.1 fusion.117
  165.6 1.4 fusion.118
  167.2 5.4 %convolution_convert_fusion.x_ref = bf16[2,2048,512]{2,1,0:T(8,128)(2,1)S(1)} fusion(bf16[2,394,512]{2,1,0:T(8,128)(2,1)S(1)} %reshape.288, bf16[2,788,2048]{2,1,0:T(8,128)(2,1)} %fusion.2), kind=kOutput, calls=%fused_computation.16 | convolution fusion | flops 1656266752 | bytes 11554816 | tf_op jit(solution)/shard_map/mnr,mnd->mrd/dot_general | solution.py:827
  172.6 40.6 %shard_map.345 = (f32[2,2048,2048]{2,1,0:T(8,128)}, bf16[2,2048,2048]{2,1,0:T(8,128)(2,1)}, bf16[2,2048,1024]{2,1,0:T(8,128)(2,1)}) custom-call(s32[8]{0:T(128)S(1)} %reshape.287.counts, bf16[2,2048,512]{2,1,0:T(8,128)(2,1)S(1)} %convolution_convert_fusion.x_ref, bf16[4,512,2048]{2,1,0:T(8,128)(2,1)} %get-tuple-element.42.w1_ref, ...), custom_call_target="tpu_custom_call" | custom-call | flops 8589934592 | bytes 31457280 | tf_op jit(solution)/shard_map/pallas_call | solution.py:541
  213.2 9.7 %fusion.1 = f32[2,788,1024]{2,1,0:T(8,128)S(1)} fusion(bf16[2,2048,1024]{2,1,0:T(8,128)(2,1)} %get-tuple-element.44, s32[2,788]{1,0:T(2,128)S(1)} %multiply_add_fusion.4), kind=kOutput, calls=%fused_computation.2 | convolution fusion | flops 6613450752 | bytes 14850208 | tf_op jit(solution)/shard_map/mnr,mrd->mnd/dot_general | solution.py:690
  223.8 2.1 fusion.112
  225.9 1.6 reshape.289
  227.4 2.7 reshape.290
  230.2 2.2 multiply_reduce_fusion.5
  232.9 2.9 multiply_convert_fusion.4
  236.6 8.3 %fusion.7.dy_ref = bf16[2,2048,512]{2,1,0:T(8,128)(2,1)} fusion(s32[2,788]{1,0:T(2,128)S(1)} %multiply_add_fusion.4, bf16[2,394,512]{2,1,0:T(8,128)(2,1)} %get-tuple-element.228, bf16[2,394,512]{2,1,0:T(8,128)(2,1)} %get-tuple-element.227), kind=kOutput, calls=%fused_computation.15 | convolution fusion | flops 3313664000 | bytes 5814432 | tf_op jit(solution)/shard_map/mnr,mnd->mrd/dot_general | solution.py:841
  245.0 52.3 %shard_map.346 = (bf16[2,2048,1024]{2,1,0:T(8,128)(2,1)}, bf16[4,512,2048]{2,1,0:T(8,128)(2,1)}, bf16[4,2048,512]{2,1,0:T(8,128)(2,1)}, f32[4,1,2048]{2,1,0:T(1,128)}, f32[4,1,512]{2,1,0:T(1,128)}) custom-call(s32[8]{0:T(128)} %copy-done.1, bf16[2,2048,512]{2,1,0:T(8,128)(2,1)} %fusion.7.dy_ref, bf16[2,2048,512]{2,1,0:T(8,128)(2,1)} %copy-done, ...), custom_call_target="tpu_custom_call" | custom-call | flops 17179869184 | bytes 100663296 | tf_op jit(solution)/shard_map/pallas_call | solution.py:617
  297.3 7.9 %fusion.44 = f32[2,394,1024]{2,1,0:T(8,128)S(1)} fusion(bf16[2,2048,1024]{2,1,0:T(8,128)(2,1)} %get-tuple-element.47, bf16[2,788,2048]{2,1,0:T(8,128)(2,1)} %fusion.2), kind=kOutput, calls=%fused_computation.79 | convolution fusion | flops 3306725376 | bytes 18169856 | tf_op jit(solution)/shard_map/mnr,mrd->mnd/dot_general | solution.py:690
  305.2 1.5 slice_add_fusion.2
  306.7 2.7 reshape.293
  309.5 2.6 multiply_reduce_fusion.2
  312.2 2.3 fusion.111
  314.6 1.1 reshape_squeeze.4
  316.8 1.9 fusion.109
  318.7 1.5 convolution_convert_fusion.3
  320.3 1.7 convolution_convert_fusion.2
  322.8 1.0 copy.336
  323.8 4.2 fusion.34
  328.0 1.8 copy.346
  329.8 3.6 reshape.297
  333.4 7.8 %multiply_reduce_fusion = (f32[4,8,197]{2,1,0:T(8,128)S(1)}, f32[4,8,197,197]{2,3,1,0:T(8,128)}) fusion(f32[4,8,197,197]{2,3,1,0:T(8,128)} %copy-done.2, f32[4,8,197]{2,1,0:T(8,128)S(1)} %log_add_fusion, bf16[4,197,8,64]{1,3,2,0:T(8,128)(2,1)S(1)} %copy.336, bf16[4,197,8,64]{1,3,2,0:T(8,128)(2,1)} %copy.328), kind=kOutput, calls=%fused_computation.5 | convolution fusion | flops 163922912 | bytes 11599360 | tf_op jit(solution)/shard_map/bqhd,bkhd->bhqk/dot_general | solution.py:751
  341.2 4.5 multiply_convert_fusion
  345.7 1.2 fusion.39
  353.3 2.0 fusion.108
  357.0 1.9 add_add_fusion.2
  358.9 3.4 convolution_convert_fusion.1
  363.7 3.5 concatenate.42
  367.2 1.7 pad.16.refs_2_
  369.0 126.1 %shard_map.347 = (f32[4,64,2048]{2,1,0:T(8,128)}, f32[4,256,512]{2,1,0:T(8,128)}, f32[64,2560]{1,0:T(8,128)}) custom-call(bf16[4,512,2048]{2,1,0:T(8,128)(2,1)} %get-tuple-element.48.refs_0_, bf16[4,2048,512]{2,1,0:T(8,128)(2,1)} %get-tuple-element.49.refs_1_, bf16[512,2560]{1,0:T(8,128)(2,1)} %pad.16.refs_2_), custom_call_target="tpu_custom_call" | custom-call | flops 9699328 | bytes 19398656 | tf_op jit(solution)/shard_map/pallas_call | solution.py:478
  495.2 0.9 broadcast_multiply_fusion.2
  507.5 1.0 fusion.57
  508.5 1.2 fusion.41
  509.7 6.9 %shard_map.349 = (f32[4,256,512]{2,1,0:T(8,128)}, f32[2,4,256,512]{3,2,1,0:T(8,128)}) custom-call(f32[4,256,512]{2,1,0:T(8,128)} %w_ref.3, f32[2,4,256,512]{3,2,1,0:T(8,128)} %m_ref.3, f32[4,256,512]{2,1,0:T(8,128)} %get-tuple-element.299.g_ref), custom_call_target="tpu_custom_call" | custom-call | flops 6291456 | bytes 14680064 | tf_op jit(solution)/shard_map/pallas_call | solution.py:647
  516.5 7.0 %shard_map.348 = (f32[4,64,2048]{2,1,0:T(8,128)}, f32[2,4,64,2048]{3,2,1,0:T(8,128)}) custom-call(f32[4,64,2048]{2,1,0:T(8,128)} %w_ref.2, f32[2,4,64,2048]{3,2,1,0:T(8,128)} %m_ref.2, f32[4,64,2048]{2,1,0:T(8,128)} %get-tuple-element.297.g_ref), custom_call_target="tpu_custom_call" | custom-call | flops 6291456 | bytes 14680064 | tf_op jit(solution)/shard_map/pallas_call | solution.py:647
  523.6 1.3 copy.398
  524.9 1.0 copy-done.16
  525.9 1.3 copy.399
  (243 shorter events, 42.5 us)
Async XLA Ops:
  0.7 15.2 %copy-start.46 = (f32[64,4]{0,1:T(4,128)S(1)}, f32[64,4]{0,1:T(4,128)}, u32[]{:S(2)}) copy-start(f32[64,4]{0,1:T(4,128)} %param.22) | copy-start | bytes 3076
  0.7 14.4 %copy-start.43 = (f32[11,64]{1,0:T(8,128)S(1)}, f32[11,64]{1,0:T(8,128)}, u32[]{:S(2)}) copy-start(f32[11,64]{1,0:T(8,128)} %param.26) | copy-start | bytes 8452
  0.7 16.2 %copy-start.33 = (f32[64,512]{1,0:T(8,128)S(1)}, f32[64,512]{1,0:T(8,128)}, u32[]{:S(2)}) copy-start(f32[64,512]{1,0:T(8,128)} %param.21) | copy-start | bytes 393220
  0.7 16.2 %copy-start.22 = (f32[64,1536]{1,0:T(8,128)S(1)}, f32[64,1536]{1,0:T(8,128)}, u32[]{:S(2)}) copy-start(f32[64,1536]{1,0:T(8,128)} %param.20) | copy-start | bytes 1179652
  12.3 160.3 %copy-start.1 = (s32[8]{0:T(128)}, s32[8]{0:T(128)S(1)}, u32[]{:S(2)}) copy-start(s32[8]{0:T(128)S(1)} %reshape.287.counts) | copy-start | bytes 100
  16.9 3.6 copy-start.15
  20.5 1.4 copy-start.9
  130.3 6.4 %copy-start.7 = (bf16[788,512]{1,0:T(8,128)(2,1)S(1)}, bf16[788,512]{1,0:T(8,128)(2,1)}, u32[]{:S(2)}) copy-start(bf16[788,512]{1,0:T(8,128)(2,1)} %param.17) | copy-start | bytes 2420740
  136.1 0.6 copy-start.54
  144.8 10.6 %copy-start.11 = (bf16[4,197,8,64]{1,3,2,0:T(8,128)(2,1)}, bf16[4,197,8,64]{1,3,2,0:T(8,128)(2,1)S(1)}, u32[]{:S(2)}) copy-start(bf16[4,197,8,64]{1,3,2,0:T(8,128)(2,1)S(1)} %copy.327) | copy-start | bytes 2420740
  148.8 6.6 %copy-start.13 = (bf16[4,197,8,64]{1,3,2,0:T(8,128)(2,1)}, bf16[4,197,8,64]{1,3,2,0:T(8,128)(2,1)S(1)}, u32[]{:S(2)}) copy-start(bf16[4,197,8,64]{1,3,2,0:T(8,128)(2,1)S(1)} %copy.326) | copy-start | bytes 2420740
  156.5 2.8 copy-start.2
  156.5 2.8 copy-start.18
  161.0 1.7 copy-start.56
  162.7 2.1 copy-start.26
  162.7 2.5 copy-start.52
  165.5 7.1 %copy-start.5 = (bf16[788,512]{1,0:T(8,128)(2,1)}, bf16[788,512]{1,0:T(8,128)(2,1)S(1)}, u32[]{:S(2)}) copy-start(bf16[788,512]{1,0:T(8,128)(2,1)S(1)} %add_convert_fusion.2) | copy-start | bytes 2420740
  172.6 40.6 %copy-start = (bf16[2,2048,512]{2,1,0:T(8,128)(2,1)}, bf16[2,2048,512]{2,1,0:T(8,128)(2,1)S(1)}, u32[]{:S(2)}) copy-start(bf16[2,2048,512]{2,1,0:T(8,128)(2,1)S(1)} %convolution_convert_fusion.x_ref) | copy-start | bytes 12582916
  230.2 2.3 copy-start.45
  230.2 2.4 copy-start.6
  309.5 2.6 copy-start.3
  312.1 2.4 copy-start.53
  312.2 2.4 copy-start.44
  315.8 3.0 copy-start.27
  329.8 11.5 %slice-start = ((s8[6553600]{0:T(1024)(128)(4,1)}), s8[2359296]{0:T(1024)(128)(4,1)S(1)}, s32[]{:S(2)}) async-start(s8[6553600]{0:T(1024)(128)(4,1)} %bitcast.121), calls=%async_computation | async-start | bytes 4718592
  333.4 7.8 %slice-start.1 = ((s8[6553600]{0:T(1024)(128)(4,1)}), s8[4194304]{0:T(1024)(128)(4,1)S(1)}, s32[]{:S(2)}) async-start(s8[6553600]{0:T(1024)(128)(4,1)} %bitcast.121), calls=%async_computation.1 | async-start | bytes 8388608
  341.2 4.5 copy-start.14
  345.7 1.2 copy-start.12
  351.0 1.2 copy-start.19
  351.1 1.3 copy-start.8
  351.1 2.2 copy-start.20
  355.3 1.4 copy-start.4
  355.3 1.6 copy-start.10
  357.0 1.9 copy-start.55
  362.6 1.0 copy-start.29
  362.6 1.1 copy-start.30
  362.7 1.1 copy-start.31
  368.9 126.3 %copy-start.35 = (f32[11,64]{0,1:T(8,128)S(1)}, f32[11,64]{0,1:T(8,128)}, u32[]{:S(2)}) copy-start(f32[11,64]{0,1:T(8,128)} %copy.366) | copy-start | bytes 8452
  368.9 126.3 %copy-start.39 = (f32[1,11,64]{1,2,0:T(8,128)S(1)}, f32[1,11,64]{1,2,0:T(8,128)}, u32[]{:S(2)}) copy-start(f32[1,11,64]{1,2,0:T(8,128)} %copy.390) | copy-start | bytes 8452
  368.9 126.3 %copy-start.40 = (f32[1,11,64]{1,2,0:T(8,128)S(1)}, f32[1,11,64]{1,2,0:T(8,128)}, u32[]{:S(2)}) copy-start(f32[1,11,64]{1,2,0:T(8,128)} %copy.391) | copy-start | bytes 8452
  368.9 127.4 %copy-start.41 = (f32[2,11,64]{2,0,1:T(2,128)S(1)}, f32[2,11,64]{2,0,1:T(2,128)}, u32[]{:S(2)}) copy-start(f32[2,11,64]{2,0,1:T(2,128)} %param.33) | copy-start | bytes 16900
  368.9 127.4 %copy-start.51 = (pred[2]{0:T(512)(128)(4,1)S(1)}, pred[2]{0:T(512)(128)(4,1)}, u32[]{:S(2)}) copy-start(pred[2]{0:T(512)(128)(4,1)} %iota_compare_fusion.8) | copy-start | bytes 10
  369.0 131.1 %copy-start.37 = (f32[1,64,4]{2,1,0:T(8,128)S(1)}, f32[1,64,4]{2,1,0:T(8,128)}, u32[]{:S(2)}) copy-start(f32[1,64,4]{2,1,0:T(8,128)} %copy.354) | copy-start | bytes 3076
  369.0 131.1 %copy-start.38 = (f32[1,64,4]{2,1,0:T(8,128)S(1)}, f32[1,64,4]{2,1,0:T(8,128)}, u32[]{:S(2)}) copy-start(f32[1,64,4]{2,1,0:T(8,128)} %copy.389) | copy-start | bytes 3076
  369.0 132.1 %copy-start.49 = (f32[2,64,4]{1,2,0:T(4,128)S(1)}, f32[2,64,4]{1,2,0:T(4,128)}, u32[]{:S(2)}) copy-start(f32[2,64,4]{1,2,0:T(4,128)} %param.29) | copy-start | bytes 6148
  369.0 132.8 %copy-start.47 = (f32[64,4]{0,1:T(4,128)S(1)}, f32[64,4]{0,1:T(4,128)}, u32[]{:S(2)}) copy-start(f32[64,4]{0,1:T(4,128)} %param.22) | copy-start | bytes 3076
  369.0 133.6 %copy-start.36 = (f32[64,4]{1,0:T(8,128)S(1)}, f32[64,4]{1,0:T(8,128)}, u32[]{:S(2)}) copy-start(f32[64,4]{1,0:T(8,128)} %copy.359) | copy-start | bytes 3076
  369.0 134.5 %copy-start.42 = (f32[2,4,256]{2,1,0:T(4,128)S(1)}, f32[2,4,256]{2,1,0:T(4,128)}, u32[]{:S(2)}) copy-start(f32[2,4,256]{2,1,0:T(4,128)} %param.31) | copy-start | bytes 24580
  369.0 134.5 %copy-start.50 = (f32[4,256]{1,0:T(4,128)S(1)}, f32[4,256]{1,0:T(4,128)}, u32[]{:S(2)}) copy-start(f32[4,256]{1,0:T(4,128)} %param.24) | copy-start | bytes 12292
  495.2 10.6 %copy-start.28 = (f32[64,2560]{1,0:T(8,128)S(1)}, f32[64,2560]{1,0:T(8,128)}, u32[]{:S(2)}) copy-start(f32[64,2560]{1,0:T(8,128)} %get-tuple-element.52) | copy-start | bytes 1966084
  495.2 10.7 %copy-start.25 = (f32[2,64,512]{2,1,0:T(8,128)S(1)}, f32[2,64,512]{2,1,0:T(8,128)}, u32[]{:S(2)}) copy-start(f32[2,64,512]{2,1,0:T(8,128)} %param.28) | copy-start | bytes 786436
  495.2 10.7 %copy-start.34 = (f32[64,512]{1,0:T(8,128)S(1)}, f32[64,512]{1,0:T(8,128)}, u32[]{:S(2)}) copy-start(f32[64,512]{1,0:T(8,128)} %param.21) | copy-start | bytes 393220
  498.5 8.9 %copy-start.21 = (f32[2,64,1536]{2,1,0:T(8,128)S(1)}, f32[2,64,1536]{2,1,0:T(8,128)}, u32[]{:S(2)}) copy-start(f32[2,64,1536]{2,1,0:T(8,128)} %param.27) | copy-start | bytes 2359300
  498.5 8.9 %copy-start.23 = (f32[64,1536]{1,0:T(8,128)S(1)}, f32[64,1536]{1,0:T(8,128)}, u32[]{:S(2)}) copy-start(f32[64,1536]{1,0:T(8,128)} %param.20) | copy-start | bytes 1179652
  503.5 5.0 copy-start.48
  505.7 2.8 copy-start.32
  505.8 3.9 copy-start.24
  516.5 7.0 %copy-start.17 = (f32[4,64,2048]{2,1,0:T(8,128)S(1)}, f32[4,64,2048]{2,1,0:T(8,128)}, u32[]{:S(2)}) copy-start(f32[4,64,2048]{2,1,0:T(8,128)} %get-tuple-element.297.g_ref) | copy-start | bytes 6291460
  523.6 2.3 copy-start.16

commit v8 on v6

--- a/solution.py
+++ b/solution.py
@@ -271,7 +271,7 @@
     return pl.pallas_call(
         functools.partial(ring_ag_kernel, groups),
         out_shape=shapes,
-        in_specs=[pl.BlockSpec(memory_space=pl.ANY)] * 3,
+        in_specs=[pl.BlockSpec(memory_space=pltpu.VMEM)] * 3,
         out_specs=[pl.BlockSpec(memory_space=pl.ANY)] * 3,
         scratch_shapes=[
             pltpu.SemaphoreType.DMA((2, groups - 1, n_items)),

time: 535 us -> 536 us (level)
  no operation moved by 1% of the time
where the time goes in v8:
time: 536 us; the launch traced here: 526 us
  Pallas kernels  334 us (62%)
  local copies, waits for them, and re-layouts  77.4 us (14%)
  matrix products  70.4 us (13%)
  other arithmetic  42 us (8%)
    pallas_call x1, Pallas kernels, grad_reduce(): pl.pallas_call(functools.partial(ring_rs2_kernel, groups, x_pair), out_sh...  126 us
    pallas_call x1, Pallas kernels, ring_all_gather(): pl.pallas_call(functools.partial(ring_ag_kernel, groups), out_shape=shape...  102 us
    pallas_call x1, Pallas kernels, ffn_backward(): pl.pallas_call(functools.partial(ffn_bwd_kernel, micro), grid_spec=grid_s...  52.4 us
    pallas_call x1, Pallas kernels, ffn_forward(): pl.pallas_call(functools.partial(ffn_fwd_kernel, micro), grid_spec=grid_s...  39.5 us
    unnamed x164, local copies, waits for them, and re-layouts  19.5 us
    dot_general x2, matrix products, pick_rows(): both = jnp.einsum('mnr,mrd->mnd', onehot, split, preferred_element_type=F32)  15.7 us
    pallas_call x2, Pallas kernels, adamw_pass(): pl.pallas_call(functools.partial(adamw_kernel, rate), grid=(n,), in_specs...  13.9 us
    reshape x8, local copies, waits for them, and re-layouts, split_heads(): return part.reshape(-1, S, HEADS, HEAD_DIM)  11.3 us

profile of v8, /device:TPU:1, one launch (start us, length us, event | category | flops | bytes accessed | tf_op | source)
XLA Modules:
  0.0 526.2 jit_solution(9119471424660552208)
XLA Ops:
  0.7 2.9 convert_element_type.104.refs_0_
  3.6 1.1 convert_element_type.105.refs_1_
  6.2 102.4 %shard_map.344 = (bf16[4,512,2048]{2,1,0:T(8,128)(2,1)}, bf16[4,2048,512]{2,1,0:T(8,128)(2,1)}, bf16[512,2560]{1,0:T(8,128)(2,1)}) custom-call(bf16[4,64,2048]{2,1,0:T(8,128)(2,1)} %convert_element_type.104.refs_0_, bf16[4,256,512]{2,1,0:T(8,128)(2,1)} %convert_element_type.105.refs_1_, bf16[64,2560]{1,0:T(8,128)(2,1)} %pad.14.refs_2_), custom_call_target="tpu_custom_call" | custom-call | bytes 19398656 | tf_op jit(solution)/shard_map/pallas_call | solution.py:271
  108.7 4.5 copy.322
  116.4 3.0 add_convert_fusion
  119.4 1.3 fusion.121
  121.5 1.0 copy.326
  122.6 3.5 reshape.311
  126.1 2.0 copy.327
  128.2 1.1 multiply_reduce_fusion.1
  129.3 1.3 fusion.7
  130.6 1.5 copy-done.2
  132.9 1.2 copy.328
  134.2 4.8 fusion.45
  140.7 2.1 fusion.125
  143.6 1.4 fusion.126
  145.5 2.3 reduce-window.6
  148.7 7.3 %fusion.9.x_ref = bf16[2,2048,512]{2,1,0:T(8,128)(2,1)} fusion(s32[2,788]{1,0:T(2,128)S(1)} %multiply_add_fusion.4, bf16[2,394,512]{2,1,0:T(8,128)(2,1)S(1)} %reshape.288), kind=kOutput, calls=%fused_computation.17 | convolution fusion | flops 3313664000 | bytes 5007520 | tf_op jit(solution)/shard_map/mnr,mnd->mrd/dot_general | solution.py:827
  159.2 2.2 copy-done
  161.4 39.5 %shard_map.345 = (f32[2,2048,2048]{2,1,0:T(8,128)}, bf16[2,2048,2048]{2,1,0:T(8,128)(2,1)}, bf16[2,2048,1024]{2,1,0:T(8,128)(2,1)}) custom-call(s32[8]{0:T(128)S(1)} %reshape.287.counts, bf16[2,2048,512]{2,1,0:T(8,128)(2,1)S(1)} %copy-done, bf16[4,512,2048]{2,1,0:T(8,128)(2,1)} %get-tuple-element.42.w1_ref, f32[4,1,2048]{2,1,0:T(1,128)S(1)} %reshape.308.b1_ref, ...), custom_call_target="tpu_custom_call" | custom-call | flops 8589934592 | bytes 31457280 | tf_op jit(solution)/shard_map/pallas_call | solution.py:541
  200.9 9.7 %fusion.2 = f32[2,788,1024]{2,1,0:T(8,128)S(1)} fusion(bf16[2,2048,1024]{2,1,0:T(8,128)(2,1)} %get-tuple-element.44, s32[2,788]{1,0:T(2,128)S(1)} %multiply_add_fusion.4), kind=kOutput, calls=%fused_computation.3 | convolution fusion | flops 6613450752 | bytes 14850208 | tf_op jit(solution)/shard_map/mnr,mrd->mnd/dot_general | solution.py:690
  211.4 2.1 fusion.120
  213.5 1.6 reshape.289
  215.1 2.7 reshape.290
  217.9 2.1 multiply_reduce_fusion.5
  220.2 2.5 reshape.292
  222.7 1.7 multiply_convert_fusion.4
  224.4 7.3 %fusion.10.dy_ref = bf16[2,2048,512]{2,1,0:T(8,128)(2,1)} fusion(s32[2,788]{1,0:T(2,128)S(1)} %multiply_add_fusion.4, bf16[2,394,512]{2,1,0:T(8,128)(2,1)S(1)} %get-tuple-element.228, bf16[2,394,512]{2,1,0:T(8,128)(2,1)S(1)} %get-tuple-element.227), kind=kOutput, calls=%fused_computation.18 | convolution fusion | flops 3313664000 | bytes 5814432 | tf_op jit(solution)/shard_map/mnr,mnd->mrd/dot_general | solution.py:841
  231.7 52.4 %shard_map.346 = (bf16[2,2048,1024]{2,1,0:T(8,128)(2,1)}, bf16[4,512,2048]{2,1,0:T(8,128)(2,1)}, bf16[4,2048,512]{2,1,0:T(8,128)(2,1)}, f32[4,1,2048]{2,1,0:T(1,128)}, f32[4,1,512]{2,1,0:T(1,128)}) custom-call(s32[8]{0:T(128)} %copy-done.1, bf16[2,2048,512]{2,1,0:T(8,128)(2,1)} %fusion.10.dy_ref, bf16[2,2048,512]{2,1,0:T(8,128)(2,1)} %fusion.9.x_ref, ...), custom_call_target="tpu_custom_call" | custom-call | flops 17179869184 | bytes 100663296 | tf_op jit(solution)/shard_map/pallas_call | solution.py:617
  284.1 1.1 fusion.1
  285.2 5.9 %fusion.13 = f32[2,394,1024]{2,1,0:T(8,128)S(1)} fusion(bf16[2,2048,1024]{2,1,0:T(8,128)(2,1)} %get-tuple-element.47, bf16[2,788,2048]{2,1,0:T(8,128)(2,1)S(1)} %fusion.1), kind=kOutput, calls=%fused_computation.21 | convolution fusion | flops 3306725376 | bytes 18169856 | tf_op jit(solution)/shard_map/mnr,mrd->mnd/dot_general | solution.py:690
  291.1 1.5 slice_add_fusion.3
  292.6 2.7 reshape.293
  295.4 2.6 multiply_reduce_fusion.2
  298.0 1.7 fusion.119
  299.8 1.2 copy-done.5
  302.1 1.7 convolution_convert_fusion.1
  304.6 1.0 copy.336
  305.7 4.2 fusion.42
  309.8 1.8 copy.346
  311.6 3.6 reshape.297
  315.3 7.8 %multiply_reduce_fusion = (f32[4,8,197]{2,1,0:T(8,128)S(1)}, f32[4,8,197,197]{2,3,1,0:T(8,128)}) fusion(f32[4,8,197,197]{2,3,1,0:T(8,128)} %copy-done.2, f32[4,8,197]{2,1,0:T(8,128)S(1)} %log_add_fusion, bf16[4,197,8,64]{1,3,2,0:T(8,128)(2,1)S(1)} %copy.336, bf16[4,197,8,64]{1,3,2,0:T(8,128)(2,1)} %copy-done.23), kind=kOutput, calls=%fused_computation.6 | convolution fusion | flops 163922912 | bytes 11599360 | tf_op jit(solution)/shard_map/bqhd,bkhd->bhqk/dot_general | solution.py:751
  323.1 4.5 multiply_convert_fusion
  327.6 1.2 fusion.47
  330.9 2.7 fusion.46
  339.6 2.0 fusion.116
  341.6 1.1 copy-done.20
  342.7 1.5 fusion.26
  345.8 1.5 convolution_convert_fusion.2
  347.7 4.1 convolution_convert_fusion
  351.9 1.1 reshape_squeeze.4
  353.5 4.4 concatenate.46
  357.9 3.3 pad.16.refs_2_
  361.2 126.1 %shard_map.347 = (f32[4,64,2048]{2,1,0:T(8,128)}, f32[4,256,512]{2,1,0:T(8,128)}, f32[64,2560]{1,0:T(8,128)}) custom-call(bf16[4,512,2048]{2,1,0:T(8,128)(2,1)} %get-tuple-element.48.refs_0_, bf16[4,2048,512]{2,1,0:T(8,128)(2,1)} %get-tuple-element.49.refs_1_, bf16[512,2560]{1,0:T(8,128)(2,1)} %pad.16.refs_2_), custom_call_target="tpu_custom_call" | custom-call | flops 9699328 | bytes 19398656 | tf_op jit(solution)/shard_map/pallas_call | solution.py:478
  492.7 1.4 broadcast_multiply_fusion.3
  494.3 1.4 fusion.99
  496.6 1.7 fusion.75
  499.2 1.0 fusion.64
  500.3 1.2 fusion.49
  501.5 6.9 %shard_map.348 = (f32[4,64,2048]{2,1,0:T(8,128)}, f32[2,4,64,2048]{3,2,1,0:T(8,128)}) custom-call(f32[4,64,2048]{2,1,0:T(8,128)} %w_ref.2, f32[2,4,64,2048]{3,2,1,0:T(8,128)} %m_ref.2, f32[4,64,2048]{2,1,0:T(8,128)} %get-tuple-element.297.g_ref), custom_call_target="tpu_custom_call" | custom-call | flops 6291456 | bytes 14680064 | tf_op jit(solution)/shard_map/pallas_call | solution.py:647
  508.4 7.0 %shard_map.349 = (f32[4,256,512]{2,1,0:T(8,128)}, f32[2,4,256,512]{3,2,1,0:T(8,128)}) custom-call(f32[4,256,512]{2,1,0:T(8,128)} %w_ref.3, f32[2,4,256,512]{3,2,1,0:T(8,128)} %m_ref.3, f32[4,256,512]{2,1,0:T(8,128)} %get-tuple-element.299.g_ref), custom_call_target="tpu_custom_call" | custom-call | flops 6291456 | bytes 14680064 | tf_op jit(solution)/shard_map/pallas_call | solution.py:647
  519.2 3.1 add_add_fusion.2
  522.3 1.3 copy.398
  524.7 1.3 copy.399
  (275 shorter events, 39.1 us)
Async XLA Ops:
  0.7 2.9 copy-start.17
  3.5 1.2 copy-start.66
  3.5 1.6 copy-start.40
  3.5 1.6 copy-start.55
  3.6 1.7 copy-start.62
  108.7 6.4 %copy-start.9 = (bf16[788,512]{1,0:T(8,128)(2,1)S(1)}, bf16[788,512]{1,0:T(8,128)(2,1)}, u32[]{:S(2)}) copy-start(bf16[788,512]{1,0:T(8,128)(2,1)} %param.17) | copy-start | bytes 2420740
  122.6 5.6 %copy-start.15 = (bf16[4,197,8,64]{1,3,2,0:T(8,128)(2,1)}, bf16[4,197,8,64]{1,3,2,0:T(8,128)(2,1)S(1)}, u32[]{:S(2)}) copy-start(bf16[4,197,8,64]{1,3,2,0:T(8,128)(2,1)S(1)} %copy.326) | copy-start | bytes 2420740
  129.3 2.8 copy-start.2
  129.3 2.8 copy-start.26
  134.2 4.8 copy-start.23
  140.7 2.1 copy-start.32
  140.7 2.5 copy-start.53
  140.7 2.5 copy-start.70
  143.3 2.0 copy-start.58
  143.6 12.4 %copy-start.7 = (bf16[788,512]{1,0:T(8,128)(2,1)}, bf16[788,512]{1,0:T(8,128)(2,1)S(1)}, u32[]{:S(2)}) copy-start(bf16[788,512]{1,0:T(8,128)(2,1)S(1)} %add_convert_fusion.2) | copy-start | bytes 2420740
  156.2 44.7 %copy-start.1 = (s32[8]{0:T(128)}, s32[8]{0:T(128)S(1)}, u32[]{:S(2)}) copy-start(s32[8]{0:T(128)S(1)} %reshape.287.counts) | copy-start | bytes 100
  159.2 2.2 copy-start
  220.1 75.3 %copy-start.43 = (bf16[788,4]{0,1:T(4,128)(2,1)}, bf16[788,4]{0,1:T(4,128)(2,1)S(1)}, u32[]{:S(2)}) copy-start(bf16[788,4]{0,1:T(4,128)(2,1)S(1)} %multiply_convert_fusion.5) | copy-start | bytes 18916
  295.4 2.6 copy-start.4
  298.0 2.9 copy-start.11
  299.8 1.5 copy-start.51
  311.6 11.4 %slice-start = ((s8[6553600]{0:T(1024)(128)(4,1)}), s8[2359296]{0:T(1024)(128)(4,1)S(1)}, s32[]{:S(2)}) async-start(s8[6553600]{0:T(1024)(128)(4,1)} %bitcast.120), calls=%async_computation | async-start | bytes 4718592
  315.3 7.8 %slice-start.1 = ((s8[6553600]{0:T(1024)(128)(4,1)}), s8[4194304]{0:T(1024)(128)(4,1)S(1)}, s32[]{:S(2)}) async-start(s8[6553600]{0:T(1024)(128)(4,1)} %bitcast.120), calls=%async_computation.1 | async-start | bytes 8388608
  323.1 4.5 copy-start.16
  327.5 1.7 copy-start.3
  329.3 1.7 copy-start.14
  335.3 1.2 copy-start.24
  336.6 1.5 copy-start.21
  337.0 1.7 copy-start.10
  337.0 2.6 copy-start.25
  337.0 2.6 copy-start.60
  339.5 3.1 copy-start.49
  339.6 4.6 copy-start.71
  341.5 3.2 copy-start.8
  341.5 3.2 copy-start.44
  341.5 4.2 copy-start.33
  341.6 4.2 copy-start.35
  341.6 5.7 %copy-start.46 = (f32[788]{0:T(1024)}, f32[788]{0:T(1024)S(1)}, u32[]{:S(2)}) copy-start(f32[788]{0:T(1024)S(1)} %multiply_multiply_fusion.10) | copy-start | bytes 9460
  344.1 3.1 copy-start.61
  345.7 2.0 copy-start.22
  347.7 4.1 copy-start.57
  347.7 5.7 %copy-start.37 = (bf16[512,512]{1,0:T(8,128)(2,1)S(1)}, bf16[512,512]{1,0:T(8,128)(2,1)}, u32[]{:S(2)}) copy-start(bf16[512,512]{1,0:T(8,128)(2,1)} %convolution_convert_fusion.2) | copy-start | bytes 1572868
  347.7 5.7 %copy-start.38 = (bf16[512,4]{1,0:T(8,128)(2,1)S(1)}, bf16[512,4]{1,0:T(8,128)(2,1)}, u32[]{:S(2)}) copy-start(bf16[512,4]{1,0:T(8,128)(2,1)} %copy.350) | copy-start | bytes 12292
  361.2 126.1 %copy-start.45 = (f32[2,11,64]{2,0,1:T(2,128)S(1)}, f32[2,11,64]{2,0,1:T(2,128)}, u32[]{:S(2)}) copy-start(f32[2,11,64]{2,0,1:T(2,128)} %param.33) | copy-start | bytes 16900
  361.2 126.3 %copy-start.56 = (f32[11,64]{1,0:T(8,128)S(1)}, f32[11,64]{1,0:T(8,128)}, u32[]{:S(2)}) copy-start(f32[11,64]{1,0:T(8,128)} %param.26) | copy-start | bytes 8452
  361.2 129.3 %copy-start.54 = (f32[2,4,256]{2,1,0:T(4,128)S(1)}, f32[2,4,256]{2,1,0:T(4,128)}, u32[]{:S(2)}) copy-start(f32[2,4,256]{2,1,0:T(4,128)} %param.31) | copy-start | bytes 24580
  361.2 129.3 %copy-start.67 = (f32[4,256]{1,0:T(4,128)S(1)}, f32[4,256]{1,0:T(4,128)}, u32[]{:S(2)}) copy-start(f32[4,256]{1,0:T(4,128)} %param.24) | copy-start | bytes 12292
  361.2 135.4 %copy-start.31 = (f32[2,64,512]{2,1,0:T(8,128)S(1)}, f32[2,64,512]{2,1,0:T(8,128)}, u32[]{:S(2)}) copy-start(f32[2,64,512]{2,1,0:T(8,128)} %param.28) | copy-start | bytes 786436
  487.3 11.8 %copy-start.36 = (f32[64,2560]{1,0:T(8,128)S(1)}, f32[64,2560]{1,0:T(8,128)}, u32[]{:S(2)}) copy-start(f32[64,2560]{1,0:T(8,128)} %get-tuple-element.52) | copy-start | bytes 1966084
  488.5 10.7 %copy-start.27 = (f32[2,64,1536]{2,1,0:T(8,128)S(1)}, f32[2,64,1536]{2,1,0:T(8,128)}, u32[]{:S(2)}) copy-start(f32[2,64,1536]{2,1,0:T(8,128)} %param.27) | copy-start | bytes 2359300
  488.5 10.7 %copy-start.29 = (f32[64,1536]{1,0:T(8,128)S(1)}, f32[64,1536]{1,0:T(8,128)}, u32[]{:S(2)}) copy-start(f32[64,1536]{1,0:T(8,128)} %param.20) | copy-start | bytes 1179652
  488.6 10.5 %copy-start.68 = (pred[2]{0:T(512)(128)(4,1)}, pred[2]{0:T(512)(128)(4,1)S(1)}, u32[]{:S(2)}) copy-start(pred[2]{0:T(512)(128)(4,1)S(1)} %iota_compare_fusion.11) | copy-start | bytes 10
  490.5 2.1 copy-start.65
  496.6 3.7 copy-start.39
  508.3 7.1 %copy-start.41 = (f32[64,4]{1,0:T(8,128)S(1)}, f32[64,4]{1,0:T(8,128)}, u32[]{:S(2)}) copy-start(f32[64,4]{1,0:T(8,128)} %get-tuple-element.235) | copy-start | bytes 3076
  508.3 7.2 %copy-start.63 = (f32[64,4]{0,1:T(4,128)S(1)}, f32[64,4]{0,1:T(4,128)}, u32[]{:S(2)}) copy-start(f32[64,4]{0,1:T(4,128)} %param.22) | copy-start | bytes 3076
  508.3 10.9 %copy-start.64 = (f32[788]{0:T(1024)S(1)}, f32[788]{0:T(1024)}, u32[]{:S(2)}) copy-start(f32[788]{0:T(1024)} %get-tuple-element.202) | copy-start | bytes 9460
  508.3 10.9 %copy-start.6 = (f32[788,512]{1,0:T(8,128)S(1)}, f32[788,512]{1,0:T(8,128)}, u32[]{:S(2)}) copy-start(f32[788,512]{1,0:T(8,128)} %copy-done.5) | copy-start | bytes 4841476
  508.3 10.9 %copy-start.12 = (bf16[788,512]{1,0:T(8,128)(2,1)S(1)}, bf16[788,512]{1,0:T(8,128)(2,1)}, u32[]{:S(2)}) copy-start(bf16[788,512]{1,0:T(8,128)(2,1)} %param.18) | copy-start | bytes 2420740
  508.4 10.9 %copy-start.47 = (f32[788]{0:T(1024)S(1)}, f32[788]{0:T(1024)}, u32[]{:S(2)}) copy-start(f32[788]{0:T(1024)} %copy-done.46) | copy-start | bytes 9460
  508.4 10.9 %copy-start.50 = (f32[788]{0:T(1024)S(1)}, f32[788]{0:T(1024)}, u32[]{:S(2)}) copy-start(f32[788]{0:T(1024)} %copy-done.48) | copy-start | bytes 9460
  508.4 10.9 %copy-start.52 = (f32[788]{0:T(1024)S(1)}, f32[788]{0:T(1024)}, u32[]{:S(2)}) copy-start(f32[788]{0:T(1024)} %copy-done.51) | copy-start | bytes 9460
  519.2 3.1 copy-start.19
  522.3 2.3 copy-start.18
  (11 other events, 10.2 us)

commit v9 on v6

--- a/solution.py
+++ b/solution.py
@@ -709,22 +709,20 @@
 
 def attention_fwd(w_qkv, w_out, table, value):
     rows = value.shape[0]
+    nb = rows // S
     scale = HEAD_DIM ** (-0.5)
     first = layer_norm(value, table[0], table[1]).astype(BF16)
-    qkv_bias = jnp.concatenate([table[2], jnp.zeros((D,), F32), table[3]])
-    qkv = (dot(first, w_qkv) + qkv_bias).astype(BF16)
-    query, key_part, val_part = (
-        split_heads(qkv[:, :D]),
-        split_heads(qkv[:, D : 2 * D]),
-        split_heads(qkv[:, 2 * D :]),
-    )
-    scores = jnp.einsum("bqhd,bkhd->bhqk", query, key_part, preferred_element_type=F32) * scale
+    qkv_bias = jnp.concatenate([table[2], jnp.zeros((D,), F32), table[3]]).reshape(3, 1, HEADS, 1, HEAD_DIM)
+    w3 = w_qkv.reshape(D, 3, HEADS, HEAD_DIM)
+    qkv = (jnp.einsum("bsk,kthd->tbhsd", first.reshape(nb, S, D), w3, preferred_element_type=F32) + qkv_bias).astype(BF16)
+    query, key_part, val_part = qkv[0], qkv[1], qkv[2]
+    scores = jnp.einsum("bhqd,bhkd->bhqk", query, key_part, preferred_element_type=F32) * scale
     peak = jnp.max(scores, -1, keepdims=True)
     expo = jnp.exp(scores - peak)
     total = jnp.sum(expo, -1, keepdims=True)
     probs_att = (expo / total).astype(BF16)
     log_total = peak + jnp.log(total)
-    attended = jnp.einsum("bhqk,bkhd->bqhd", probs_att, val_part, preferred_element_type=F32)
+    attended = jnp.einsum("bhqk,bhkd->bqhd", probs_att, val_part, preferred_element_type=F32)
     attended = attended.reshape(rows, D).astype(BF16)
     resid = value + (dot(attended, w_out) + table[4])
     return first, qkv, log_total, attended, resid
@@ -732,34 +730,31 @@
 
 def attention_bwd(w_qkv, w_out, table, value, first, qkv, log_total, attended, d_resid):
     rows = value.shape[0]
+    nb = rows // S
     scale = HEAD_DIM ** (-0.5)
     d_branch = d_resid.astype(BF16)
     g_bias_out = jnp.sum(d_branch.astype(F32), 0)
     g_out = lax.dot_general(attended, d_branch, (((0,), (0,)), ((), ())), preferred_element_type=F32)
-    d_att = split_heads(
-        lax.dot_general(d_branch, w_out, (((1,), (1,)), ((), ())), preferred_element_type=F32).astype(BF16)
-    )
-    query, key_part, val_part = (
-        split_heads(qkv[:, :D]),
-        split_heads(qkv[:, D : 2 * D]),
-        split_heads(qkv[:, 2 * D :]),
-    )
-    scores = jnp.einsum("bqhd,bkhd->bhqk", query, key_part, preferred_element_type=F32) * scale
+    d_att = jnp.einsum(
+        "bsn,hdn->bhsd", d_branch.reshape(nb, S, D), w_out.reshape(HEADS, HEAD_DIM, D), preferred_element_type=F32
+    ).astype(BF16)
+    query, key_part, val_part = qkv[0], qkv[1], qkv[2]
+    scores = jnp.einsum("bhqd,bhkd->bhqk", query, key_part, preferred_element_type=F32) * scale
     probs_f = jnp.exp(scores - log_total)
     probs_att = probs_f.astype(BF16)
-    d_val = jnp.einsum("bhqk,bqhd->bkhd", probs_att, d_att, preferred_element_type=F32)
-    d_prob = jnp.einsum("bqhd,bkhd->bhqk", d_att, val_part, preferred_element_type=F32)
+    d_val = jnp.einsum("bhqk,bhqd->bhkd", probs_att, d_att, preferred_element_type=F32)
+    d_prob = jnp.einsum("bhqd,bhkd->bhqk", d_att, val_part, preferred_element_type=F32)
     d_score = (probs_f * (d_prob - jnp.sum(d_prob * probs_f, -1, keepdims=True))).astype(BF16)
-    d_query = jnp.einsum("bhqk,bkhd->bqhd", d_score, key_part, preferred_element_type=F32) * scale
-    d_key = jnp.einsum("bhqk,bqhd->bkhd", d_score, query, preferred_element_type=F32) * scale
-    d_qkv = jnp.concatenate(
-        [d_query.reshape(rows, D), d_key.reshape(rows, D), d_val.reshape(rows, D)], 1
-    ).astype(BF16)
+    d_query = jnp.einsum("bhqk,bhkd->bhqd", d_score, key_part, preferred_element_type=F32) * scale
+    d_key = jnp.einsum("bhqk,bhqd->bhkd", d_score, query, preferred_element_type=F32) * scale
+    d_qkv = jnp.stack([d_query, d_key, d_val]).astype(BF16)
     d_qkv_f = d_qkv.astype(F32)
-    g_bias_q = jnp.sum(d_qkv_f[:, :D], 0)
-    g_bias_v = jnp.sum(d_qkv_f[:, 2 * D :], 0)
-    g_qkv = lax.dot_general(first, d_qkv, (((0,), (0,)), ((), ())), preferred_element_type=F32)
-    d_first = lax.dot_general(d_qkv, w_qkv, (((1,), (1,)), ((), ())), preferred_element_type=F32)
+    g_bias_q = jnp.sum(d_qkv_f[0], (0, 2)).reshape(D)
+    g_bias_v = jnp.sum(d_qkv_f[2], (0, 2)).reshape(D)
+    first_b = first.reshape(nb, S, D)
+    g_qkv = jnp.einsum("bsk,tbhsd->kthd", first_b, d_qkv, preferred_element_type=F32).reshape(D, 3 * D)
+    w3 = w_qkv.reshape(D, 3, HEADS, HEAD_DIM)
+    d_first = jnp.einsum("tbhsd,kthd->bsk", d_qkv, w3, preferred_element_type=F32).reshape(rows, D)
     first_pull = jax.vjp(layer_norm, value, table[0], table[1])[1]
     d_input, g_gain_one, g_shift_one = first_pull(d_first)
     return (g_qkv, g_out, g_bias_out, g_bias_q, g_bias_v, g_gain_one, g_shift_one), d_input

time: 535 us -> 529 us (0.989); the launches traced: 525 us -> 525 us
  other arithmetic: 42 us -> 49.1 us
    dot_general x0 -> x3, local copies, waits for them, and re-layouts: none -> 15.4 us  [the longest x2 11.4 us: attention_bwd(): jnp.einsum('tbhsd,kthd->bsk', d_qkv, w3, preferred_element_type=F32)]
    reshape x11 -> x3, local copies, waits for them, and re-layouts: 16.6 us -> 3.57 us  [the longest x2 2.46 us: attention_fwd(): first.reshape(nb, S, D)]
    unnamed x164 -> x188, local copies, waits for them, and re-layouts: 19.5 us -> 15.5 us
    dot_general x9 -> x10, matrix products: 29.4 us -> 25.5 us  [the longest x1 7.52 us: attention_bwd(): jnp.einsum('bhqd,bhkd->bhqk', d_att, val_part, preferred_element_type=F32)]
where the time goes in v9:
time: 529 us; the launch traced here: 525 us
  Pallas kernels  333 us (63%)
  local copies, waits for them, and re-layouts  74.5 us (14%)
  matrix products  66.2 us (13%)
  other arithmetic  49.1 us (9%)
    pallas_call x1, Pallas kernels, grad_reduce(): pl.pallas_call(functools.partial(ring_rs2_kernel, groups, x_pair), out_sh...  126 us
    pallas_call x1, Pallas kernels, ring_all_gather(): pl.pallas_call(functools.partial(ring_ag_kernel, groups), out_shape=shape...  101 us
    pallas_call x1, Pallas kernels, ffn_backward(): pl.pallas_call(functools.partial(ffn_bwd_kernel, micro), grid_spec=grid_s...  52.2 us
    pallas_call x1, Pallas kernels, ffn_forward(): pl.pallas_call(functools.partial(ffn_fwd_kernel, micro), grid_spec=grid_s...  39.4 us
    dot_general x2, matrix products, pick_rows(): both = jnp.einsum('mnr,mrd->mnd', onehot, split, preferred_element_type=F32)  15.6 us
    unnamed x188, local copies, waits for them, and re-layouts  15.5 us
    pallas_call x2, Pallas kernels, adamw_pass(): pl.pallas_call(functools.partial(adamw_kernel, rate), grid=(n,), in_specs...  13.9 us
    dot_general x2, local copies, waits for them, and re-layouts, attention_bwd(): jnp.einsum('tbhsd,kthd->bsk', d_qkv, w3, preferred_element_type=F32)  11.4 us

profile of v9, /device:TPU:1, one launch (start us, length us, event | category | flops | bytes accessed | tf_op | source)
XLA Modules:
  0.0 524.9 jit_solution(16143508632482500559)
XLA Ops:
  0.7 2.9 convert_element_type.110.refs_0_
  6.2 101.1 %shard_map.344 = (bf16[4,512,2048]{2,1,0:T(8,128)(2,1)}, bf16[4,2048,512]{2,1,0:T(8,128)(2,1)}, bf16[512,2560]{1,0:T(8,128)(2,1)}) custom-call(bf16[4,64,2048]{2,1,0:T(8,128)(2,1)} %convert_element_type.110.refs_0_, bf16[4,256,512]{2,1,0:T(8,128)(2,1)} %convert_element_type.111.refs_1_, bf16[64,2560]{1,0:T(8,128)(2,1)} %pad.14.refs_2_), custom_call_target="tpu_custom_call" | custom-call | bytes 19398656 | tf_op jit(solution)/shard_map/pallas_call | solution.py:271
  107.3 3.2 copy.321
  112.5 1.3 fusion.27
  113.8 2.2 reshape.302
  116.3 1.2 slice.172
  117.6 1.8 copy.320
  119.4 1.8 fusion.18
  122.9 1.3 fusion.7
  124.2 1.5 copy-done.2
  125.7 1.6 fusion.46
  129.0 2.1 fusion.136
  132.4 1.2 fusion.137
  135.7 2.3 reduce-window.6
  138.9 8.6 %fusion.9.x_ref = bf16[2,2048,512]{2,1,0:T(8,128)(2,1)} fusion(s32[2,788]{1,0:T(2,128)S(1)} %multiply_add_fusion.4, bf16[2,394,512]{2,1,0:T(8,128)(2,1)} %reshape.283), kind=kOutput, calls=%fused_computation.17 | convolution fusion | flops 3313664000 | bytes 5007520 | tf_op jit(solution)/shard_map/mnr,mnd->mrd/dot_general | solution.py:822
  148.8 1.3 copy.329
  150.2 2.0 reshape.308.b1_ref
  152.2 2.2 copy-done
  154.4 39.4 %shard_map.345 = (f32[2,2048,2048]{2,1,0:T(8,128)}, bf16[2,2048,2048]{2,1,0:T(8,128)(2,1)}, bf16[2,2048,1024]{2,1,0:T(8,128)(2,1)}) custom-call(s32[8]{0:T(128)S(1)} %reshape.282.counts, bf16[2,2048,512]{2,1,0:T(8,128)(2,1)S(1)} %copy-done, bf16[4,512,2048]{2,1,0:T(8,128)(2,1)} %get-tuple-element.42.w1_ref, f32[4,1,2048]{2,1,0:T(1,128)S(1)} %reshape.308.b1_ref, ...), custom_call_target="tpu_custom_call" | custom-call | flops 8589934592 | bytes 31457280 | tf_op jit(solution)/shard_map/pallas_call | solution.py:541
  193.8 9.3 %fusion.2 = f32[2,788,1024]{2,1,0:T(8,128)S(1)} fusion(bf16[2,2048,1024]{2,1,0:T(8,128)(2,1)} %get-tuple-element.44, s32[2,788]{1,0:T(2,128)S(1)} %copy-done.75), kind=kOutput, calls=%fused_computation.3 | convolution fusion | flops 6613450752 | bytes 14850208 | tf_op jit(solution)/shard_map/mnr,mrd->mnd/dot_general | solution.py:690
  203.9 2.1 fusion.132
  206.1 2.7 reshape.284
  208.8 2.7 reshape.285
  211.6 2.7 multiply_reduce_fusion.5
  214.5 2.5 reshape.287
  217.0 1.7 multiply_convert_fusion.4
  218.7 7.7 %fusion.10.dy_ref = bf16[2,2048,512]{2,1,0:T(8,128)(2,1)} fusion(s32[2,788]{1,0:T(2,128)S(1)} %copy-done.75, bf16[2,394,512]{2,1,0:T(8,128)(2,1)S(1)} %get-tuple-element.233, bf16[2,394,512]{2,1,0:T(8,128)(2,1)S(1)} %get-tuple-element.232), kind=kOutput, calls=%fused_computation.18 | convolution fusion | flops 3313664000 | bytes 5814432 | tf_op jit(solution)/shard_map/mnr,mnd->mrd/dot_general | solution.py:836
  226.4 52.2 %shard_map.346 = (bf16[2,2048,1024]{2,1,0:T(8,128)(2,1)}, bf16[4,512,2048]{2,1,0:T(8,128)(2,1)}, bf16[4,2048,512]{2,1,0:T(8,128)(2,1)}, f32[4,1,2048]{2,1,0:T(1,128)}, f32[4,1,512]{2,1,0:T(1,128)}) custom-call(s32[8]{0:T(128)} %copy-done.1, bf16[2,2048,512]{2,1,0:T(8,128)(2,1)} %fusion.10.dy_ref, bf16[2,2048,512]{2,1,0:T(8,128)(2,1)} %fusion.9.x_ref, ...), custom_call_target="tpu_custom_call" | custom-call | flops 17179869184 | bytes 100663296 | tf_op jit(solution)/shard_map/pallas_call | solution.py:617
  278.6 1.1 fusion.1
  279.7 6.2 %fusion.13 = f32[2,394,1024]{2,1,0:T(8,128)S(1)} fusion(bf16[2,2048,1024]{2,1,0:T(8,128)(2,1)} %get-tuple-element.47, bf16[2,788,2048]{2,1,0:T(8,128)(2,1)S(1)} %fusion.1), kind=kOutput, calls=%fused_computation.21 | convolution fusion | flops 3306725376 | bytes 18169856 | tf_op jit(solution)/shard_map/mnr,mrd->mnd/dot_general | solution.py:690
  285.9 1.5 slice_add_fusion.3
  287.5 2.8 reshape.288
  290.3 2.7 multiply_reduce_fusion.2
  293.0 1.7 fusion.131
  294.7 1.2 copy-done.6
  298.2 1.2 slice.181
  299.4 1.9 fusion.49
  301.3 7.5 %multiply_reduce_fusion = (f32[4,8,197]{2,1,0:T(8,128)S(1)}, f32[4,8,197,197]{2,3,1,0:T(8,128)}) fusion(f32[4,8,197,197]{2,3,1,0:T(8,128)} %copy-done.2, f32[4,8,197]{2,1,0:T(8,128)S(1)} %log_add_fusion, bf16[4,8,197,64]{2,3,0,1:T(8,128)(2,1)S(1)} %copy-done.21, bf16[4,8,197,64]{2,3,0,1:T(8,128)(2,1)S(1)} %fusion.49), kind=kOutput, calls=%fused_computation.6 | convolution fusion | flops 163922912 | bytes 11599360 | tf_op jit(solution)/shard_map/bhqd,bhkd->bhqk/dot_general | solution.py:746
  308.9 4.6 multiply_convert_fusion
  314.7 1.1 fusion.48
  315.8 1.3 fusion.43
  317.1 4.4 fusion.126
  321.5 4.5 copy.382
  326.0 6.9 %reshape.310 = bf16[788,64,8,3]{0,1,3,2:T(8,128)(2,1)} reshape(bf16[4,197,64,8,3]{1,0,2,4,3:T(4,128)(2,1)} %copy.382) | data formatting | bytes 4841472 | tf_op jit(solution)/shard_map/tbhsd,kthd->bsk/dot_general | solution.py:757
  332.9 3.6 bitcast_reduce_fusion
  336.6 1.4 fusion.28
  339.5 2.7 convolution_convert_fusion.1
  342.1 4.0 copy.342
  346.4 4.9 fusion.19
  351.4 1.1 reshape_squeeze.4
  353.0 3.8 concatenate.48
  356.8 1.7 pad.16.refs_2_
  358.5 126.2 %shard_map.347 = (f32[4,64,2048]{2,1,0:T(8,128)}, f32[4,256,512]{2,1,0:T(8,128)}, f32[64,2560]{1,0:T(8,128)}) custom-call(bf16[4,512,2048]{2,1,0:T(8,128)(2,1)} %get-tuple-element.48.refs_0_, bf16[4,2048,512]{2,1,0:T(8,128)(2,1)} %get-tuple-element.49.refs_1_, bf16[512,2560]{1,0:T(8,128)(2,1)} %pad.16.refs_2_), custom_call_target="tpu_custom_call" | custom-call | flops 9699328 | bytes 19398656 | tf_op jit(solution)/shard_map/pallas_call | solution.py:478
  486.1 1.5 fusion.102
  488.7 1.3 broadcast_multiply_fusion.4
  490.1 1.4 fusion.107
  492.3 1.4 broadcast_multiply_fusion.3
  493.9 1.4 fusion.110
  498.9 1.2 fusion.62
  500.1 6.9 %shard_map.348 = (f32[4,64,2048]{2,1,0:T(8,128)}, f32[2,4,64,2048]{3,2,1,0:T(8,128)}) custom-call(f32[4,64,2048]{2,1,0:T(8,128)} %w_ref.2, f32[2,4,64,2048]{3,2,1,0:T(8,128)} %m_ref.2, f32[4,64,2048]{2,1,0:T(8,128)} %get-tuple-element.302.g_ref), custom_call_target="tpu_custom_call" | custom-call | flops 6291456 | bytes 14680064 | tf_op jit(solution)/shard_map/pallas_call | solution.py:647
  507.1 7.0 %shard_map.349 = (f32[4,256,512]{2,1,0:T(8,128)}, f32[2,4,256,512]{3,2,1,0:T(8,128)}) custom-call(f32[4,256,512]{2,1,0:T(8,128)} %w_ref.3, f32[2,4,256,512]{3,2,1,0:T(8,128)} %m_ref.3, f32[4,256,512]{2,1,0:T(8,128)} %get-tuple-element.304.g_ref), custom_call_target="tpu_custom_call" | custom-call | flops 6291456 | bytes 14680064 | tf_op jit(solution)/shard_map/pallas_call | solution.py:647
  517.9 3.0 add_add_fusion.2
  521.0 1.3 copy.420
  523.3 1.3 copy.421
  (297 shorter events, 32.3 us)
Async XLA Ops:
  0.7 2.9 copy-start.15
  107.3 3.3 copy-start.3
  110.6 20.9 %copy-start.69 = (f32[1,512]{1,0:T(1,128)}, f32[1,512]{1,0:T(1,128)S(1)}, u32[]{:S(2)}) copy-start(f32[1,512]{1,0:T(1,128)S(1)} %get-tuple-element.246) | copy-start | bytes 6148
  110.8 5.5 %copy-start.10 = (bf16[512,2560]{1,0:T(8,128)(2,1)S(1)}, bf16[512,2560]{1,0:T(8,128)(2,1)}, u32[]{:S(2)}) copy-start(bf16[512,2560]{1,0:T(8,128)(2,1)} %get-tuple-element.41) | copy-start | bytes 7864324
  121.6 2.6 copy-start.20
  122.9 2.8 copy-start.2
  122.9 2.8 copy-start.39
  124.2 3.1 copy-start.41
  129.0 2.1 copy-start.31
  131.5 3.9 copy-start.60
  132.1 3.3 copy-start.76
  133.7 13.8 %copy-start.37 = (f32[788,4]{0,1:T(4,128)}, f32[788,4]{0,1:T(4,128)S(1)}, u32[]{:S(2)}) copy-start(f32[788,4]{0,1:T(4,128)S(1)} %get-tuple-element.269) | copy-start | bytes 37828
  138.9 8.6 %copy-start.74 = (s32[2,788]{1,0:T(2,128)}, s32[2,788]{1,0:T(2,128)S(1)}, u32[]{:S(2)}) copy-start(s32[2,788]{1,0:T(2,128)S(1)} %multiply_add_fusion.4) | copy-start | bytes 18916
  147.7 46.1 %copy-start.1 = (s32[8]{0:T(128)}, s32[8]{0:T(128)S(1)}, u32[]{:S(2)}) copy-start(s32[8]{0:T(128)S(1)} %reshape.282.counts) | copy-start | bytes 100
  152.2 2.2 copy-start
  154.4 39.5 %copy-start.75 = (s32[2,788]{1,0:T(2,128)S(1)}, s32[2,788]{1,0:T(2,128)}, u32[]{:S(2)}) copy-start(s32[2,788]{1,0:T(2,128)} %copy-done.74) | copy-start | bytes 18916
  211.5 2.7 copy-start.56
  211.5 2.7 copy-start.77
  211.5 2.8 copy-start.38
  211.5 2.8 copy-start.46
  211.6 2.8 copy-start.52
  287.4 2.8 copy-start.50
  287.5 2.8 copy-start.70
  290.2 2.7 copy-start.61
  290.2 2.7 copy-start.4
  290.2 2.7 copy-start.5
  293.0 2.9 copy-start.8
  294.7 3.5 copy-start.64
  298.2 3.1 copy-start.40
  298.2 3.1 copy-start.42
  298.2 3.1 copy-start.21
  301.3 7.6 %slice-start = ((s8[6553600]{0:T(1024)(128)(4,1)}), s8[4194304]{0:T(1024)(128)(4,1)S(1)}, s32[]{:S(2)}) async-start(s8[6553600]{0:T(1024)(128)(4,1)} %bitcast.158), calls=%async_computation | async-start | bytes 8388608
  301.3 7.5 %slice-start.1 = ((s8[6553600]{0:T(1024)(128)(4,1)}), s8[2359296]{0:T(1024)(128)(4,1)S(1)}, s32[]{:S(2)}) async-start(s8[6553600]{0:T(1024)(128)(4,1)} %bitcast.158), calls=%async_computation.1 | async-start | bytes 4718592
  308.9 4.6 copy-start.14
  326.0 6.9 %copy-start.26 = (bf16[512,1536]{0,1:T(8,128)(2,1)S(1)}, bf16[512,1536]{0,1:T(8,128)(2,1)}, u32[]{:S(2)}) copy-start(bf16[512,1536]{0,1:T(8,128)(2,1)} %copy-done.25) | copy-start | bytes 4718596
  326.0 6.9 %copy-start.48 = (f32[788]{0:T(1024)S(1)}, f32[788]{0:T(1024)}, u32[]{:S(2)}) copy-start(f32[788]{0:T(1024)} %copy-done.47) | copy-start | bytes 9460
  326.0 6.9 %copy-start.67 = (f32[1,512]{1,0:T(1,128)S(1)}, f32[1,512]{1,0:T(1,128)}, u32[]{:S(2)}) copy-start(f32[1,512]{1,0:T(1,128)} %copy-done.66) | copy-start | bytes 6148
  332.9 5.1 slice-start.2
  332.9 3.6 copy-start.59
  332.9 3.6 copy-start.54
  332.9 5.1 slice-start.3
  342.1 4.0 copy-start.18
  346.4 4.9 copy-start.73
  358.5 126.2 %copy-start.57 = (f32[2,11,64]{2,0,1:T(2,128)S(1)}, f32[2,11,64]{2,0,1:T(2,128)}, u32[]{:S(2)}) copy-start(f32[2,11,64]{2,0,1:T(2,128)} %param.33) | copy-start | bytes 16900
  358.5 126.4 %copy-start.72 = (f32[11,64]{1,0:T(8,128)S(1)}, f32[11,64]{1,0:T(8,128)}, u32[]{:S(2)}) copy-start(f32[11,64]{1,0:T(8,128)} %param.26) | copy-start | bytes 8452
  358.5 137.7 %copy-start.30 = (f32[2,64,512]{2,1,0:T(8,128)S(1)}, f32[2,64,512]{2,1,0:T(8,128)}, u32[]{:S(2)}) copy-start(f32[2,64,512]{2,1,0:T(8,128)} %param.28) | copy-start | bytes 786436
  358.5 137.7 %copy-start.36 = (f32[64,512]{1,0:T(8,128)S(1)}, f32[64,512]{1,0:T(8,128)}, u32[]{:S(2)}) copy-start(f32[64,512]{1,0:T(8,128)} %param.21) | copy-start | bytes 393220
  484.7 13.1 %copy-start.33 = (f32[64,2560]{1,0:T(8,128)S(1)}, f32[64,2560]{1,0:T(8,128)}, u32[]{:S(2)}) copy-start(f32[64,2560]{1,0:T(8,128)} %get-tuple-element.52) | copy-start | bytes 1966084
  485.9 12.0 %copy-start.24 = (f32[2,64,1536]{2,1,0:T(8,128)S(1)}, f32[2,64,1536]{2,1,0:T(8,128)}, u32[]{:S(2)}) copy-start(f32[2,64,1536]{2,1,0:T(8,128)} %param.27) | copy-start | bytes 2359300
  485.9 12.0 %copy-start.28 = (f32[64,1536]{1,0:T(8,128)S(1)}, f32[64,1536]{1,0:T(8,128)}, u32[]{:S(2)}) copy-start(f32[64,1536]{1,0:T(8,128)} %param.20) | copy-start | bytes 1179652
  488.7 10.2 %copy-start.81 = (f32[4,256]{1,0:T(4,128)}, f32[4,256]{1,0:T(4,128)S(1)}, u32[]{:S(2)}) copy-start(f32[4,256]{1,0:T(4,128)S(1)} %reshape.297) | copy-start | bytes 12292
  496.2 2.8 copy-start.34
  507.0 7.1 %copy-start.44 = (f32[64,4]{1,0:T(8,128)S(1)}, f32[64,4]{1,0:T(8,128)}, u32[]{:S(2)}) copy-start(f32[64,4]{1,0:T(8,128)} %get-tuple-element.240) | copy-start | bytes 3076
  507.0 7.2 %copy-start.79 = (f32[64,4]{0,1:T(4,128)S(1)}, f32[64,4]{0,1:T(4,128)}, u32[]{:S(2)}) copy-start(f32[64,4]{0,1:T(4,128)} %param.22) | copy-start | bytes 3076
  507.0 8.7 %copy-start.43 = (f32[64,4]{1,0:T(8,128)S(1)}, f32[64,4]{1,0:T(8,128)}, u32[]{:S(2)}) copy-start(f32[64,4]{1,0:T(8,128)} %get-tuple-element.241) | copy-start | bytes 3076
  507.0 10.9 %copy-start.80 = (f32[788]{0:T(1024)S(1)}, f32[788]{0:T(1024)}, u32[]{:S(2)}) copy-start(f32[788]{0:T(1024)} %get-tuple-element.202) | copy-start | bytes 9460
  507.0 10.9 %copy-start.7 = (f32[788,512]{1,0:T(8,128)S(1)}, f32[788,512]{1,0:T(8,128)}, u32[]{:S(2)}) copy-start(f32[788,512]{1,0:T(8,128)} %copy-done.6) | copy-start | bytes 4841476
  507.0 10.9 %copy-start.9 = (bf16[788,512]{1,0:T(8,128)(2,1)S(1)}, bf16[788,512]{1,0:T(8,128)(2,1)}, u32[]{:S(2)}) copy-start(bf16[788,512]{1,0:T(8,128)(2,1)} %param.18) | copy-start | bytes 2420740
  507.0 10.9 %copy-start.55 = (f32[788]{0:T(1024)S(1)}, f32[788]{0:T(1024)}, u32[]{:S(2)}) copy-start(f32[788]{0:T(1024)} %copy-done.53) | copy-start | bytes 9460
  507.0 10.9 %copy-start.63 = (f32[788]{0:T(1024)S(1)}, f32[788]{0:T(1024)}, u32[]{:S(2)}) copy-start(f32[788]{0:T(1024)} %copy-done.62) | copy-start | bytes 9460
  507.0 10.9 %copy-start.65 = (f32[788]{0:T(1024)S(1)}, f32[788]{0:T(1024)}, u32[]{:S(2)}) copy-start(f32[788]{0:T(1024)} %copy-done.64) | copy-start | bytes 9460
  507.1 10.9 %copy-start.68 = (f32[1,512]{1,0:T(1,128)S(1)}, f32[1,512]{1,0:T(1,128)}, u32[]{:S(2)}) copy-start(f32[1,512]{1,0:T(1,128)} %copy-done.66) | copy-start | bytes 6148
  517.9 3.1 copy-start.17
  521.0 2.3 copy-start.16
  (24 other events, 31.3 us)

commit v10 on v9

--- a/solution.py
+++ b/solution.py
@@ -722,9 +722,9 @@
     total = jnp.sum(expo, -1, keepdims=True)
     probs_att = (expo / total).astype(BF16)
     log_total = peak + jnp.log(total)
-    attended = jnp.einsum("bhqk,bhkd->bqhd", probs_att, val_part, preferred_element_type=F32)
-    attended = attended.reshape(rows, D).astype(BF16)
-    resid = value + (dot(attended, w_out) + table[4])
+    attended = jnp.einsum("bhqk,bhkd->bhqd", probs_att, val_part, preferred_element_type=F32).astype(BF16)
+    branch = jnp.einsum("bhqd,hdn->bqn", attended, w_out.reshape(HEADS, HEAD_DIM, D), preferred_element_type=F32)
+    resid = value + (branch.reshape(rows, D) + table[4])
     return first, qkv, log_total, attended, resid
 
 
@@ -734,7 +734,7 @@
     scale = HEAD_DIM ** (-0.5)
     d_branch = d_resid.astype(BF16)
     g_bias_out = jnp.sum(d_branch.astype(F32), 0)
-    g_out = lax.dot_general(attended, d_branch, (((0,), (0,)), ((), ())), preferred_element_type=F32)
+    g_out = jnp.einsum("bhqd,bqn->hdn", attended, d_branch.reshape(nb, S, D), preferred_element_type=F32).reshape(D, D)
     d_att = jnp.einsum(
         "bsn,hdn->bhsd", d_branch.reshape(nb, S, D), w_out.reshape(HEADS, HEAD_DIM, D), preferred_element_type=F32
     ).astype(BF16)

time: 529 us -> 534 us (level)
    unnamed x188 -> x186, local copies, waits for them, and re-layouts: 15.5 us -> 15.7 us
where the time goes in v10:
time: 534 us; the launch traced here: 532 us
  Pallas kernels  337 us (63%)
  local copies, waits for them, and re-layouts  74.9 us (14%)
  matrix products  68.6 us (13%)
  other arithmetic  49.1 us (9%)
    pallas_call x1, Pallas kernels, grad_reduce(): pl.pallas_call(functools.partial(ring_rs2_kernel, groups, x_pair), out_sh...  126 us
    pallas_call x1, Pallas kernels, ring_all_gather(): pl.pallas_call(functools.partial(ring_ag_kernel, groups), out_shape=shape...  101 us
    pallas_call x1, Pallas kernels, ffn_backward(): pl.pallas_call(functools.partial(ffn_bwd_kernel, micro), grid_spec=grid_s...  56.2 us
    pallas_call x1, Pallas kernels, ffn_forward(): pl.pallas_call(functools.partial(ffn_fwd_kernel, micro), grid_spec=grid_s...  40 us
    unnamed x186, local copies, waits for them, and re-layouts  15.7 us
    dot_general x2, matrix products, pick_rows(): both = jnp.einsum('mnr,mrd->mnd', onehot, split, preferred_element_type=F32)  15.6 us
    pallas_call x2, Pallas kernels, adamw_pass(): pl.pallas_call(functools.partial(adamw_kernel, rate), grid=(n,), in_specs...  13.9 us
    dot_general x2, local copies, waits for them, and re-layouts, attention_bwd(): jnp.einsum('tbhsd,kthd->bsk', d_qkv, w3, preferred_element_type=F32)  11.3 us

profile of v10, /device:TPU:1, one launch (start us, length us, event | category | flops | bytes accessed | tf_op | source)
XLA Modules:
  0.0 532.2 jit_solution(14200237766696474966)
XLA Ops:
  0.7 2.9 convert_element_type.112.refs_0_
  6.2 101.1 %shard_map.344 = (bf16[4,512,2048]{2,1,0:T(8,128)(2,1)}, bf16[4,2048,512]{2,1,0:T(8,128)(2,1)}, bf16[512,2560]{1,0:T(8,128)(2,1)}) custom-call(bf16[4,64,2048]{2,1,0:T(8,128)(2,1)} %convert_element_type.112.refs_0_, bf16[4,256,512]{2,1,0:T(8,128)(2,1)} %convert_element_type.113.refs_1_, bf16[64,2560]{1,0:T(8,128)(2,1)} %pad.14.refs_2_), custom_call_target="tpu_custom_call" | custom-call | bytes 19398656 | tf_op jit(solution)/shard_map/pallas_call | solution.py:271
  107.3 3.2 copy.330
  112.5 1.3 fusion.27
  113.8 2.2 reshape.306
  116.3 1.2 slice.172
  117.6 2.6 copy.329
  120.1 3.4 fusion.18
  125.3 1.3 fusion.7
  126.7 1.5 copy-done.2
  128.2 1.4 fusion.39
  130.5 1.8 copy.394
  132.3 3.1 reshape.314
  135.5 2.1 fusion.135
  138.9 1.2 fusion.136
  142.1 2.3 reduce-window.6
  145.4 8.6 %fusion.9.x_ref = bf16[2,2048,512]{2,1,0:T(8,128)(2,1)} fusion(s32[2,788]{1,0:T(2,128)S(1)} %multiply_add_fusion.4, bf16[2,394,512]{2,1,0:T(8,128)(2,1)} %reshape.288), kind=kOutput, calls=%fused_computation.17 | convolution fusion | flops 3313664000 | bytes 5007520 | tf_op jit(solution)/shard_map/mnr,mnd->mrd/dot_general | solution.py:822
  155.3 1.3 copy.339
  156.6 2.0 reshape.315.b1_ref
  158.6 2.2 copy-done
  160.8 40.0 %shard_map.345 = (f32[2,2048,2048]{2,1,0:T(8,128)}, bf16[2,2048,2048]{2,1,0:T(8,128)(2,1)}, bf16[2,2048,1024]{2,1,0:T(8,128)(2,1)}) custom-call(s32[8]{0:T(128)S(1)} %reshape.287.counts, bf16[2,2048,512]{2,1,0:T(8,128)(2,1)S(1)} %copy-done, bf16[4,512,2048]{2,1,0:T(8,128)(2,1)} %get-tuple-element.42.w1_ref, f32[4,1,2048]{2,1,0:T(1,128)S(1)} %reshape.315.b1_ref, ...), custom_call_target="tpu_custom_call" | custom-call | flops 8589934592 | bytes 31457280 | tf_op jit(solution)/shard_map/pallas_call | solution.py:541
  200.8 9.3 %fusion.2 = f32[2,788,1024]{2,1,0:T(8,128)S(1)} fusion(bf16[2,2048,1024]{2,1,0:T(8,128)(2,1)} %get-tuple-element.44, s32[2,788]{1,0:T(2,128)S(1)} %copy-done.74), kind=kOutput, calls=%fused_computation.3 | convolution fusion | flops 6613450752 | bytes 14850208 | tf_op jit(solution)/shard_map/mnr,mrd->mnd/dot_general | solution.py:690
  211.0 2.1 fusion.131
  213.1 2.7 reshape.289
  215.8 2.7 reshape.290
  218.6 2.7 multiply_reduce_fusion.5
  221.5 2.5 reshape.292
  224.0 1.7 multiply_convert_fusion.4
  225.7 7.7 %fusion.10.dy_ref = bf16[2,2048,512]{2,1,0:T(8,128)(2,1)} fusion(s32[2,788]{1,0:T(2,128)S(1)} %copy-done.74, bf16[2,394,512]{2,1,0:T(8,128)(2,1)S(1)} %get-tuple-element.233, bf16[2,394,512]{2,1,0:T(8,128)(2,1)S(1)} %get-tuple-element.232), kind=kOutput, calls=%fused_computation.18 | convolution fusion | flops 3313664000 | bytes 5814432 | tf_op jit(solution)/shard_map/mnr,mnd->mrd/dot_general | solution.py:836
  233.4 56.2 %shard_map.346 = (bf16[2,2048,1024]{2,1,0:T(8,128)(2,1)}, bf16[4,512,2048]{2,1,0:T(8,128)(2,1)}, bf16[4,2048,512]{2,1,0:T(8,128)(2,1)}, f32[4,1,2048]{2,1,0:T(1,128)}, f32[4,1,512]{2,1,0:T(1,128)}) custom-call(s32[8]{0:T(128)} %copy-done.1, bf16[2,2048,512]{2,1,0:T(8,128)(2,1)} %fusion.10.dy_ref, bf16[2,2048,512]{2,1,0:T(8,128)(2,1)} %fusion.9.x_ref, ...), custom_call_target="tpu_custom_call" | custom-call | flops 17179869184 | bytes 100663296 | tf_op jit(solution)/shard_map/pallas_call | solution.py:617
  290.7 6.2 %fusion.13 = f32[2,394,1024]{2,1,0:T(8,128)S(1)} fusion(bf16[2,2048,1024]{2,1,0:T(8,128)(2,1)} %get-tuple-element.47, bf16[2,788,2048]{2,1,0:T(8,128)(2,1)S(1)} %fusion.1), kind=kOutput, calls=%fused_computation.21 | convolution fusion | flops 3306725376 | bytes 18169856 | tf_op jit(solution)/shard_map/mnr,mrd->mnd/dot_general | solution.py:690
  296.9 1.5 slice_add_fusion.3
  298.5 2.8 reshape.293
  301.3 2.7 multiply_reduce_fusion.2
  304.0 1.7 fusion.130
  305.7 1.2 copy-done.6
  307.5 1.9 fusion.48
  309.4 7.8 %multiply_reduce_fusion = (f32[4,8,197]{2,1,0:T(8,128)S(1)}, f32[4,8,197,197]{2,3,1,0:T(8,128)}) fusion(f32[4,8,197,197]{2,3,1,0:T(8,128)} %copy-done.2, f32[4,8,197]{2,1,0:T(8,128)S(1)} %log_add_fusion, bf16[4,8,197,64]{2,3,0,1:T(8,128)(2,1)S(1)} %copy-done.24, bf16[4,8,197,64]{2,3,0,1:T(8,128)(2,1)S(1)} %fusion.48), kind=kOutput, calls=%fused_computation.6 | convolution fusion | flops 163922912 | bytes 11599360 | tf_op jit(solution)/shard_map/bhqd,bhkd->bhqk/dot_general | solution.py:746
  317.2 4.6 multiply_convert_fusion
  323.0 1.1 fusion.47
  324.3 1.3 fusion.43
  325.6 4.4 fusion.125
  329.9 4.5 copy.395
  334.4 6.8 %reshape.317 = bf16[788,64,8,3]{0,1,3,2:T(8,128)(2,1)} reshape(bf16[4,197,64,8,3]{1,0,2,4,3:T(4,128)(2,1)} %copy.395) | data formatting | bytes 4841472 | tf_op jit(solution)/shard_map/tbhsd,kthd->bsk/dot_general | solution.py:757
  341.2 4.0 bitcast_reduce_fusion
  345.3 1.4 fusion.28
  348.5 2.9 fusion.49
  351.4 2.1 copy.352
  353.7 4.9 fusion.19
  358.7 1.1 reshape_squeeze.4
  360.2 3.8 concatenate.48
  364.1 1.7 pad.16.refs_2_
  365.8 126.2 %shard_map.347 = (f32[4,64,2048]{2,1,0:T(8,128)}, f32[4,256,512]{2,1,0:T(8,128)}, f32[64,2560]{1,0:T(8,128)}) custom-call(bf16[4,512,2048]{2,1,0:T(8,128)(2,1)} %get-tuple-element.48.refs_0_, bf16[4,2048,512]{2,1,0:T(8,128)(2,1)} %get-tuple-element.49.refs_1_, bf16[512,2560]{1,0:T(8,128)(2,1)} %pad.16.refs_2_), custom_call_target="tpu_custom_call" | custom-call | flops 9699328 | bytes 19398656 | tf_op jit(solution)/shard_map/pallas_call | solution.py:478
  493.3 1.5 fusion.102
  496.0 1.3 broadcast_multiply_fusion.4
  497.3 1.4 fusion.107
  499.6 1.4 broadcast_multiply_fusion.3
  501.1 1.4 fusion.110
  506.2 1.2 fusion.62
  507.4 6.9 %shard_map.348 = (f32[4,64,2048]{2,1,0:T(8,128)}, f32[2,4,64,2048]{3,2,1,0:T(8,128)}) custom-call(f32[4,64,2048]{2,1,0:T(8,128)} %w_ref.2, f32[2,4,64,2048]{3,2,1,0:T(8,128)} %m_ref.2, f32[4,64,2048]{2,1,0:T(8,128)} %get-tuple-element.302.g_ref), custom_call_target="tpu_custom_call" | custom-call | flops 6291456 | bytes 14680064 | tf_op jit(solution)/shard_map/pallas_call | solution.py:647
  514.3 7.0 %shard_map.349 = (f32[4,256,512]{2,1,0:T(8,128)}, f32[2,4,256,512]{3,2,1,0:T(8,128)}) custom-call(f32[4,256,512]{2,1,0:T(8,128)} %w_ref.3, f32[2,4,256,512]{3,2,1,0:T(8,128)} %m_ref.3, f32[4,256,512]{2,1,0:T(8,128)} %get-tuple-element.304.g_ref), custom_call_target="tpu_custom_call" | custom-call | flops 6291456 | bytes 14680064 | tf_op jit(solution)/shard_map/pallas_call | solution.py:647
  525.2 3.0 add_add_fusion.2
  528.2 1.3 copy.435
  530.6 1.3 copy.436
  (296 shorter events, 31.4 us)
Async XLA Ops:
  0.7 2.9 copy-start.16
  107.3 3.3 copy-start.3
  110.6 27.4 %copy-start.68 = (f32[1,512]{1,0:T(1,128)}, f32[1,512]{1,0:T(1,128)S(1)}, u32[]{:S(2)}) copy-start(f32[1,512]{1,0:T(1,128)S(1)} %get-tuple-element.246) | copy-start | bytes 6148
  110.8 5.5 %copy-start.11 = (bf16[512,2560]{1,0:T(8,128)(2,1)S(1)}, bf16[512,2560]{1,0:T(8,128)(2,1)}, u32[]{:S(2)}) copy-start(bf16[512,2560]{1,0:T(8,128)(2,1)} %get-tuple-element.41) | copy-start | bytes 7864324
  124.0 2.6 copy-start.23
  125.3 2.8 copy-start.2
  125.3 2.8 copy-start.38
  126.6 2.9 copy-start.40
  135.4 2.1 copy-start.32
  137.9 3.9 copy-start.59
  138.6 3.3 copy-start.75
  140.1 13.8 %copy-start.36 = (f32[788,4]{0,1:T(4,128)}, f32[788,4]{0,1:T(4,128)S(1)}, u32[]{:S(2)}) copy-start(f32[788,4]{0,1:T(4,128)S(1)} %get-tuple-element.269) | copy-start | bytes 37828
  145.4 8.6 %copy-start.73 = (s32[2,788]{1,0:T(2,128)}, s32[2,788]{1,0:T(2,128)S(1)}, u32[]{:S(2)}) copy-start(s32[2,788]{1,0:T(2,128)S(1)} %multiply_add_fusion.4) | copy-start | bytes 18916
  154.1 46.7 %copy-start.1 = (s32[8]{0:T(128)}, s32[8]{0:T(128)S(1)}, u32[]{:S(2)}) copy-start(s32[8]{0:T(128)S(1)} %reshape.287.counts) | copy-start | bytes 100
  158.6 2.2 copy-start
  160.8 40.0 %copy-start.74 = (s32[2,788]{1,0:T(2,128)S(1)}, s32[2,788]{1,0:T(2,128)}, u32[]{:S(2)}) copy-start(s32[2,788]{1,0:T(2,128)} %copy-done.73) | copy-start | bytes 18916
  218.6 2.7 copy-start.55
  218.6 2.7 copy-start.76
  218.6 2.8 copy-start.37
  218.6 2.8 copy-start.45
  218.6 2.8 copy-start.51
  298.5 2.8 copy-start.49
  298.5 2.8 copy-start.69
  301.3 2.7 copy-start.60
  301.3 2.7 copy-start.4
  301.3 2.7 copy-start.5
  304.0 2.9 copy-start.8
  307.2 2.1 copy-start.39
  307.2 2.1 copy-start.41
  307.5 1.9 copy-start.24
  309.4 7.8 %copy-start.21 = (bf16[4,8,197,64]{2,3,0,1:T(8,128)(2,1)}, bf16[4,8,197,64]{2,3,0,1:T(8,128)(2,1)S(1)}, u32[]{:S(2)}) copy-start(bf16[4,8,197,64]{2,3,0,1:T(8,128)(2,1)S(1)} %fusion.48) | copy-start | bytes 2420740
  309.4 7.8 %slice-start = ((s8[6553600]{0:T(1024)(128)(4,1)}), s8[4194304]{0:T(1024)(128)(4,1)S(1)}, s32[]{:S(2)}) async-start(s8[6553600]{0:T(1024)(128)(4,1)} %bitcast.169), calls=%async_computation | async-start | bytes 8388608
  309.4 7.8 %slice-start.1 = ((s8[6553600]{0:T(1024)(128)(4,1)}), s8[2359296]{0:T(1024)(128)(4,1)S(1)}, s32[]{:S(2)}) async-start(s8[6553600]{0:T(1024)(128)(4,1)} %bitcast.169), calls=%async_computation.1 | async-start | bytes 4718592
  317.2 4.6 copy-start.15
  334.4 6.8 %copy-start.47 = (f32[788]{0:T(1024)S(1)}, f32[788]{0:T(1024)}, u32[]{:S(2)}) copy-start(f32[788]{0:T(1024)} %copy-done.46) | copy-start | bytes 9460
  334.4 6.8 %copy-start.66 = (f32[1,512]{1,0:T(1,128)S(1)}, f32[1,512]{1,0:T(1,128)}, u32[]{:S(2)}) copy-start(f32[1,512]{1,0:T(1,128)} %copy-done.65) | copy-start | bytes 6148
  341.2 5.6 %slice-start.2 = ((s8[6291456]{0:T(1024)(128)(4,1)}), s8[4194304]{0:T(1024)(128)(4,1)S(1)}, s32[]{:S(2)}) async-start(s8[6291456]{0:T(1024)(128)(4,1)} %bitcast.171), calls=%async_computation.2 | async-start | bytes 8388608
  341.2 4.1 copy-start.58
  341.2 4.1 copy-start.53
  341.2 5.5 %slice-start.3 = ((s8[6291456]{0:T(1024)(128)(4,1)}), s8[2097152]{0:T(1024)(128)(4,1)S(1)}, s32[]{:S(2)}) async-start(s8[6291456]{0:T(1024)(128)(4,1)} %bitcast.171), calls=%async_computation.3 | async-start | bytes 4194304
  348.4 2.9 copy-start.10
  351.4 2.1 copy-start.19
  353.7 4.9 copy-start.72
  365.8 126.2 %copy-start.56 = (f32[2,11,64]{2,0,1:T(2,128)S(1)}, f32[2,11,64]{2,0,1:T(2,128)}, u32[]{:S(2)}) copy-start(f32[2,11,64]{2,0,1:T(2,128)} %param.33) | copy-start | bytes 16900
  365.8 126.4 %copy-start.71 = (f32[11,64]{1,0:T(8,128)S(1)}, f32[11,64]{1,0:T(8,128)}, u32[]{:S(2)}) copy-start(f32[11,64]{1,0:T(8,128)} %param.26) | copy-start | bytes 8452
  365.8 137.7 %copy-start.30 = (f32[2,64,512]{2,1,0:T(8,128)S(1)}, f32[2,64,512]{2,1,0:T(8,128)}, u32[]{:S(2)}) copy-start(f32[2,64,512]{2,1,0:T(8,128)} %param.28) | copy-start | bytes 786436
  365.8 137.7 %copy-start.35 = (f32[64,512]{1,0:T(8,128)S(1)}, f32[64,512]{1,0:T(8,128)}, u32[]{:S(2)}) copy-start(f32[64,512]{1,0:T(8,128)} %param.21) | copy-start | bytes 393220
  492.0 13.1 %copy-start.31 = (f32[64,2560]{1,0:T(8,128)S(1)}, f32[64,2560]{1,0:T(8,128)}, u32[]{:S(2)}) copy-start(f32[64,2560]{1,0:T(8,128)} %get-tuple-element.52) | copy-start | bytes 1966084
  493.1 12.0 %copy-start.25 = (f32[2,64,1536]{2,1,0:T(8,128)S(1)}, f32[2,64,1536]{2,1,0:T(8,128)}, u32[]{:S(2)}) copy-start(f32[2,64,1536]{2,1,0:T(8,128)} %param.27) | copy-start | bytes 2359300
  493.2 12.0 %copy-start.27 = (f32[64,1536]{1,0:T(8,128)S(1)}, f32[64,1536]{1,0:T(8,128)}, u32[]{:S(2)}) copy-start(f32[64,1536]{1,0:T(8,128)} %param.20) | copy-start | bytes 1179652
  496.0 10.2 %copy-start.80 = (f32[4,256]{1,0:T(4,128)}, f32[4,256]{1,0:T(4,128)S(1)}, u32[]{:S(2)}) copy-start(f32[4,256]{1,0:T(4,128)S(1)} %reshape.301) | copy-start | bytes 12292
  503.4 2.8 copy-start.33
  514.2 7.1 %copy-start.43 = (f32[64,4]{1,0:T(8,128)S(1)}, f32[64,4]{1,0:T(8,128)}, u32[]{:S(2)}) copy-start(f32[64,4]{1,0:T(8,128)} %get-tuple-element.240) | copy-start | bytes 3076
  514.2 7.2 %copy-start.78 = (f32[64,4]{0,1:T(4,128)S(1)}, f32[64,4]{0,1:T(4,128)}, u32[]{:S(2)}) copy-start(f32[64,4]{0,1:T(4,128)} %param.22) | copy-start | bytes 3076
  514.2 8.7 %copy-start.42 = (f32[64,4]{1,0:T(8,128)S(1)}, f32[64,4]{1,0:T(8,128)}, u32[]{:S(2)}) copy-start(f32[64,4]{1,0:T(8,128)} %get-tuple-element.241) | copy-start | bytes 3076
  514.2 10.9 %copy-start.79 = (f32[788]{0:T(1024)S(1)}, f32[788]{0:T(1024)}, u32[]{:S(2)}) copy-start(f32[788]{0:T(1024)} %get-tuple-element.202) | copy-start | bytes 9460
  514.3 10.9 %copy-start.7 = (f32[788,512]{1,0:T(8,128)S(1)}, f32[788,512]{1,0:T(8,128)}, u32[]{:S(2)}) copy-start(f32[788,512]{1,0:T(8,128)} %copy-done.6) | copy-start | bytes 4841476
  514.3 10.9 %copy-start.9 = (bf16[788,512]{1,0:T(8,128)(2,1)S(1)}, bf16[788,512]{1,0:T(8,128)(2,1)}, u32[]{:S(2)}) copy-start(bf16[788,512]{1,0:T(8,128)(2,1)} %param.18) | copy-start | bytes 2420740
  514.3 10.9 %copy-start.54 = (f32[788]{0:T(1024)S(1)}, f32[788]{0:T(1024)}, u32[]{:S(2)}) copy-start(f32[788]{0:T(1024)} %copy-done.52) | copy-start | bytes 9460
  514.3 10.9 %copy-start.62 = (f32[788]{0:T(1024)S(1)}, f32[788]{0:T(1024)}, u32[]{:S(2)}) copy-start(f32[788]{0:T(1024)} %copy-done.61) | copy-start | bytes 9460
  514.3 10.9 %copy-start.64 = (f32[788]{0:T(1024)S(1)}, f32[788]{0:T(1024)}, u32[]{:S(2)}) copy-start(f32[788]{0:T(1024)} %copy-done.63) | copy-start | bytes 9460
  514.3 10.9 %copy-start.67 = (f32[1,512]{1,0:T(1,128)S(1)}, f32[1,512]{1,0:T(1,128)}, u32[]{:S(2)}) copy-start(f32[1,512]{1,0:T(1,128)} %copy-done.65) | copy-start | bytes 6148
  525.2 3.1 copy-start.18
  528.2 2.3 copy-start.17
  (23 other events, 29.0 us)

commit v11 on v9

--- a/solution.py
+++ b/solution.py
@@ -415,7 +415,7 @@
                 copies.append(c)
         return copies
 
-    wave_a, wave_b = (0, 1, 2, 4), (3,)
+    wave_a, wave_b = (0, 1, 2, 3), (4,)
     ring_wave(wave_a)
     if x_pair:
         xa = x_start(wave_a)

time: 529 us -> 529 us (level)
  no operation moved by 1% of the time
where the time goes in v11:
time: 529 us; the launch traced here: 525 us
  Pallas kernels  333 us (63%)
  local copies, waits for them, and re-layouts  74.5 us (14%)
  matrix products  66.2 us (13%)
  other arithmetic  49.1 us (9%)
    pallas_call x1, Pallas kernels, grad_reduce(): pl.pallas_call(functools.partial(ring_rs2_kernel, groups, x_pair), out_sh...  126 us
    pallas_call x1, Pallas kernels, ring_all_gather(): pl.pallas_call(functools.partial(ring_ag_kernel, groups), out_shape=shape...  101 us
    pallas_call x1, Pallas kernels, ffn_backward(): pl.pallas_call(functools.partial(ffn_bwd_kernel, micro), grid_spec=grid_s...  52.2 us
    pallas_call x1, Pallas kernels, ffn_forward(): pl.pallas_call(functools.partial(ffn_fwd_kernel, micro), grid_spec=grid_s...  39.4 us
    dot_general x2, matrix products, pick_rows(): both = jnp.einsum('mnr,mrd->mnd', onehot, split, preferred_element_type=F32)  15.6 us
    unnamed x188, local copies, waits for them, and re-layouts  15.5 us
    pallas_call x2, Pallas kernels, adamw_pass(): pl.pallas_call(functools.partial(adamw_kernel, rate), grid=(n,), in_specs...  13.9 us
    dot_general x2, local copies, waits for them, and re-layouts, attention_bwd(): jnp.einsum('tbhsd,kthd->bsk', d_qkv, w3, preferred_element_type=F32)  11.4 us

profile of v11, /device:TPU:1, one launch (start us, length us, event | category | flops | bytes accessed | tf_op | source)
XLA Modules:
  0.0 525.1 jit_solution(4028348360379107290)
XLA Ops:
  0.7 2.9 convert_element_type.110.refs_0_
  6.2 101.1 %shard_map.344 = (bf16[4,512,2048]{2,1,0:T(8,128)(2,1)}, bf16[4,2048,512]{2,1,0:T(8,128)(2,1)}, bf16[512,2560]{1,0:T(8,128)(2,1)}) custom-call(bf16[4,64,2048]{2,1,0:T(8,128)(2,1)} %convert_element_type.110.refs_0_, bf16[4,256,512]{2,1,0:T(8,128)(2,1)} %convert_element_type.111.refs_1_, bf16[64,2560]{1,0:T(8,128)(2,1)} %pad.14.refs_2_), custom_call_target="tpu_custom_call" | custom-call | bytes 19398656 | tf_op jit(solution)/shard_map/pallas_call | solution.py:271
  107.3 3.2 copy.321
  112.5 1.3 fusion.27
  113.8 2.2 reshape.302
  116.3 1.2 slice.172
  117.6 1.8 copy.320
  119.4 1.8 fusion.18
  122.9 1.3 fusion.7
  124.2 1.5 copy-done.2
  125.7 1.6 fusion.46
  129.0 2.1 fusion.136
  132.4 1.2 fusion.137
  135.7 2.3 reduce-window.6
  138.9 8.6 %fusion.9.x_ref = bf16[2,2048,512]{2,1,0:T(8,128)(2,1)} fusion(s32[2,788]{1,0:T(2,128)S(1)} %multiply_add_fusion.4, bf16[2,394,512]{2,1,0:T(8,128)(2,1)} %reshape.283), kind=kOutput, calls=%fused_computation.17 | convolution fusion | flops 3313664000 | bytes 5007520 | tf_op jit(solution)/shard_map/mnr,mnd->mrd/dot_general | solution.py:822
  148.8 1.3 copy.329
  150.2 2.0 reshape.308.b1_ref
  152.2 2.2 copy-done
  154.4 39.4 %shard_map.345 = (f32[2,2048,2048]{2,1,0:T(8,128)}, bf16[2,2048,2048]{2,1,0:T(8,128)(2,1)}, bf16[2,2048,1024]{2,1,0:T(8,128)(2,1)}) custom-call(s32[8]{0:T(128)S(1)} %reshape.282.counts, bf16[2,2048,512]{2,1,0:T(8,128)(2,1)S(1)} %copy-done, bf16[4,512,2048]{2,1,0:T(8,128)(2,1)} %get-tuple-element.42.w1_ref, f32[4,1,2048]{2,1,0:T(1,128)S(1)} %reshape.308.b1_ref, ...), custom_call_target="tpu_custom_call" | custom-call | flops 8589934592 | bytes 31457280 | tf_op jit(solution)/shard_map/pallas_call | solution.py:541
  193.8 9.3 %fusion.2 = f32[2,788,1024]{2,1,0:T(8,128)S(1)} fusion(bf16[2,2048,1024]{2,1,0:T(8,128)(2,1)} %get-tuple-element.44, s32[2,788]{1,0:T(2,128)S(1)} %copy-done.75), kind=kOutput, calls=%fused_computation.3 | convolution fusion | flops 6613450752 | bytes 14850208 | tf_op jit(solution)/shard_map/mnr,mrd->mnd/dot_general | solution.py:690
  203.9 2.1 fusion.132
  206.0 2.7 reshape.284
  208.8 2.7 reshape.285
  211.6 2.7 multiply_reduce_fusion.5
  214.5 2.5 reshape.287
  217.0 1.7 multiply_convert_fusion.4
  218.7 7.7 %fusion.10.dy_ref = bf16[2,2048,512]{2,1,0:T(8,128)(2,1)} fusion(s32[2,788]{1,0:T(2,128)S(1)} %copy-done.75, bf16[2,394,512]{2,1,0:T(8,128)(2,1)S(1)} %get-tuple-element.233, bf16[2,394,512]{2,1,0:T(8,128)(2,1)S(1)} %get-tuple-element.232), kind=kOutput, calls=%fused_computation.18 | convolution fusion | flops 3313664000 | bytes 5814432 | tf_op jit(solution)/shard_map/mnr,mnd->mrd/dot_general | solution.py:836
  226.4 52.2 %shard_map.346 = (bf16[2,2048,1024]{2,1,0:T(8,128)(2,1)}, bf16[4,512,2048]{2,1,0:T(8,128)(2,1)}, bf16[4,2048,512]{2,1,0:T(8,128)(2,1)}, f32[4,1,2048]{2,1,0:T(1,128)}, f32[4,1,512]{2,1,0:T(1,128)}) custom-call(s32[8]{0:T(128)} %copy-done.1, bf16[2,2048,512]{2,1,0:T(8,128)(2,1)} %fusion.10.dy_ref, bf16[2,2048,512]{2,1,0:T(8,128)(2,1)} %fusion.9.x_ref, ...), custom_call_target="tpu_custom_call" | custom-call | flops 17179869184 | bytes 100663296 | tf_op jit(solution)/shard_map/pallas_call | solution.py:617
  278.6 1.1 fusion.1
  279.7 6.2 %fusion.13 = f32[2,394,1024]{2,1,0:T(8,128)S(1)} fusion(bf16[2,2048,1024]{2,1,0:T(8,128)(2,1)} %get-tuple-element.47, bf16[2,788,2048]{2,1,0:T(8,128)(2,1)S(1)} %fusion.1), kind=kOutput, calls=%fused_computation.21 | convolution fusion | flops 3306725376 | bytes 18169856 | tf_op jit(solution)/shard_map/mnr,mrd->mnd/dot_general | solution.py:690
  285.9 1.5 slice_add_fusion.3
  287.5 2.8 reshape.288
  290.3 2.7 multiply_reduce_fusion.2
  293.0 1.7 fusion.131
  294.7 1.2 copy-done.6
  298.2 1.2 slice.181
  299.4 1.9 fusion.49
  301.3 7.5 %multiply_reduce_fusion = (f32[4,8,197]{2,1,0:T(8,128)S(1)}, f32[4,8,197,197]{2,3,1,0:T(8,128)}) fusion(f32[4,8,197,197]{2,3,1,0:T(8,128)} %copy-done.2, f32[4,8,197]{2,1,0:T(8,128)S(1)} %log_add_fusion, bf16[4,8,197,64]{2,3,0,1:T(8,128)(2,1)S(1)} %copy-done.21, bf16[4,8,197,64]{2,3,0,1:T(8,128)(2,1)S(1)} %fusion.49), kind=kOutput, calls=%fused_computation.6 | convolution fusion | flops 163922912 | bytes 11599360 | tf_op jit(solution)/shard_map/bhqd,bhkd->bhqk/dot_general | solution.py:746
  308.9 4.6 multiply_convert_fusion
  314.7 1.1 fusion.48
  315.8 1.3 fusion.43
  317.1 4.4 fusion.126
  321.5 4.5 copy.382
  326.0 6.9 %reshape.310 = bf16[788,64,8,3]{0,1,3,2:T(8,128)(2,1)} reshape(bf16[4,197,64,8,3]{1,0,2,4,3:T(4,128)(2,1)} %copy.382) | data formatting | bytes 4841472 | tf_op jit(solution)/shard_map/tbhsd,kthd->bsk/dot_general | solution.py:757
  332.9 3.6 bitcast_reduce_fusion
  336.6 1.4 fusion.28
  339.5 2.7 convolution_convert_fusion.1
  342.1 4.0 copy.342
  346.4 4.9 fusion.19
  351.4 1.1 reshape_squeeze.4
  353.0 3.8 concatenate.48
  356.8 1.7 pad.16.refs_2_
  358.5 126.4 %shard_map.347 = (f32[4,64,2048]{2,1,0:T(8,128)}, f32[4,256,512]{2,1,0:T(8,128)}, f32[64,2560]{1,0:T(8,128)}) custom-call(bf16[4,512,2048]{2,1,0:T(8,128)(2,1)} %get-tuple-element.48.refs_0_, bf16[4,2048,512]{2,1,0:T(8,128)(2,1)} %get-tuple-element.49.refs_1_, bf16[512,2560]{1,0:T(8,128)(2,1)} %pad.16.refs_2_), custom_call_target="tpu_custom_call" | custom-call | flops 9699328 | bytes 19398656 | tf_op jit(solution)/shard_map/pallas_call | solution.py:478
  486.3 1.5 fusion.102
  488.9 1.3 broadcast_multiply_fusion.4
  490.2 1.4 fusion.107
  492.5 1.4 broadcast_multiply_fusion.3
  494.1 1.4 fusion.110
  499.1 1.2 fusion.62
  500.3 6.9 %shard_map.348 = (f32[4,64,2048]{2,1,0:T(8,128)}, f32[2,4,64,2048]{3,2,1,0:T(8,128)}) custom-call(f32[4,64,2048]{2,1,0:T(8,128)} %w_ref.2, f32[2,4,64,2048]{3,2,1,0:T(8,128)} %m_ref.2, f32[4,64,2048]{2,1,0:T(8,128)} %get-tuple-element.302.g_ref), custom_call_target="tpu_custom_call" | custom-call | flops 6291456 | bytes 14680064 | tf_op jit(solution)/shard_map/pallas_call | solution.py:647
  507.2 7.0 %shard_map.349 = (f32[4,256,512]{2,1,0:T(8,128)}, f32[2,4,256,512]{3,2,1,0:T(8,128)}) custom-call(f32[4,256,512]{2,1,0:T(8,128)} %w_ref.3, f32[2,4,256,512]{3,2,1,0:T(8,128)} %m_ref.3, f32[4,256,512]{2,1,0:T(8,128)} %get-tuple-element.304.g_ref), custom_call_target="tpu_custom_call" | custom-call | flops 6291456 | bytes 14680064 | tf_op jit(solution)/shard_map/pallas_call | solution.py:647
  518.1 3.0 add_add_fusion.2
  521.2 1.3 copy.420
  523.5 1.3 copy.421
  (297 shorter events, 32.3 us)
Async XLA Ops:
  0.7 2.9 copy-start.15
  107.3 3.3 copy-start.3
  110.6 20.9 %copy-start.69 = (f32[1,512]{1,0:T(1,128)}, f32[1,512]{1,0:T(1,128)S(1)}, u32[]{:S(2)}) copy-start(f32[1,512]{1,0:T(1,128)S(1)} %get-tuple-element.246) | copy-start | bytes 6148
  110.8 5.5 %copy-start.10 = (bf16[512,2560]{1,0:T(8,128)(2,1)S(1)}, bf16[512,2560]{1,0:T(8,128)(2,1)}, u32[]{:S(2)}) copy-start(bf16[512,2560]{1,0:T(8,128)(2,1)} %get-tuple-element.41) | copy-start | bytes 7864324
  121.6 2.6 copy-start.20
  122.9 2.8 copy-start.2
  122.9 2.8 copy-start.39
  124.2 3.1 copy-start.41
  129.0 2.1 copy-start.31
  131.5 3.9 copy-start.60
  132.1 3.3 copy-start.76
  133.7 13.8 %copy-start.37 = (f32[788,4]{0,1:T(4,128)}, f32[788,4]{0,1:T(4,128)S(1)}, u32[]{:S(2)}) copy-start(f32[788,4]{0,1:T(4,128)S(1)} %get-tuple-element.269) | copy-start | bytes 37828
  138.9 8.6 %copy-start.74 = (s32[2,788]{1,0:T(2,128)}, s32[2,788]{1,0:T(2,128)S(1)}, u32[]{:S(2)}) copy-start(s32[2,788]{1,0:T(2,128)S(1)} %multiply_add_fusion.4) | copy-start | bytes 18916
  147.7 46.1 %copy-start.1 = (s32[8]{0:T(128)}, s32[8]{0:T(128)S(1)}, u32[]{:S(2)}) copy-start(s32[8]{0:T(128)S(1)} %reshape.282.counts) | copy-start | bytes 100
  152.2 2.2 copy-start
  154.4 39.5 %copy-start.75 = (s32[2,788]{1,0:T(2,128)S(1)}, s32[2,788]{1,0:T(2,128)}, u32[]{:S(2)}) copy-start(s32[2,788]{1,0:T(2,128)} %copy-done.74) | copy-start | bytes 18916
  211.5 2.7 copy-start.56
  211.5 2.7 copy-start.77
  211.5 2.8 copy-start.38
  211.5 2.8 copy-start.46
  211.5 2.8 copy-start.52
  287.4 2.8 copy-start.50
  287.4 2.8 copy-start.70
  290.2 2.7 copy-start.61
  290.2 2.7 copy-start.4
  290.2 2.7 copy-start.5
  293.0 2.9 copy-start.8
  294.7 3.5 copy-start.64
  298.2 3.1 copy-start.40
  298.2 3.1 copy-start.42
  298.2 3.1 copy-start.21
  301.3 7.6 %slice-start = ((s8[6553600]{0:T(1024)(128)(4,1)}), s8[4194304]{0:T(1024)(128)(4,1)S(1)}, s32[]{:S(2)}) async-start(s8[6553600]{0:T(1024)(128)(4,1)} %bitcast.158), calls=%async_computation | async-start | bytes 8388608
  301.3 7.5 %slice-start.1 = ((s8[6553600]{0:T(1024)(128)(4,1)}), s8[2359296]{0:T(1024)(128)(4,1)S(1)}, s32[]{:S(2)}) async-start(s8[6553600]{0:T(1024)(128)(4,1)} %bitcast.158), calls=%async_computation.1 | async-start | bytes 4718592
  308.9 4.6 copy-start.14
  326.0 6.9 %copy-start.26 = (bf16[512,1536]{0,1:T(8,128)(2,1)S(1)}, bf16[512,1536]{0,1:T(8,128)(2,1)}, u32[]{:S(2)}) copy-start(bf16[512,1536]{0,1:T(8,128)(2,1)} %copy-done.25) | copy-start | bytes 4718596
  326.0 6.9 %copy-start.48 = (f32[788]{0:T(1024)S(1)}, f32[788]{0:T(1024)}, u32[]{:S(2)}) copy-start(f32[788]{0:T(1024)} %copy-done.47) | copy-start | bytes 9460
  326.0 6.9 %copy-start.67 = (f32[1,512]{1,0:T(1,128)S(1)}, f32[1,512]{1,0:T(1,128)}, u32[]{:S(2)}) copy-start(f32[1,512]{1,0:T(1,128)} %copy-done.66) | copy-start | bytes 6148
  332.9 5.1 slice-start.2
  332.9 3.6 copy-start.59
  332.9 3.6 copy-start.54
  332.9 5.1 slice-start.3
  342.1 4.0 copy-start.18
  346.4 4.9 copy-start.73
  358.5 126.4 %copy-start.57 = (f32[2,11,64]{2,0,1:T(2,128)S(1)}, f32[2,11,64]{2,0,1:T(2,128)}, u32[]{:S(2)}) copy-start(f32[2,11,64]{2,0,1:T(2,128)} %param.33) | copy-start | bytes 16900
  358.5 126.6 %copy-start.72 = (f32[11,64]{1,0:T(8,128)S(1)}, f32[11,64]{1,0:T(8,128)}, u32[]{:S(2)}) copy-start(f32[11,64]{1,0:T(8,128)} %param.26) | copy-start | bytes 8452
  358.5 137.9 %copy-start.30 = (f32[2,64,512]{2,1,0:T(8,128)S(1)}, f32[2,64,512]{2,1,0:T(8,128)}, u32[]{:S(2)}) copy-start(f32[2,64,512]{2,1,0:T(8,128)} %param.28) | copy-start | bytes 786436
  358.5 137.9 %copy-start.36 = (f32[64,512]{1,0:T(8,128)S(1)}, f32[64,512]{1,0:T(8,128)}, u32[]{:S(2)}) copy-start(f32[64,512]{1,0:T(8,128)} %param.21) | copy-start | bytes 393220
  484.9 13.1 %copy-start.33 = (f32[64,2560]{1,0:T(8,128)S(1)}, f32[64,2560]{1,0:T(8,128)}, u32[]{:S(2)}) copy-start(f32[64,2560]{1,0:T(8,128)} %get-tuple-element.52) | copy-start | bytes 1966084
  486.1 12.0 %copy-start.24 = (f32[2,64,1536]{2,1,0:T(8,128)S(1)}, f32[2,64,1536]{2,1,0:T(8,128)}, u32[]{:S(2)}) copy-start(f32[2,64,1536]{2,1,0:T(8,128)} %param.27) | copy-start | bytes 2359300
  486.1 12.0 %copy-start.28 = (f32[64,1536]{1,0:T(8,128)S(1)}, f32[64,1536]{1,0:T(8,128)}, u32[]{:S(2)}) copy-start(f32[64,1536]{1,0:T(8,128)} %param.20) | copy-start | bytes 1179652
  488.9 10.2 %copy-start.81 = (f32[4,256]{1,0:T(4,128)}, f32[4,256]{1,0:T(4,128)S(1)}, u32[]{:S(2)}) copy-start(f32[4,256]{1,0:T(4,128)S(1)} %reshape.297) | copy-start | bytes 12292
  496.4 2.8 copy-start.34
  507.2 7.1 %copy-start.44 = (f32[64,4]{1,0:T(8,128)S(1)}, f32[64,4]{1,0:T(8,128)}, u32[]{:S(2)}) copy-start(f32[64,4]{1,0:T(8,128)} %get-tuple-element.240) | copy-start | bytes 3076
  507.2 7.2 %copy-start.79 = (f32[64,4]{0,1:T(4,128)S(1)}, f32[64,4]{0,1:T(4,128)}, u32[]{:S(2)}) copy-start(f32[64,4]{0,1:T(4,128)} %param.22) | copy-start | bytes 3076
  507.2 8.7 %copy-start.43 = (f32[64,4]{1,0:T(8,128)S(1)}, f32[64,4]{1,0:T(8,128)}, u32[]{:S(2)}) copy-start(f32[64,4]{1,0:T(8,128)} %get-tuple-element.241) | copy-start | bytes 3076
  507.2 10.9 %copy-start.80 = (f32[788]{0:T(1024)S(1)}, f32[788]{0:T(1024)}, u32[]{:S(2)}) copy-start(f32[788]{0:T(1024)} %get-tuple-element.202) | copy-start | bytes 9460
  507.2 10.9 %copy-start.7 = (f32[788,512]{1,0:T(8,128)S(1)}, f32[788,512]{1,0:T(8,128)}, u32[]{:S(2)}) copy-start(f32[788,512]{1,0:T(8,128)} %copy-done.6) | copy-start | bytes 4841476
  507.2 10.9 %copy-start.9 = (bf16[788,512]{1,0:T(8,128)(2,1)S(1)}, bf16[788,512]{1,0:T(8,128)(2,1)}, u32[]{:S(2)}) copy-start(bf16[788,512]{1,0:T(8,128)(2,1)} %param.18) | copy-start | bytes 2420740
  507.2 10.9 %copy-start.55 = (f32[788]{0:T(1024)S(1)}, f32[788]{0:T(1024)}, u32[]{:S(2)}) copy-start(f32[788]{0:T(1024)} %copy-done.53) | copy-start | bytes 9460
  507.2 10.9 %copy-start.63 = (f32[788]{0:T(1024)S(1)}, f32[788]{0:T(1024)}, u32[]{:S(2)}) copy-start(f32[788]{0:T(1024)} %copy-done.62) | copy-start | bytes 9460
  507.2 10.9 %copy-start.65 = (f32[788]{0:T(1024)S(1)}, f32[788]{0:T(1024)}, u32[]{:S(2)}) copy-start(f32[788]{0:T(1024)} %copy-done.64) | copy-start | bytes 9460
  507.2 10.9 %copy-start.68 = (f32[1,512]{1,0:T(1,128)S(1)}, f32[1,512]{1,0:T(1,128)}, u32[]{:S(2)}) copy-start(f32[1,512]{1,0:T(1,128)} %copy-done.66) | copy-start | bytes 6148
  518.1 3.1 copy-start.17
  521.2 2.3 copy-start.16
  (24 other events, 31.3 us)

commit v12 on v9

--- a/solution.py
+++ b/solution.py
@@ -888,7 +888,8 @@
         if weight.ndim == 3:
             new_weight, new_state = adamw_pass(weight, state, grad, rate)
         else:
-            new_weight, new_state = adamw(weight, state, grad, rate)
+            new_weight, new_state = adamw_pass(weight[None], state[:, None], grad[None], rate)
+            new_weight, new_state = new_weight[0], new_state[:, 0]
         news.append(new_weight)
         states.append(new_state)
     return (result.astype(BF16), input_grad) + reduced + tuple(news) + tuple(states)

time: 529 us -> 539 us (1.019)
  local copies, waits for them, and re-layouts: 74.5 us -> 88.6 us
  other arithmetic: 49.1 us -> 36.5 us
  Pallas kernels: 333 us -> 341 us
    pallas_call x2 -> x7, Pallas kernels: 13.9 us -> 22.5 us  [adamw_pass(): pl.pallas_call(functools.partial(adamw_kernel, rate), grid=(n,), in_specs...]
    mul x8 -> x0, other arithmetic: 6.38 us -> none  [the longest x5 4.59 us: adamw(): first = 0.5 * moments[0] + 0.5 * grad]
    select_n x5 -> x0, other arithmetic: 6.25 us -> none  [adamw(): jnp.where(which, 0.5 * moments + 0.5 * grad, jnp.sqrt(0.5 * moments * mom...]
    unnamed x188 -> x168, local copies, waits for them, and re-layouts: 15.5 us -> 19.3 us
where the time goes in v12:
time: 539 us; the launch traced here: 535 us
  Pallas kernels  341 us (63%)
  local copies, waits for them, and re-layouts  88.6 us (16%)
  matrix products  66.3 us (12%)
  other arithmetic  36.5 us (7%)
    pallas_call x1, Pallas kernels, grad_reduce(): pl.pallas_call(functools.partial(ring_rs2_kernel, groups, x_pair), out_sh...  126 us
    pallas_call x1, Pallas kernels, ring_all_gather(): pl.pallas_call(functools.partial(ring_ag_kernel, groups), out_shape=shape...  101 us
    pallas_call x1, Pallas kernels, ffn_backward(): pl.pallas_call(functools.partial(ffn_bwd_kernel, micro), grid_spec=grid_s...  52.2 us
    pallas_call x1, Pallas kernels, ffn_forward(): pl.pallas_call(functools.partial(ffn_fwd_kernel, micro), grid_spec=grid_s...  39.5 us
    pallas_call x7, Pallas kernels, adamw_pass(): pl.pallas_call(functools.partial(adamw_kernel, rate), grid=(n,), in_specs...  22.5 us
    unnamed x168, local copies, waits for them, and re-layouts  19.3 us
    dot_general x2, matrix products, pick_rows(): both = jnp.einsum('mnr,mrd->mnd', onehot, split, preferred_element_type=F32)  15.6 us
    dot_general x2, local copies, waits for them, and re-layouts, attention_bwd(): jnp.einsum('tbhsd,kthd->bsk', d_qkv, w3, preferred_element_type=F32)  11.4 us

profile of v12, /device:TPU:1, one launch (start us, length us, event | category | flops | bytes accessed | tf_op | source)
XLA Modules:
  0.0 534.7 jit_solution(2558039743240738583)
XLA Ops:
  0.7 2.9 convert_element_type.110.refs_0_
  6.2 101.1 %shard_map.344 = (bf16[4,512,2048]{2,1,0:T(8,128)(2,1)}, bf16[4,2048,512]{2,1,0:T(8,128)(2,1)}, bf16[512,2560]{1,0:T(8,128)(2,1)}) custom-call(bf16[4,64,2048]{2,1,0:T(8,128)(2,1)} %convert_element_type.110.refs_0_, bf16[4,256,512]{2,1,0:T(8,128)(2,1)} %convert_element_type.111.refs_1_, bf16[64,2560]{1,0:T(8,128)(2,1)} %pad.14.refs_2_), custom_call_target="tpu_custom_call" | custom-call | bytes 19398656 | tf_op jit(solution)/shard_map/pallas_call | solution.py:271
  107.3 3.2 copy.270
  113.8 2.2 reshape.272
  117.6 1.8 copy.269
  119.4 1.8 fusion.18
  122.9 1.3 fusion.7
  124.2 1.5 copy-done.2
  125.7 1.6 fusion.46
  129.0 2.1 fusion.85
  135.6 2.3 reduce-window.6
  138.9 8.6 %fusion.9.x_ref = bf16[2,2048,512]{2,1,0:T(8,128)(2,1)} fusion(s32[2,788]{1,0:T(2,128)S(1)} %multiply_add_fusion, bf16[2,394,512]{2,1,0:T(8,128)(2,1)} %reshape.253), kind=kOutput, calls=%fused_computation.17 | convolution fusion | flops 3313664000 | bytes 5007520 | tf_op jit(solution)/shard_map/mnr,mnd->mrd/dot_general | solution.py:822
  148.8 1.3 copy.278
  150.2 2.0 reshape.278.b1_ref
  152.2 2.2 copy-done
  154.3 39.5 %shard_map.345 = (f32[2,2048,2048]{2,1,0:T(8,128)}, bf16[2,2048,2048]{2,1,0:T(8,128)(2,1)}, bf16[2,2048,1024]{2,1,0:T(8,128)(2,1)}) custom-call(s32[8]{0:T(128)S(1)} %reshape.252.counts, bf16[2,2048,512]{2,1,0:T(8,128)(2,1)S(1)} %copy-done, bf16[4,512,2048]{2,1,0:T(8,128)(2,1)} %get-tuple-element.52.w1_ref, f32[4,1,2048]{2,1,0:T(1,128)S(1)} %reshape.278.b1_ref, ...), custom_call_target="tpu_custom_call" | custom-call | flops 8589934592 | bytes 31457280 | tf_op jit(solution)/shard_map/pallas_call | solution.py:541
  193.8 9.3 %fusion.2 = f32[2,788,1024]{2,1,0:T(8,128)S(1)} fusion(bf16[2,2048,1024]{2,1,0:T(8,128)(2,1)} %get-tuple-element.54, s32[2,788]{1,0:T(2,128)S(1)} %copy-done.65), kind=kOutput, calls=%fused_computation.3 | convolution fusion | flops 6613450752 | bytes 14850208 | tf_op jit(solution)/shard_map/mnr,mrd->mnd/dot_general | solution.py:690
  203.9 2.1 fusion.83
  206.0 2.7 reshape.254
  208.8 2.7 reshape.255
  211.6 2.7 multiply_reduce_fusion.5
  214.5 2.5 reshape.257
  217.0 1.7 multiply_convert_fusion.4
  218.7 7.7 %fusion.10.dy_ref = bf16[2,2048,512]{2,1,0:T(8,128)(2,1)} fusion(s32[2,788]{1,0:T(2,128)S(1)} %copy-done.65, bf16[2,394,512]{2,1,0:T(8,128)(2,1)S(1)} %get-tuple-element.249, bf16[2,394,512]{2,1,0:T(8,128)(2,1)S(1)} %get-tuple-element.248), kind=kOutput, calls=%fused_computation.18 | convolution fusion | flops 3313664000 | bytes 5814432 | tf_op jit(solution)/shard_map/mnr,mnd->mrd/dot_general | solution.py:836
  226.4 52.2 %shard_map.346 = (bf16[2,2048,1024]{2,1,0:T(8,128)(2,1)}, bf16[4,512,2048]{2,1,0:T(8,128)(2,1)}, bf16[4,2048,512]{2,1,0:T(8,128)(2,1)}, f32[4,1,2048]{2,1,0:T(1,128)}, f32[4,1,512]{2,1,0:T(1,128)}) custom-call(s32[8]{0:T(128)} %copy-done.1, bf16[2,2048,512]{2,1,0:T(8,128)(2,1)} %fusion.10.dy_ref, bf16[2,2048,512]{2,1,0:T(8,128)(2,1)} %fusion.9.x_ref, ...), custom_call_target="tpu_custom_call" | custom-call | flops 17179869184 | bytes 100663296 | tf_op jit(solution)/shard_map/pallas_call | solution.py:617
  279.7 6.2 %fusion.13 = f32[2,394,1024]{2,1,0:T(8,128)S(1)} fusion(bf16[2,2048,1024]{2,1,0:T(8,128)(2,1)} %get-tuple-element.57, bf16[2,788,2048]{2,1,0:T(8,128)(2,1)S(1)} %fusion.1), kind=kOutput, calls=%fused_computation.21 | convolution fusion | flops 3306725376 | bytes 18169856 | tf_op jit(solution)/shard_map/mnr,mrd->mnd/dot_general | solution.py:690
  285.9 1.5 slice_add_fusion.3
  287.4 2.8 reshape.258
  290.2 2.7 multiply_reduce_fusion.2
  293.0 1.7 fusion.82
  299.4 1.9 fusion.49
  301.3 7.5 %multiply_reduce_fusion = (f32[4,8,197]{2,1,0:T(8,128)S(1)}, f32[4,8,197,197]{2,3,1,0:T(8,128)}) fusion(f32[4,8,197,197]{2,3,1,0:T(8,128)} %copy-done.2, f32[4,8,197]{2,1,0:T(8,128)S(1)} %log_add_fusion, bf16[4,8,197,64]{2,3,0,1:T(8,128)(2,1)S(1)} %copy-done.22, bf16[4,8,197,64]{2,3,0,1:T(8,128)(2,1)S(1)} %fusion.49), kind=kOutput, calls=%fused_computation.6 | convolution fusion | flops 163922912 | bytes 11599360 | tf_op jit(solution)/shard_map/bhqd,bhkd->bhqk/dot_general | solution.py:746
  308.9 4.6 multiply_convert_fusion
  315.8 1.3 fusion.43
  317.1 4.4 fusion.77
  321.5 4.5 copy.319
  326.0 6.9 %reshape.280 = bf16[788,64,8,3]{0,1,3,2:T(8,128)(2,1)} reshape(bf16[4,197,64,8,3]{1,0,2,4,3:T(4,128)(2,1)} %copy.319) | data formatting | bytes 4841472 | tf_op jit(solution)/shard_map/tbhsd,kthd->bsk/dot_general | solution.py:757
  332.9 3.6 bitcast_reduce_fusion
  336.5 1.4 fusion.28
  339.5 2.7 convolution_convert_fusion.1
  342.1 4.0 copy.291
  346.4 4.9 fusion.19
  353.0 3.8 concatenate.48
  356.8 1.7 pad.16.refs_2_
  358.5 126.1 %shard_map.347 = (f32[4,64,2048]{2,1,0:T(8,128)}, f32[4,256,512]{2,1,0:T(8,128)}, f32[64,2560]{1,0:T(8,128)}) custom-call(bf16[4,512,2048]{2,1,0:T(8,128)(2,1)} %get-tuple-element.58.refs_0_, bf16[4,2048,512]{2,1,0:T(8,128)(2,1)} %get-tuple-element.59.refs_1_, bf16[512,2560]{1,0:T(8,128)(2,1)} %pad.16.refs_2_), custom_call_target="tpu_custom_call" | custom-call | flops 9699328 | bytes 19398656 | tf_op jit(solution)/shard_map/pallas_call | solution.py:478
  484.6 6.9 %shard_map.351 = (f32[4,64,2048]{2,1,0:T(8,128)}, f32[2,4,64,2048]{3,2,1,0:T(8,128)}) custom-call(f32[4,64,2048]{2,1,0:T(8,128)} %w_ref.2, f32[2,4,64,2048]{3,2,1,0:T(8,128)} %m_ref.2, f32[4,64,2048]{2,1,0:T(8,128)} %get-tuple-element.304.g_ref), custom_call_target="tpu_custom_call" | custom-call | flops 6291456 | bytes 14680064 | tf_op jit(solution)/shard_map/pallas_call | solution.py:647
  491.4 6.9 %shard_map.353 = (f32[4,256,512]{2,1,0:T(8,128)}, f32[2,4,256,512]{3,2,1,0:T(8,128)}) custom-call(f32[4,256,512]{2,1,0:T(8,128)} %w_ref.3, f32[2,4,256,512]{3,2,1,0:T(8,128)} %m_ref.3, f32[4,256,512]{2,1,0:T(8,128)} %get-tuple-element.306.g_ref), custom_call_target="tpu_custom_call" | custom-call | flops 6291456 | bytes 14680064 | tf_op jit(solution)/shard_map/pallas_call | solution.py:647
  499.2 2.6 shard_map.348
  501.9 2.7 copy.300
  504.6 1.3 slice_bitcast_fusion.3
  506.5 1.4 shard_map.354
  507.8 1.3 copy.308
  509.2 1.6 slice_bitcast_fusion.10.g_ref
  510.7 1.9 shard_map.349
  512.6 1.8 slice.172
  514.4 1.4 slice_bitcast_fusion.9
  517.2 1.5 shard_map.350
  518.7 1.5 copy.307
  520.2 1.4 copy.306
  523.4 1.3 shard_map.352
  525.4 1.6 slice.173
  527.7 3.0 add_add_fusion.2
  530.8 1.3 copy.356
  533.1 1.3 copy.357
  (265 shorter events, 36.8 us)
Async XLA Ops:
  0.7 2.9 copy-start.15
  3.5 1.6 copy-start.63
  3.6 1.7 copy-start.71
  107.3 3.3 copy-start.3
  110.6 20.9 %copy-start.60 = (f32[1,512]{1,0:T(1,128)}, f32[1,512]{1,0:T(1,128)S(1)}, u32[]{:S(2)}) copy-start(f32[1,512]{1,0:T(1,128)S(1)} %get-tuple-element.255) | copy-start | bytes 6148
  110.8 5.5 %copy-start.10 = (bf16[512,2560]{1,0:T(8,128)(2,1)S(1)}, bf16[512,2560]{1,0:T(8,128)(2,1)}, u32[]{:S(2)}) copy-start(bf16[512,2560]{1,0:T(8,128)(2,1)} %get-tuple-element.51) | copy-start | bytes 7864324
  117.6 1.8 copy-start.29
  119.4 1.8 copy-start.25
  121.6 2.6 copy-start.21
  122.9 2.8 copy-start.2
  122.9 2.8 copy-start.33
  124.2 3.1 copy-start.35
  129.0 2.1 copy-start.28
  131.5 3.9 copy-start.51
  132.1 3.3 copy-start.66
  133.7 1.9 copy-start.37
  133.7 13.8 %copy-start.31 = (f32[788,4]{0,1:T(4,128)}, f32[788,4]{0,1:T(4,128)S(1)}, u32[]{:S(2)}) copy-start(f32[788,4]{0,1:T(4,128)S(1)} %get-tuple-element.271) | copy-start | bytes 37828
  133.7 1.9 copy-start.43
  138.9 8.6 %copy-start.64 = (s32[2,788]{1,0:T(2,128)}, s32[2,788]{1,0:T(2,128)S(1)}, u32[]{:S(2)}) copy-start(s32[2,788]{1,0:T(2,128)S(1)} %multiply_add_fusion) | copy-start | bytes 18916
  147.7 46.1 %copy-start.1 = (s32[8]{0:T(128)}, s32[8]{0:T(128)S(1)}, u32[]{:S(2)}) copy-start(s32[8]{0:T(128)S(1)} %reshape.252.counts) | copy-start | bytes 100
  152.2 2.2 copy-start
  154.3 39.5 %copy-start.65 = (s32[2,788]{1,0:T(2,128)S(1)}, s32[2,788]{1,0:T(2,128)}, u32[]{:S(2)}) copy-start(s32[2,788]{1,0:T(2,128)} %copy-done.64) | copy-start | bytes 18916
  211.5 2.7 copy-start.48
  211.5 2.7 copy-start.67
  211.5 2.8 copy-start.32
  211.5 2.8 copy-start.38
  211.5 2.8 copy-start.44
  287.4 2.8 copy-start.42
  287.4 2.8 copy-start.61
  290.2 2.7 copy-start.52
  290.2 2.7 copy-start.4
  290.2 2.7 copy-start.5
  293.0 2.9 copy-start.8
  294.7 3.5 copy-start.55
  298.2 3.1 copy-start.34
  298.2 3.1 copy-start.36
  298.2 3.1 copy-start.22
  301.3 7.6 %slice-start = ((s8[6553600]{0:T(1024)(128)(4,1)}), s8[4194304]{0:T(1024)(128)(4,1)S(1)}, s32[]{:S(2)}) async-start(s8[6553600]{0:T(1024)(128)(4,1)} %bitcast.149), calls=%async_computation | async-start | bytes 8388608
  301.3 7.5 %slice-start.1 = ((s8[6553600]{0:T(1024)(128)(4,1)}), s8[2359296]{0:T(1024)(128)(4,1)S(1)}, s32[]{:S(2)}) async-start(s8[6553600]{0:T(1024)(128)(4,1)} %bitcast.149), calls=%async_computation.1 | async-start | bytes 4718592
  308.8 4.6 copy-start.14
  326.0 6.9 %copy-start.26 = (bf16[512,1536]{0,1:T(8,128)(2,1)S(1)}, bf16[512,1536]{0,1:T(8,128)(2,1)}, u32[]{:S(2)}) copy-start(bf16[512,1536]{0,1:T(8,128)(2,1)} %copy-done.25) | copy-start | bytes 4718596
  326.0 6.9 %copy-start.40 = (f32[788]{0:T(1024)S(1)}, f32[788]{0:T(1024)}, u32[]{:S(2)}) copy-start(f32[788]{0:T(1024)} %copy-done.39) | copy-start | bytes 9460
  326.0 6.9 %copy-start.58 = (f32[1,512]{1,0:T(1,128)S(1)}, f32[1,512]{1,0:T(1,128)}, u32[]{:S(2)}) copy-start(f32[1,512]{1,0:T(1,128)} %copy-done.57) | copy-start | bytes 6148
  332.9 5.1 slice-start.2
  332.9 3.6 copy-start.50
  332.9 3.6 copy-start.46
  332.9 5.1 slice-start.3
  336.5 1.8 copy-start.19
  336.5 1.8 copy-start.53
  342.1 4.0 copy-start.18
  346.4 4.9 copy-start.62
  491.4 6.9 %copy-start.20 = (f32[64,2560]{1,0:T(8,128)S(1)}, f32[64,2560]{1,0:T(8,128)}, u32[]{:S(2)}) copy-start(f32[64,2560]{1,0:T(8,128)} %get-tuple-element.62) | copy-start | bytes 1966084
  498.4 7.5 %copy-start.70 = (f32[2,11,64]{2,0,1:T(2,128)S(1)}, f32[2,11,64]{2,0,1:T(2,128)}, u32[]{:S(2)}) copy-start(f32[2,11,64]{2,0,1:T(2,128)} %param.33) | copy-start | bytes 16900
  501.8 14.0 %copy-start.74 = (f32[2,64,4]{1,2,0:T(4,128)S(1)}, f32[2,64,4]{1,2,0:T(4,128)}, u32[]{:S(2)}) copy-start(f32[2,64,4]{1,2,0:T(4,128)} %param.29) | copy-start | bytes 6148
  501.8 14.7 %copy-start.72 = (f32[64,4]{0,1:T(4,128)S(1)}, f32[64,4]{0,1:T(4,128)}, u32[]{:S(2)}) copy-start(f32[64,4]{0,1:T(4,128)} %param.22) | copy-start | bytes 3076
  501.8 25.9 %copy-start.68 = (f32[788]{0:T(1024)S(1)}, f32[788]{0:T(1024)}, u32[]{:S(2)}) copy-start(f32[788]{0:T(1024)} %get-tuple-element.222) | copy-start | bytes 9460
  501.8 25.9 %copy-start.7 = (f32[788,512]{1,0:T(8,128)S(1)}, f32[788,512]{1,0:T(8,128)}, u32[]{:S(2)}) copy-start(f32[788,512]{1,0:T(8,128)} %copy-done.6) | copy-start | bytes 4841476
  501.8 25.8 %copy-start.9 = (bf16[788,512]{1,0:T(8,128)(2,1)S(1)}, bf16[788,512]{1,0:T(8,128)(2,1)}, u32[]{:S(2)}) copy-start(bf16[788,512]{1,0:T(8,128)(2,1)} %param.18) | copy-start | bytes 2420740
  501.8 25.8 %copy-start.47 = (f32[788]{0:T(1024)S(1)}, f32[788]{0:T(1024)}, u32[]{:S(2)}) copy-start(f32[788]{0:T(1024)} %copy-done.45) | copy-start | bytes 9460
  501.8 25.8 %copy-start.54 = (f32[788]{0:T(1024)S(1)}, f32[788]{0:T(1024)}, u32[]{:S(2)}) copy-start(f32[788]{0:T(1024)} %copy-done.53) | copy-start | bytes 9460
  501.8 25.8 %copy-start.56 = (f32[788]{0:T(1024)S(1)}, f32[788]{0:T(1024)}, u32[]{:S(2)}) copy-start(f32[788]{0:T(1024)} %copy-done.55) | copy-start | bytes 9460
  501.8 25.8 %copy-start.59 = (f32[1,512]{1,0:T(1,128)S(1)}, f32[1,512]{1,0:T(1,128)}, u32[]{:S(2)}) copy-start(f32[1,512]{1,0:T(1,128)} %copy-done.57) | copy-start | bytes 6148
  527.7 3.1 copy-start.17
  530.7 2.3 copy-start.16
  (15 other events, 15.9 us)

commit v13 on v9

--- a/solution.py
+++ b/solution.py
@@ -488,7 +488,7 @@
     )(gu, gd, gdense)
 
 
-TILE = 256
+TILE = 128
 TILE_B = 256
 CAPP = 512
 SQRT_HALF = float(np.sqrt(0.5))

time: 529 us -> 531 us (level)
  no operation moved by 1% of the time
where the time goes in v13:
time: 531 us; the launch traced here: 526 us
  Pallas kernels  333 us (63%)
  local copies, waits for them, and re-layouts  74.5 us (14%)
  matrix products  66.2 us (12%)
  other arithmetic  49.1 us (9%)
    pallas_call x1, Pallas kernels, grad_reduce(): pl.pallas_call(functools.partial(ring_rs2_kernel, groups, x_pair), out_sh...  126 us
    pallas_call x1, Pallas kernels, ring_all_gather(): pl.pallas_call(functools.partial(ring_ag_kernel, groups), out_shape=shape...  101 us
    pallas_call x1, Pallas kernels, ffn_backward(): pl.pallas_call(functools.partial(ffn_bwd_kernel, micro), grid_spec=grid_s...  52.2 us
    pallas_call x1, Pallas kernels, ffn_forward(): pl.pallas_call(functools.partial(ffn_fwd_kernel, micro), grid_spec=grid_s...  40.8 us
    dot_general x2, matrix products, pick_rows(): both = jnp.einsum('mnr,mrd->mnd', onehot, split, preferred_element_type=F32)  15.6 us
    unnamed x188, local copies, waits for them, and re-layouts  15.5 us
    pallas_call x2, Pallas kernels, adamw_pass(): pl.pallas_call(functools.partial(adamw_kernel, rate), grid=(n,), in_specs...  13.9 us
    dot_general x2, local copies, waits for them, and re-layouts, attention_bwd(): jnp.einsum('tbhsd,kthd->bsk', d_qkv, w3, preferred_element_type=F32)  11.4 us

profile of v13, /device:TPU:1, one launch (start us, length us, event | category | flops | bytes accessed | tf_op | source)
XLA Modules:
  0.0 525.6 jit_solution(15024143649483636245)
XLA Ops:
  0.7 2.9 convert_element_type.110.refs_0_
  6.2 101.1 %shard_map.344 = (bf16[4,512,2048]{2,1,0:T(8,128)(2,1)}, bf16[4,2048,512]{2,1,0:T(8,128)(2,1)}, bf16[512,2560]{1,0:T(8,128)(2,1)}) custom-call(bf16[4,64,2048]{2,1,0:T(8,128)(2,1)} %convert_element_type.110.refs_0_, bf16[4,256,512]{2,1,0:T(8,128)(2,1)} %convert_element_type.111.refs_1_, bf16[64,2560]{1,0:T(8,128)(2,1)} %pad.14.refs_2_), custom_call_target="tpu_custom_call" | custom-call | bytes 19398656 | tf_op jit(solution)/shard_map/pallas_call | solution.py:271
  107.3 3.2 copy.321
  112.5 1.3 fusion.27
  113.8 2.2 reshape.302
  116.3 1.2 slice.172
  117.6 1.8 copy.320
  119.4 1.8 fusion.18
  122.9 1.3 fusion.7
  124.2 1.5 copy-done.2
  125.7 1.6 fusion.46
  129.0 2.1 fusion.136
  132.4 1.2 fusion.137
  135.7 2.3 reduce-window.6
  138.9 8.6 %fusion.9.x_ref = bf16[2,2048,512]{2,1,0:T(8,128)(2,1)} fusion(s32[2,788]{1,0:T(2,128)S(1)} %multiply_add_fusion.4, bf16[2,394,512]{2,1,0:T(8,128)(2,1)} %reshape.283), kind=kOutput, calls=%fused_computation.17 | convolution fusion | flops 3313664000 | bytes 5007520 | tf_op jit(solution)/shard_map/mnr,mnd->mrd/dot_general | solution.py:822
  148.8 1.3 copy.329
  150.2 2.0 reshape.308.b1_ref
  152.2 2.2 copy-done
  154.4 40.8 %shard_map.345 = (f32[2,2048,2048]{2,1,0:T(8,128)}, bf16[2,2048,2048]{2,1,0:T(8,128)(2,1)}, bf16[2,2048,1024]{2,1,0:T(8,128)(2,1)}) custom-call(s32[8]{0:T(128)S(1)} %reshape.282.counts, bf16[2,2048,512]{2,1,0:T(8,128)(2,1)S(1)} %copy-done, bf16[4,512,2048]{2,1,0:T(8,128)(2,1)} %get-tuple-element.42.w1_ref, f32[4,1,2048]{2,1,0:T(1,128)S(1)} %reshape.308.b1_ref, ...), custom_call_target="tpu_custom_call" | custom-call | flops 8589934592 | bytes 31457280 | tf_op jit(solution)/shard_map/pallas_call | solution.py:541
  195.1 9.3 %fusion.2 = f32[2,788,1024]{2,1,0:T(8,128)S(1)} fusion(bf16[2,2048,1024]{2,1,0:T(8,128)(2,1)} %get-tuple-element.44, s32[2,788]{1,0:T(2,128)S(1)} %copy-done.75), kind=kOutput, calls=%fused_computation.3 | convolution fusion | flops 6613450752 | bytes 14850208 | tf_op jit(solution)/shard_map/mnr,mrd->mnd/dot_general | solution.py:690
  205.3 2.1 fusion.132
  207.4 2.7 reshape.284
  210.1 2.7 reshape.285
  212.9 2.7 multiply_reduce_fusion.5
  215.9 2.5 reshape.287
  218.3 1.7 multiply_convert_fusion.4
  220.0 7.7 %fusion.10.dy_ref = bf16[2,2048,512]{2,1,0:T(8,128)(2,1)} fusion(s32[2,788]{1,0:T(2,128)S(1)} %copy-done.75, bf16[2,394,512]{2,1,0:T(8,128)(2,1)S(1)} %get-tuple-element.233, bf16[2,394,512]{2,1,0:T(8,128)(2,1)S(1)} %get-tuple-element.232), kind=kOutput, calls=%fused_computation.18 | convolution fusion | flops 3313664000 | bytes 5814432 | tf_op jit(solution)/shard_map/mnr,mnd->mrd/dot_general | solution.py:836
  227.7 52.2 %shard_map.346 = (bf16[2,2048,1024]{2,1,0:T(8,128)(2,1)}, bf16[4,512,2048]{2,1,0:T(8,128)(2,1)}, bf16[4,2048,512]{2,1,0:T(8,128)(2,1)}, f32[4,1,2048]{2,1,0:T(1,128)}, f32[4,1,512]{2,1,0:T(1,128)}) custom-call(s32[8]{0:T(128)} %copy-done.1, bf16[2,2048,512]{2,1,0:T(8,128)(2,1)} %fusion.10.dy_ref, bf16[2,2048,512]{2,1,0:T(8,128)(2,1)} %fusion.9.x_ref, ...), custom_call_target="tpu_custom_call" | custom-call | flops 17179869184 | bytes 100663296 | tf_op jit(solution)/shard_map/pallas_call | solution.py:617
  279.9 1.1 fusion.1
  281.0 6.2 %fusion.13 = f32[2,394,1024]{2,1,0:T(8,128)S(1)} fusion(bf16[2,2048,1024]{2,1,0:T(8,128)(2,1)} %get-tuple-element.47, bf16[2,788,2048]{2,1,0:T(8,128)(2,1)S(1)} %fusion.1), kind=kOutput, calls=%fused_computation.21 | convolution fusion | flops 3306725376 | bytes 18169856 | tf_op jit(solution)/shard_map/mnr,mrd->mnd/dot_general | solution.py:690
  287.3 1.5 slice_add_fusion.3
  288.8 2.8 reshape.288
  291.6 2.7 multiply_reduce_fusion.2
  294.3 1.7 fusion.131
  296.1 1.2 copy-done.6
  299.5 1.2 slice.181
  300.7 1.9 fusion.49
  302.7 7.5 %multiply_reduce_fusion = (f32[4,8,197]{2,1,0:T(8,128)S(1)}, f32[4,8,197,197]{2,3,1,0:T(8,128)}) fusion(f32[4,8,197,197]{2,3,1,0:T(8,128)} %copy-done.2, f32[4,8,197]{2,1,0:T(8,128)S(1)} %log_add_fusion, bf16[4,8,197,64]{2,3,0,1:T(8,128)(2,1)S(1)} %copy-done.21, bf16[4,8,197,64]{2,3,0,1:T(8,128)(2,1)S(1)} %fusion.49), kind=kOutput, calls=%fused_computation.6 | convolution fusion | flops 163922912 | bytes 11599360 | tf_op jit(solution)/shard_map/bhqd,bhkd->bhqk/dot_general | solution.py:746
  310.2 4.6 multiply_convert_fusion
  316.0 1.1 fusion.48
  317.2 1.3 fusion.43
  318.5 4.4 fusion.126
  322.8 4.5 copy.382
  327.3 6.9 %reshape.310 = bf16[788,64,8,3]{0,1,3,2:T(8,128)(2,1)} reshape(bf16[4,197,64,8,3]{1,0,2,4,3:T(4,128)(2,1)} %copy.382) | data formatting | bytes 4841472 | tf_op jit(solution)/shard_map/tbhsd,kthd->bsk/dot_general | solution.py:757
  334.3 3.6 bitcast_reduce_fusion
  337.9 1.4 fusion.28
  340.8 2.7 convolution_convert_fusion.1
  343.5 4.0 copy.342
  347.8 4.9 fusion.19
  352.8 1.1 reshape_squeeze.4
  354.3 3.8 concatenate.48
  358.1 1.7 pad.16.refs_2_
  359.8 125.5 %shard_map.347 = (f32[4,64,2048]{2,1,0:T(8,128)}, f32[4,256,512]{2,1,0:T(8,128)}, f32[64,2560]{1,0:T(8,128)}) custom-call(bf16[4,512,2048]{2,1,0:T(8,128)(2,1)} %get-tuple-element.48.refs_0_, bf16[4,2048,512]{2,1,0:T(8,128)(2,1)} %get-tuple-element.49.refs_1_, bf16[512,2560]{1,0:T(8,128)(2,1)} %pad.16.refs_2_), custom_call_target="tpu_custom_call" | custom-call | flops 9699328 | bytes 19398656 | tf_op jit(solution)/shard_map/pallas_call | solution.py:478
  486.7 1.5 fusion.102
  489.4 1.3 broadcast_multiply_fusion.4
  490.7 1.4 fusion.107
  493.0 1.4 broadcast_multiply_fusion.3
  494.5 1.4 fusion.110
  499.6 1.2 fusion.62
  500.8 6.9 %shard_map.348 = (f32[4,64,2048]{2,1,0:T(8,128)}, f32[2,4,64,2048]{3,2,1,0:T(8,128)}) custom-call(f32[4,64,2048]{2,1,0:T(8,128)} %w_ref.2, f32[2,4,64,2048]{3,2,1,0:T(8,128)} %m_ref.2, f32[4,64,2048]{2,1,0:T(8,128)} %get-tuple-element.302.g_ref), custom_call_target="tpu_custom_call" | custom-call | flops 6291456 | bytes 14680064 | tf_op jit(solution)/shard_map/pallas_call | solution.py:647
  507.7 7.0 %shard_map.349 = (f32[4,256,512]{2,1,0:T(8,128)}, f32[2,4,256,512]{3,2,1,0:T(8,128)}) custom-call(f32[4,256,512]{2,1,0:T(8,128)} %w_ref.3, f32[2,4,256,512]{3,2,1,0:T(8,128)} %m_ref.3, f32[4,256,512]{2,1,0:T(8,128)} %get-tuple-element.304.g_ref), custom_call_target="tpu_custom_call" | custom-call | flops 6291456 | bytes 14680064 | tf_op jit(solution)/shard_map/pallas_call | solution.py:647
  518.6 3.0 add_add_fusion.2
  521.6 1.3 copy.420
  524.0 1.3 copy.421
  (297 shorter events, 32.3 us)
Async XLA Ops:
  0.7 2.9 copy-start.15
  107.3 3.3 copy-start.3
  110.6 20.9 %copy-start.69 = (f32[1,512]{1,0:T(1,128)}, f32[1,512]{1,0:T(1,128)S(1)}, u32[]{:S(2)}) copy-start(f32[1,512]{1,0:T(1,128)S(1)} %get-tuple-element.246) | copy-start | bytes 6148
  110.8 5.5 %copy-start.10 = (bf16[512,2560]{1,0:T(8,128)(2,1)S(1)}, bf16[512,2560]{1,0:T(8,128)(2,1)}, u32[]{:S(2)}) copy-start(bf16[512,2560]{1,0:T(8,128)(2,1)} %get-tuple-element.41) | copy-start | bytes 7864324
  121.6 2.6 copy-start.20
  122.9 2.8 copy-start.2
  122.9 2.8 copy-start.39
  124.2 3.1 copy-start.41
  129.0 2.1 copy-start.31
  131.5 3.9 copy-start.60
  132.1 3.3 copy-start.76
  133.7 13.8 %copy-start.37 = (f32[788,4]{0,1:T(4,128)}, f32[788,4]{0,1:T(4,128)S(1)}, u32[]{:S(2)}) copy-start(f32[788,4]{0,1:T(4,128)S(1)} %get-tuple-element.269) | copy-start | bytes 37828
  138.9 8.6 %copy-start.74 = (s32[2,788]{1,0:T(2,128)}, s32[2,788]{1,0:T(2,128)S(1)}, u32[]{:S(2)}) copy-start(s32[2,788]{1,0:T(2,128)S(1)} %multiply_add_fusion.4) | copy-start | bytes 18916
  147.7 47.5 %copy-start.1 = (s32[8]{0:T(128)}, s32[8]{0:T(128)S(1)}, u32[]{:S(2)}) copy-start(s32[8]{0:T(128)S(1)} %reshape.282.counts) | copy-start | bytes 100
  152.2 2.2 copy-start
  154.4 40.8 %copy-start.75 = (s32[2,788]{1,0:T(2,128)S(1)}, s32[2,788]{1,0:T(2,128)}, u32[]{:S(2)}) copy-start(s32[2,788]{1,0:T(2,128)} %copy-done.74) | copy-start | bytes 18916
  212.9 2.7 copy-start.56
  212.9 2.7 copy-start.77
  212.9 2.8 copy-start.38
  212.9 2.8 copy-start.46
  212.9 2.8 copy-start.52
  288.8 2.8 copy-start.50
  288.8 2.8 copy-start.70
  291.6 2.7 copy-start.61
  291.6 2.7 copy-start.4
  291.6 2.7 copy-start.5
  294.3 2.9 copy-start.8
  296.1 3.5 copy-start.64
  299.5 3.1 copy-start.40
  299.5 3.1 copy-start.42
  299.5 3.1 copy-start.21
  302.6 7.6 %slice-start = ((s8[6553600]{0:T(1024)(128)(4,1)}), s8[4194304]{0:T(1024)(128)(4,1)S(1)}, s32[]{:S(2)}) async-start(s8[6553600]{0:T(1024)(128)(4,1)} %bitcast.158), calls=%async_computation | async-start | bytes 8388608
  302.7 7.5 %slice-start.1 = ((s8[6553600]{0:T(1024)(128)(4,1)}), s8[2359296]{0:T(1024)(128)(4,1)S(1)}, s32[]{:S(2)}) async-start(s8[6553600]{0:T(1024)(128)(4,1)} %bitcast.158), calls=%async_computation.1 | async-start | bytes 4718592
  310.2 4.6 copy-start.14
  327.3 6.9 %copy-start.26 = (bf16[512,1536]{0,1:T(8,128)(2,1)S(1)}, bf16[512,1536]{0,1:T(8,128)(2,1)}, u32[]{:S(2)}) copy-start(bf16[512,1536]{0,1:T(8,128)(2,1)} %copy-done.25) | copy-start | bytes 4718596
  327.3 6.9 %copy-start.48 = (f32[788]{0:T(1024)S(1)}, f32[788]{0:T(1024)}, u32[]{:S(2)}) copy-start(f32[788]{0:T(1024)} %copy-done.47) | copy-start | bytes 9460
  327.3 6.9 %copy-start.67 = (f32[1,512]{1,0:T(1,128)S(1)}, f32[1,512]{1,0:T(1,128)}, u32[]{:S(2)}) copy-start(f32[1,512]{1,0:T(1,128)} %copy-done.66) | copy-start | bytes 6148
  334.2 5.1 slice-start.2
  334.2 3.6 copy-start.59
  334.2 3.6 copy-start.54
  334.3 5.1 slice-start.3
  343.5 4.0 copy-start.18
  347.7 4.9 copy-start.73
  359.8 125.6 %copy-start.57 = (f32[2,11,64]{2,0,1:T(2,128)S(1)}, f32[2,11,64]{2,0,1:T(2,128)}, u32[]{:S(2)}) copy-start(f32[2,11,64]{2,0,1:T(2,128)} %param.33) | copy-start | bytes 16900
  359.8 125.8 %copy-start.72 = (f32[11,64]{1,0:T(8,128)S(1)}, f32[11,64]{1,0:T(8,128)}, u32[]{:S(2)}) copy-start(f32[11,64]{1,0:T(8,128)} %param.26) | copy-start | bytes 8452
  359.8 137.0 %copy-start.30 = (f32[2,64,512]{2,1,0:T(8,128)S(1)}, f32[2,64,512]{2,1,0:T(8,128)}, u32[]{:S(2)}) copy-start(f32[2,64,512]{2,1,0:T(8,128)} %param.28) | copy-start | bytes 786436
  359.8 137.0 %copy-start.36 = (f32[64,512]{1,0:T(8,128)S(1)}, f32[64,512]{1,0:T(8,128)}, u32[]{:S(2)}) copy-start(f32[64,512]{1,0:T(8,128)} %param.21) | copy-start | bytes 393220
  485.4 13.1 %copy-start.33 = (f32[64,2560]{1,0:T(8,128)S(1)}, f32[64,2560]{1,0:T(8,128)}, u32[]{:S(2)}) copy-start(f32[64,2560]{1,0:T(8,128)} %get-tuple-element.52) | copy-start | bytes 1966084
  486.6 12.0 %copy-start.24 = (f32[2,64,1536]{2,1,0:T(8,128)S(1)}, f32[2,64,1536]{2,1,0:T(8,128)}, u32[]{:S(2)}) copy-start(f32[2,64,1536]{2,1,0:T(8,128)} %param.27) | copy-start | bytes 2359300
  486.6 12.0 %copy-start.28 = (f32[64,1536]{1,0:T(8,128)S(1)}, f32[64,1536]{1,0:T(8,128)}, u32[]{:S(2)}) copy-start(f32[64,1536]{1,0:T(8,128)} %param.20) | copy-start | bytes 1179652
  489.4 10.2 %copy-start.81 = (f32[4,256]{1,0:T(4,128)}, f32[4,256]{1,0:T(4,128)S(1)}, u32[]{:S(2)}) copy-start(f32[4,256]{1,0:T(4,128)S(1)} %reshape.297) | copy-start | bytes 12292
  496.8 2.8 copy-start.34
  507.6 7.1 %copy-start.44 = (f32[64,4]{1,0:T(8,128)S(1)}, f32[64,4]{1,0:T(8,128)}, u32[]{:S(2)}) copy-start(f32[64,4]{1,0:T(8,128)} %get-tuple-element.240) | copy-start | bytes 3076
  507.6 7.2 %copy-start.79 = (f32[64,4]{0,1:T(4,128)S(1)}, f32[64,4]{0,1:T(4,128)}, u32[]{:S(2)}) copy-start(f32[64,4]{0,1:T(4,128)} %param.22) | copy-start | bytes 3076
  507.6 8.7 %copy-start.43 = (f32[64,4]{1,0:T(8,128)S(1)}, f32[64,4]{1,0:T(8,128)}, u32[]{:S(2)}) copy-start(f32[64,4]{1,0:T(8,128)} %get-tuple-element.241) | copy-start | bytes 3076
  507.6 10.9 %copy-start.80 = (f32[788]{0:T(1024)S(1)}, f32[788]{0:T(1024)}, u32[]{:S(2)}) copy-start(f32[788]{0:T(1024)} %get-tuple-element.202) | copy-start | bytes 9460
  507.7 10.9 %copy-start.7 = (f32[788,512]{1,0:T(8,128)S(1)}, f32[788,512]{1,0:T(8,128)}, u32[]{:S(2)}) copy-start(f32[788,512]{1,0:T(8,128)} %copy-done.6) | copy-start | bytes 4841476
  507.7 10.9 %copy-start.9 = (bf16[788,512]{1,0:T(8,128)(2,1)S(1)}, bf16[788,512]{1,0:T(8,128)(2,1)}, u32[]{:S(2)}) copy-start(bf16[788,512]{1,0:T(8,128)(2,1)} %param.18) | copy-start | bytes 2420740
  507.7 10.9 %copy-start.55 = (f32[788]{0:T(1024)S(1)}, f32[788]{0:T(1024)}, u32[]{:S(2)}) copy-start(f32[788]{0:T(1024)} %copy-done.53) | copy-start | bytes 9460
  507.7 10.9 %copy-start.63 = (f32[788]{0:T(1024)S(1)}, f32[788]{0:T(1024)}, u32[]{:S(2)}) copy-start(f32[788]{0:T(1024)} %copy-done.62) | copy-start | bytes 9460
  507.7 10.9 %copy-start.65 = (f32[788]{0:T(1024)S(1)}, f32[788]{0:T(1024)}, u32[]{:S(2)}) copy-start(f32[788]{0:T(1024)} %copy-done.64) | copy-start | bytes 9460
  507.7 10.9 %copy-start.68 = (f32[1,512]{1,0:T(1,128)S(1)}, f32[1,512]{1,0:T(1,128)}, u32[]{:S(2)}) copy-start(f32[1,512]{1,0:T(1,128)} %copy-done.66) | copy-start | bytes 6148
  518.6 3.1 copy-start.17
  521.6 2.3 copy-start.16
  (24 other events, 31.3 us)
